TPU v7x, 32 devices: a whole 2x2x4 slice. The times are simulated.
32 devices in a mesh: dp: 2 (over core), ctx: 4 (over y, x), hd: 4 (over z).
Axes of the slice: x: 2, y: 2, z: 4, core: 2. Of those that a mesh axis runs over, the one named last changes fastest.
Arguments:
- tokens_in: bfloat16 [4, 2048, 1536], P('dp', ('ctx', 'hd')), may hold values from -6 to 6
- seg_ids: int32 [4, 2048], P('dp'), may hold values from 0 to 7, never falling along the last dimension, each value on 1 to 512 neighbouring positions
- in_norm: float32 [1536], replicated, may hold values from 0.5 to 1.5
- z_proj: bfloat16 [1536, 3072], P(('dp', 'ctx', 'hd')), may hold values from -0.15625 to 0.15625
- xbc_proj: bfloat16 [1536, 3328], P(('dp', 'ctx', 'hd')), may hold values from -0.15625 to 0.15625
- dt_proj: bfloat16 [1536, 48], P(('dp', 'ctx', 'hd')), may hold values from -0.0390625 to 0.0390625
- conv_taps: float32 [4, 3328], replicated, may hold values from -3 to 3
- conv_bias: float32 [3328], replicated, may hold values from -2 to 2
- dt_bias: float32 [48], replicated, may hold values from -9 to -2
- a_log: float32 [48], replicated, may hold values from 0 to 2.77
- d_skip: float32 [48], replicated, may hold values from 0.5 to 2
- gate_norm: float32 [3072], replicated, may hold values from 0.5 to 1.5
- out_proj: bfloat16 [3072, 1536], P(('dp', 'ctx', 'hd')), may hold values from -0.109375 to 0.109375
- out_cotangent: bfloat16 [4, 2048, 1536], P('dp', ('ctx', 'hd')), may hold values from -6 to 6
Outputs:
- layer_out: bfloat16 [4, 2048, 1536], P('dp', ('ctx', 'hd'))
- tokens_grad: float32 [4, 2048, 1536], P('dp', ('ctx', 'hd'))
- in_norm_grad: float32 [1536], replicated
- z_proj_grad: float32 [1536, 3072], P(('dp', 'ctx', 'hd'))
- xbc_proj_grad: float32 [1536, 3328], P(('dp', 'ctx', 'hd'))
- dt_proj_grad: float32 [1536, 48], P(('dp', 'ctx', 'hd'))
- conv_taps_grad: float32 [4, 3328], replicated
- conv_bias_grad: float32 [3328], replicated
- dt_bias_grad: float32 [48], replicated
- a_log_grad: float32 [48], replicated
- d_skip_grad: float32 [48], replicated
- gate_norm_grad: float32 [3072], replicated
- out_proj_grad: float32 [3072, 1536], P(('dp', 'ctx', 'hd'))
Inputs may be any that keep to these rules, and one draw needn't show every extreme that they name: `seg_ids`: along each sequence the document numbers never fall; each document has 1 to 512 tokens and one has exactly that many.
All inputs are finite; a program needn't handle non-finite values.
Results may differ from a plain program's by a relative error of at most 0.0097.
Values may be sent and summed in bfloat16 or wider, within the bound.
No kernel may reach another device: no remote copies, remote signals or barrier semaphores. Data moves between devices by JAX's collectives and lax.ppermute only.
A program may use at most 320 MiB of HBM per device.

v0:
```python
import jax
import jax.numpy as jnp
from jax import lax
from jax.sharding import PartitionSpec as P

H = 48
P_SIZE = 64
N = 128
KW = 4
Q = 256
DI = 3072


HIGH = lax.Precision.HIGHEST
EPS = 1e-05


def from_behind(shard, axis, by):
    count = lax.axis_size(axis)
    pairs = [(i, i + by) for i in range(count) if 0 <= i + by < count]
    return lax.ppermute(shard, axis, pairs)


def carried_in(shard, axis, combine, identity, reverse):
    count, place = (lax.axis_size(axis), lax.axis_index(axis))
    everything = jax.tree.map(
        lambda part, kind: lax.all_gather(part.astype(kind), axis),
        shard,
        (jnp.bfloat16, jnp.bfloat16),
    )
    start = jax.tree.map(
        lambda part, zero: jnp.broadcast_to(jnp.asarray(zero, part.dtype), part.shape),
        shard,
        identity,
    )

    def turn(k, before):
        at = count - 1 - k if reverse else k
        reached = at > place if reverse else at < place
        new = combine(
            before, jax.tree.map(lambda part, own: part[at].astype(own.dtype), everything, shard)
        )
        return jax.tree.map(lambda a, b: jnp.where(reached, a, b), new, before)

    return lax.fori_loop(0, count, turn, start)


def norm_rows(values, gain):
    return values * lax.rsqrt(jnp.mean(values * values, axis=-1, keepdims=True) + EPS) * gain


def gate_tail(mixer_val, gate_val, gain):
    return norm_rows(mixer_val * jax.nn.silu(gate_val), gain)


def conv_act(padded, taps, bias, masks):
    length = masks.shape[1]
    mixed = bias
    for tap in range(taps.shape[0]):
        mixed = mixed + taps[tap] * padded[tap : tap + length] * masks[tap][:, None]
    return jax.nn.silu(mixed)


def back_dot(grad_val, weight):
    return lax.dot_general(
        grad_val, weight, (((1,), (1,)), ((), ())), preferred_element_type=jnp.float32
    )


def compose(earlier, later):
    return (earlier[0] * later[0], later[0][:, None, None] * earlier[1] + later[1])


def block_decay(rate_val, bias_here, decay_log, seg_blk, seg_before):
    log_rate = jax.nn.softplus(rate_val + bias_here) * -jnp.exp(decay_log)
    cumul = jnp.cumsum(log_rate, axis=0)
    keep = (seg_blk == seg_before).astype(jnp.float32)
    lead = jnp.exp(cumul) * keep[:, None]
    return (lead[-1], lead)


def block_ssd(
    x_val,
    rate_val,
    bias_here,
    decay_log,
    skip_here,
    bc_val,
    state_in,
    seg_blk,
    seg_before,
    span_len,
):
    length, heads = rate_val.shape
    count = length // span_len
    width_n = bc_val.shape[1] // 2
    x_groups = x_val.reshape(count, span_len, heads, -1)
    dt_groups = jax.nn.softplus(rate_val + bias_here).reshape(count, span_len, heads)
    cumul = jnp.cumsum(dt_groups * -jnp.exp(decay_log), axis=1)
    b_groups = bc_val[:, :width_n].reshape(count, span_len, width_n)
    c_groups = bc_val[:, width_n:].reshape(count, span_len, width_n)
    seg_groups = seg_blk.reshape(count, span_len)
    before = jnp.concatenate([seg_before, seg_groups[:-1, -1]])
    order = jnp.arange(span_len)
    mask = (seg_groups[:, :, None] == seg_groups[:, None, :]) & (order[:, None] >= order[None, :])
    gaps = cumul[:, :, None, :] - cumul[:, None, :, :]
    decay = jnp.exp(jnp.where(mask[..., None], gaps, 0.0)) * mask[..., None].astype(jnp.float32)
    scores = jnp.einsum("ctn,csn->cts", c_groups, b_groups, precision=HIGH)
    mix_w = scores[..., None] * decay * dt_groups[:, None, :, :]
    y_part = jnp.einsum("ctsh,cshp->cthp", mix_w, x_groups, precision=HIGH)
    keep = (seg_groups == before[:, None]).astype(jnp.float32)
    lead = jnp.exp(cumul) * keep[..., None]
    tail = (
        jnp.exp(cumul[:, -1:, :] - cumul)
        * (seg_groups == seg_groups[:, -1:]).astype(jnp.float32)[..., None]
        * dt_groups
    )
    pieces = jnp.einsum("csh,cshp,csn->chpn", tail, x_groups, b_groups, precision=HIGH)

    def advance(state, item):
        piece, factor = item
        return (state * factor[:, None, None] + piece, state)

    state_end, entering = lax.scan(advance, state_in, (pieces, lead[:, -1, :]))
    y_part = y_part + lead[..., None] * jnp.einsum(
        "ctn,chpn->cthp", c_groups, entering, precision=HIGH
    )
    y_part = y_part + skip_here[:, None] * x_groups
    return (y_part.reshape(length, -1), state_end)


def shards(
    tokens_in,
    seg_ids,
    in_norm,
    z_proj,
    xbc_proj,
    dt_proj,
    conv_taps,
    conv_bias,
    dt_bias,
    a_log,
    d_skip,
    gate_norm,
    out_proj,
    out_cotangent,
):
    batches, rows, width = tokens_in.shape
    n_heads_axis = lax.axis_size("hd")
    heads_here = H // n_heads_axis
    block = rows * n_heads_axis
    channels = DI + 2 * N
    start_tok = lax.axis_index(("ctx", "hd")) * rows
    start_blk = lax.axis_index("ctx") * block
    head_low = lax.axis_index("hd") * heads_here
    bias_here = lax.dynamic_slice_in_dim(dt_bias, head_low, heads_here)
    decay_log = lax.dynamic_slice_in_dim(a_log, head_low, heads_here)
    skip_here = lax.dynamic_slice_in_dim(d_skip, head_low, heads_here)
    unit = (jnp.ones((heads_here,), jnp.float32), jnp.zeros((heads_here, P_SIZE, N), jnp.float32))

    def fetch():
        return (
            lax.all_gather(z_proj, ("dp", "ctx", "hd"), axis=0, tiled=True),
            lax.all_gather(xbc_proj, ("dp", "ctx", "hd"), axis=0, tiled=True),
            lax.all_gather(dt_proj, ("dp", "ctx", "hd"), axis=0, tiled=True),
            lax.all_gather(out_proj, ("dp", "ctx", "hd"), axis=0, tiled=True),
        )

    stored = []
    outputs = []
    for batch in range(batches):
        zed_weight, xbc_weight, rate_weight, out_weight = fetch()
        seg_row = seg_ids[batch]
        seg_pad = jnp.concatenate([jnp.full((KW - 1,), -1, jnp.int32), seg_row])
        seg_near = lax.dynamic_slice_in_dim(seg_pad, start_tok, rows + KW - 1)
        seg_own = seg_near[KW - 1 :]
        masks = jnp.stack([seg_near[tap : tap + rows] == seg_own for tap in range(KW)]).astype(
            jnp.float32
        )
        seg_blk = lax.dynamic_slice_in_dim(seg_row, start_blk, block)
        seg_before = lax.dynamic_slice_in_dim(seg_pad, start_blk + KW - 2, 1)
        source = tokens_in[batch].astype(jnp.float32)
        normed = norm_rows(source, in_norm).astype(jnp.bfloat16)
        gate_in = jnp.dot(normed, zed_weight, preferred_element_type=jnp.float32)
        raw_xbc = jnp.dot(normed, xbc_weight, preferred_element_type=jnp.float32).astype(
            jnp.bfloat16
        )
        rate_raw = jnp.dot(normed, rate_weight, preferred_element_type=jnp.float32).astype(
            jnp.bfloat16
        )
        rim_rows = from_behind(raw_xbc[rows - (KW - 1) :], ("ctx", "hd"), 1)
        padded = jnp.concatenate([rim_rows, raw_xbc], 0).astype(jnp.float32)
        active = conv_act(padded, conv_taps, conv_bias, masks)
        x_low = active[:, :DI].astype(jnp.bfloat16)
        bc_low = active[:, DI:].astype(jnp.bfloat16)
        x_heads, rate_heads = (
            lax.all_to_all(x_low, "hd", split_axis=1, concat_axis=0, tiled=True),
            lax.all_to_all(rate_raw, "hd", split_axis=1, concat_axis=0, tiled=True),
        )
        bc_all = lax.all_gather(bc_low, "hd", axis=0, tiled=True)
        x_float = x_heads.astype(jnp.float32)
        rate_float = rate_heads.astype(jnp.float32)
        bc_float = bc_all.astype(jnp.float32)
        zero_state = jnp.zeros((heads_here, P_SIZE, N), jnp.float32)
        y_zero, state_local = block_ssd(
            x_float,
            rate_float,
            bias_here,
            decay_log,
            skip_here,
            bc_float,
            zero_state,
            seg_blk,
            seg_before,
            Q,
        )
        total_decay, lead_blk = block_decay(rate_float, bias_here, decay_log, seg_blk, seg_before)
        unused, state_in = carried_in((total_decay, state_local), "ctx", compose, unit, False)
        carried = lead_blk[:, :, None] * jnp.einsum(
            "tn,hpn->thp", bc_float[:, N:], state_in, precision=HIGH
        )
        y_heads = y_zero + carried.reshape(block, -1)
        y_tokens = lax.all_to_all(
            y_heads.astype(jnp.bfloat16), "hd", split_axis=0, concat_axis=1, tiled=True
        )
        y_float = y_tokens.astype(jnp.float32)
        gated = gate_tail(y_float, gate_in, gate_norm).astype(jnp.bfloat16)
        result = source + jnp.dot(gated, out_weight, preferred_element_type=jnp.float32)
        outputs.append(result.astype(jnp.bfloat16))
        stored.append(
            (
                source,
                normed,
                gate_in,
                padded,
                masks,
                x_float,
                rate_float,
                bc_float,
                seg_blk,
                seg_before,
                lead_blk,
                total_decay,
                state_in,
                y_float,
                gated,
            )
        )
    grads_tok = []
    normed_rows = []
    proj_grads = []
    gated_rows = []
    cot_rows = []
    norm_total = jnp.zeros((width,), jnp.float32)
    taps_total = jnp.zeros(conv_taps.shape, jnp.float32)
    cbias_total = jnp.zeros((channels,), jnp.float32)
    dtb_total = jnp.zeros((H,), jnp.float32)
    alog_total = jnp.zeros((H,), jnp.float32)
    skip_total = jnp.zeros((H,), jnp.float32)
    gate_total = jnp.zeros((DI,), jnp.float32)
    for batch in range(batches):
        zed_weight, xbc_weight, rate_weight, out_weight = fetch()
        (
            source,
            normed,
            gate_in,
            padded,
            masks,
            x_float,
            rate_float,
            bc_float,
            seg_blk,
            seg_before,
            lead_blk,
            total_decay,
            state_in,
            y_float,
            gated,
        ) = stored[batch]
        cot_low = out_cotangent[batch]
        d_gated = back_dot(cot_low, out_weight)
        unused, tail_pull = jax.vjp(gate_tail, y_float, gate_in, gate_norm)
        d_mixer, d_gate_in, d_gain = tail_pull(d_gated)
        d_mixer_heads = lax.all_to_all(
            d_mixer.astype(jnp.bfloat16), "hd", split_axis=1, concat_axis=0, tiled=True
        )
        d_y_float = d_mixer_heads.astype(jnp.float32)
        d_local = jnp.einsum(
            "th,thp,tn->hpn",
            lead_blk,
            d_y_float.reshape(block, heads_here, P_SIZE),
            bc_float[:, N:],
            precision=HIGH,
        )
        unused, d_end = carried_in((total_decay, d_local), "ctx", compose, unit, True)

        def with_state(x_value, rate_value, bias_value, decay_value, skip_value, bc_value):
            return block_ssd(
                x_value,
                rate_value,
                bias_value,
                decay_value,
                skip_value,
                bc_value,
                state_in,
                seg_blk,
                seg_before,
                Q,
            )

        unused, ssd_pull = jax.vjp(
            with_state, x_float, rate_float, bias_here, decay_log, skip_here, bc_float
        )
        d_x_heads, d_rate_heads, d_bias_h, d_decay_h, d_skip_h, d_bc_heads = ssd_pull(
            (d_y_float, d_end)
        )
        d_x_tok, d_rate_tok = (
            lax.all_to_all(
                d_x_heads.astype(jnp.bfloat16), "hd", split_axis=0, concat_axis=1, tiled=True
            ),
            lax.all_to_all(
                d_rate_heads.astype(jnp.bfloat16), "hd", split_axis=0, concat_axis=1, tiled=True
            ),
        )
        d_bc_tok = lax.psum_scatter(
            d_bc_heads.astype(jnp.bfloat16), "hd", scatter_dimension=0, tiled=True
        ).astype(jnp.float32)
        d_active = jnp.concatenate([d_x_tok.astype(jnp.float32), d_bc_tok], axis=1)

        def conv_here(pad_value, taps_value, bias_value):
            return conv_act(pad_value, taps_value, bias_value, masks)

        unused, conv_pull = jax.vjp(conv_here, padded, conv_taps, conv_bias)
        d_padded, d_taps, d_cbias = conv_pull(d_active)
        back_rim = from_behind(d_padded[: KW - 1].astype(jnp.bfloat16), ("ctx", "hd"), -1).astype(
            jnp.float32
        )
        d_raw = d_padded[KW - 1 :] + jnp.concatenate(
            [jnp.zeros((rows - (KW - 1), channels), jnp.float32), back_rim], 0
        )
        d_raw_low = d_raw.astype(jnp.bfloat16)
        d_gate_low = d_gate_in.astype(jnp.bfloat16)
        d_normed = (
            back_dot(d_gate_low, zed_weight)
            + back_dot(d_raw_low, xbc_weight)
            + back_dot(d_rate_tok, rate_weight)
        )
        unused, norm_pull = jax.vjp(norm_rows, source, in_norm)
        d_source, d_norm_gain = norm_pull(d_normed)
        grads_tok.append(d_source + cot_low.astype(jnp.float32))
        normed_rows.append(normed)
        proj_grads.append(jnp.concatenate([d_gate_low, d_raw_low, d_rate_tok], axis=1))
        gated_rows.append(gated)
        cot_rows.append(cot_low)
        norm_total = norm_total + d_norm_gain
        taps_total = taps_total + d_taps
        cbias_total = cbias_total + d_cbias
        dtb_total = dtb_total + lax.dynamic_update_slice_in_dim(
            jnp.zeros((H,), jnp.float32), d_bias_h, head_low, 0
        )
        alog_total = alog_total + lax.dynamic_update_slice_in_dim(
            jnp.zeros((H,), jnp.float32), d_decay_h, head_low, 0
        )
        skip_total = skip_total + lax.dynamic_update_slice_in_dim(
            jnp.zeros((H,), jnp.float32), d_skip_h, head_low, 0
        )
        gate_total = gate_total + d_gain
    normed_all = jnp.concatenate(normed_rows, 0)
    proj_all = jnp.concatenate(proj_grads, 0)
    gated_all = jnp.concatenate(gated_rows, 0)
    cot_all = jnp.concatenate(cot_rows, 0)
    part = normed_all
    in_grad = lax.psum_scatter(
        lax.dot_general(
            part, proj_all, (((0,), (0,)), ((), ())), preferred_element_type=jnp.float32
        ),
        ("dp", "ctx", "hd"),
        scatter_dimension=0,
        tiled=True,
    )
    part = gated_all
    out_grad = lax.psum_scatter(
        lax.dot_general(
            part, cot_all, (((0,), (0,)), ((), ())), preferred_element_type=jnp.float32
        ),
        ("dp", "ctx", "hd"),
        scatter_dimension=0,
        tiled=True,
    )
    norm_sum, taps_sum, cbias_sum, dtb_sum, alog_sum, skip_sum, gate_sum = lax.psum(
        (norm_total, taps_total, cbias_total, dtb_total, alog_total, skip_total, gate_total),
        ("dp", "ctx", "hd"),
    )
    return (
        jnp.stack(outputs),
        jnp.stack(grads_tok),
        norm_sum,
        in_grad[:, :DI],
        in_grad[:, DI : DI + channels],
        in_grad[:, DI + channels :],
        taps_sum,
        cbias_sum,
        dtb_sum,
        alog_sum,
        skip_sum,
        gate_sum,
        out_grad,
    )


def solution(mesh):
    in_specs = (
        P("dp", ("ctx", "hd"), None),
        P("dp", None),
        P(),
        P(("dp", "ctx", "hd"), None),
        P(("dp", "ctx", "hd"), None),
        P(("dp", "ctx", "hd"), None),
        P(),
        P(),
        P(),
        P(),
        P(),
        P(),
        P(("dp", "ctx", "hd"), None),
        P("dp", ("ctx", "hd"), None),
    )
    out_specs = (
        P("dp", ("ctx", "hd"), None),
        P("dp", ("ctx", "hd"), None),
        P(),
        P(("dp", "ctx", "hd"), None),
        P(("dp", "ctx", "hd"), None),
        P(("dp", "ctx", "hd"), None),
        P(),
        P(),
        P(),
        P(),
        P(),
        P(),
        P(("dp", "ctx", "hd"), None),
    )
    return jax.shard_map(shards, mesh=mesh, in_specs=in_specs, out_specs=out_specs, check_vma=False)
```

profile of v0, /device:TPU:0, one launch (start us, length us, event | category | flops | bytes accessed | tf_op | source)
XLA Modules:
  0.0 1491.1 jit_solution(12795185626710274791)
XLA Ops:
  8.7 76.8 %all_gather.68 = bf16[1536,48]{1,0:T(8,128)(2,1)S(1)} all-gather(bf16[48,48]{1,0:T(8,128)(2,1)} %param.40), channel_id=1, replica_groups=mesh['dp'=2,'ctx'=4,'hd'=4] {'dp','ctx','hd'}, dimensions={0}, use_global_device_ids=true | all-gather | bytes 152064 | tf_op jit(solution)/shard_map/all_gather | solution.py:165
  110.2 5.7 all-to-all-done.1
  125.4 14.0 all-gather.5
  141.8 6.4 all-gather.4
  152.6 6.6 convolution_convert_fusion
  173.7 6.7 all-to-all-start.3
  188.7 17.7 %all_gather.74 = bf16[512,256]{1,0:T(8,128)(2,1)S(1)} all-gather(bf16[128,256]{1,0:T(8,128)(2,1)S(1)} %slice.403), channel_id=1, replica_groups=mesh['dp'=2,'ctx'=4,'hd'=4] {'hd'}, dimensions={0}, use_global_device_ids=true | all-gather | bytes 327680 | tf_op jit(solution)/shard_map/all_gather | solution.py:200
  206.4 15.0 %all_gather.33 = bf16[512,256]{1,0:T(8,128)(2,1)S(1)} all-gather(bf16[128,256]{1,0:T(8,128)(2,1)S(1)} %slice.386), channel_id=1, replica_groups=mesh['dp'=2,'ctx'=4,'hd'=4] {'hd'}, dimensions={0}, use_global_device_ids=true | all-gather | bytes 327680 | tf_op jit(solution)/shard_map/all_gather | solution.py:200
  238.3 7.7 while.156
  247.1 12.9 all-gather.1
  260.0 6.8 while.157
  289.1 14.6 all-to-all-start.5
  313.3 7.6 while.154
  321.9 11.6 all-gather
  336.4 6.8 while.155
  343.1 7.1 fusion.101
  369.2 5.5 all-to-all-start.2
  376.4 6.3 while.152
  393.6 7.3 multiply_reduce_fusion.19
  401.5 9.2 multiply_reduce_fusion.13
  410.8 7.1 multiply_reduce_fusion.18
  418.0 9.1 multiply_convert_fusion.3
  434.2 5.1 all-to-all-start.9
  446.5 13.0 all-to-all-done.9
  472.3 10.0 all-gather.3
  495.6 7.8 while.153
  509.5 6.3 fusion.53
  524.5 12.2 all-gather.2
  553.0 6.8 while.151
  565.2 6.4 fusion.51
  580.1 6.3 reduce-window.70
  603.2 6.2 reduce-window.76
  637.2 6.4 fusion.116
  653.0 6.3 fusion.109
  675.4 5.2 all-to-all-start.7
  708.2 16.6 %reduce-scatter.5.cloned.1.call-done = bf16[128,256]{1,0:T(8,128)(2,1)} async-done(((bf16[512,256]{1,0:T(8,128)(2,1)}), bf16[128,256]{1,0:T(8,128)(2,1)}) %reduce-scatter.5.cloned.1.call-update) | async-done | bytes 65552 | tf_op jit(solution)/shard_map/reduce_scatter | solution.py:325
  724.8 6.5 multiply_reduce_fusion.9
  741.9 19.9 %fusion.38 = f32[1536,6448]{1,0:T(8,128)} fusion(bf16[128,48]{1,0:T(8,128)(2,1)S(1)} %copy.500, bf16[128,3328]{1,0:T(8,128)(2,1)S(1)} %fusion.98, bf16[128,3072]{1,0:T(8,128)(2,1)S(1)} %copy-done.28, bf16[128,48]{1,0:T(8,128)(2,1)S(1)} %copy-done.103, bf16[128,3328]{1,0:T(8,128)(2,1)S(1)} %fusion.99, bf16[128,3072]{1,0:T(8,128)(2,1)} %get-tuple-element.1175, ...), kind=kOutput, calls=%fused_computation.78 | convolution fusion | flops 5092294656 | bytes 43704320 | tf_op jit(solution)/shard_map/dot_general | solution.py:374
  764.4 7.0 fusion.278
  771.4 9.5 fusion.276
  788.5 8.9 convolution_add_fusion.2
  798.7 9.0 convolution_add_fusion.3
  809.9 11.9 fusion.118
  821.8 6.1 fusion.84
  828.0 5.1 fusion.85
  836.5 293.6 %reduce-scatter.9.cloned.1.call-done = f32[48,6448]{1,0:T(8,128)} async-done(((f32[1536,6448]{1,0:T(8,128)}), f32[48,6448]{1,0:T(8,128)}) %reduce-scatter.9.cloned.1.call-update) | async-done | bytes 1238032 | tf_op jit(solution)/shard_map/reduce_scatter | solution.py:373
  1135.3 125.0 %all-reduce.31.cloned.1.call-done = (f32[1536]{0:T(1024)}, f32[4,3328]{1,0:T(4,128)}, f32[3328]{0:T(1024)}, f32[48]{0:T(128)}, f32[48]{0:T(128)}, /*index=5*/f32[48]{0:T(128)}, f32[3072]{0:T(1024)}) async-done(((f32[1536]{0:T(1024)}, f32[4,3328]{1,0:T(4,128)}, f32[3328]{0:T(1024)}, f32[48]{0:T(128)}, f32[48]{0:T(128)}, /*index=5*/f32[48]{0:T(128)}, f32[3072]{0:T(1024)}), (f32[1536]{0:T(1024)}, ...) | async-done | bytes 85584 | tf_op jit(solution)/shard_map/psum | solution.py:390
  1260.2 214.8 %reduce-scatter.11.cloned.1.call-done = f32[96,1536]{1,0:T(8,128)} async-done(((f32[3072,1536]{1,0:T(8,128)}), f32[96,1536]{1,0:T(8,128)}) %reduce-scatter.11.cloned.1.call-update) | async-done | bytes 589840 | tf_op jit(solution)/shard_map/reduce_scatter | solution.py:382
  (830 shorter events, 433.9 us)
Async XLA Ops:
  7.2 80.4 %copy-start.12 = (bf16[2,128,1536]{2,1,0:T(8,128)(2,1)S(1)}, bf16[2,128,1536]{2,1,0:T(8,128)(2,1)}, u32[]{:S(2)}) copy-start(bf16[2,128,1536]{2,1,0:T(8,128)(2,1)} %param.35) | copy-start | bytes 2359300
  7.2 80.4 %copy-start.127 = (f32[1536]{0:T(1024)S(1)}, f32[1536]{0:T(1024)}, u32[]{:S(2)}) copy-start(f32[1536]{0:T(1024)} %param.37) | copy-start | bytes 18436
  7.2 145.4 %all-gather.10.cloned.1.call-start = ((), (), s32[]{:S(2)}) async-start(), calls=%async_computation.16 | async-start | bytes 10543104 | tf_op jit(solution)/shard_map/all_gather | solution.py:164
  7.9 385.7 %all-gather.12.cloned.1.call-start = ((), (), s32[]{:S(2)}) async-start(), calls=%async_computation.17 | async-start | bytes 9732096 | tf_op jit(solution)/shard_map/all_gather | solution.py:163
  87.8 64.8 %copy-start.18 = (bf16[128,1536]{1,0:T(8,128)(2,1)}, bf16[128,1536]{1,0:T(8,128)(2,1)S(1)}, u32[]{:S(2)}) copy-start(bf16[128,1536]{1,0:T(8,128)(2,1)S(1)} %get-tuple-element.1191) | copy-start | bytes 1179652
  87.8 74.5 %copy-start.15 = (bf16[128,1536]{1,0:T(8,128)(2,1)}, bf16[128,1536]{1,0:T(8,128)(2,1)S(1)}, u32[]{:S(2)}) copy-start(bf16[128,1536]{1,0:T(8,128)(2,1)S(1)} %get-tuple-element.1190) | copy-start | bytes 1179652
  88.8 16.4 %all-to-all-start.4 = ((bf16[128,4,12]{0,2,1:T(8,128)(2,1)}), bf16[128,4,12]{0,2,1:T(8,128)(2,1)S(1)}, u32[]{:S(2)}, u32[]{:S(2)}) async-start(bf16[128,4,12]{0,2,1:T(8,128)(2,1)} %all_to_all.141), calls=%async_computation.4 | async-start | bytes 32768 | tf_op jit(solution)/shard_map/all_to_all | solution.py:198
  92.1 309.4 %all-gather.14.cloned.1.call-start = ((), (), s32[]{:S(2)}) async-start(), calls=%async_computation.18 | async-start | bytes 9732096 | tf_op jit(solution)/shard_map/all_gather | solution.py:166
  97.3 84.5 %copy-start.80 = (f32[3328]{0:T(1024)}, f32[3328]{0:T(1024)S(1)}, u32[]{:S(2)}) copy-start(f32[3328]{0:T(1024)S(1)} %get-tuple-element.1033) | copy-start | bytes 39940
  101.0 47.9 %copy-start.121 = (f32[2,256]{1,0:T(2,128)}, f32[2,256]{1,0:T(2,128)S(1)}, u32[]{:S(2)}) copy-start(f32[2,256]{1,0:T(2,128)S(1)} %get-tuple-element.1240) | copy-start | bytes 6148
  101.0 47.9 %copy-start.137 = (f32[2,256]{1,0:T(2,128)}, f32[2,256]{1,0:T(2,128)S(1)}, u32[]{:S(2)}) copy-start(f32[2,256]{1,0:T(2,128)S(1)} %get-tuple-element.1241) | copy-start | bytes 6148
  102.4 46.4 %copy-start.136 = (f32[2,256]{1,0:T(2,128)}, f32[2,256]{1,0:T(2,128)S(1)}, u32[]{:S(2)}) copy-start(f32[2,256]{1,0:T(2,128)S(1)} %get-tuple-element.1247) | copy-start | bytes 6148
  104.0 44.9 %copy-start.157 = (f32[12]{0:T(128)}, f32[12]{0:T(128)S(1)}, u32[]{:S(2)}) copy-start(f32[12]{0:T(128)S(1)} %dynamic_slice.178) | copy-start | bytes 148
  105.2 10.8 all-to-all-start.1
  116.1 25.5 %copy-start.78 = (f32[2,8,4,128]{3,1,2,0:T(8,128)}, f32[2,8,4,128]{3,1,2,0:T(8,128)S(1)}, u32[]{:S(2)}) copy-start(f32[2,8,4,128]{3,1,2,0:T(8,128)S(1)} %copy.565) | copy-start | bytes 98308
  116.1 25.5 %copy-start.79 = (f32[2,8,4,128]{3,1,2,0:T(8,128)}, f32[2,8,4,128]{3,1,2,0:T(8,128)S(1)}, u32[]{:S(2)}) copy-start(f32[2,8,4,128]{3,1,2,0:T(8,128)S(1)} %copy.563) | copy-start | bytes 98308
  116.2 33.4 %copy-start.63 = (f32[2,256,12]{1,0,2:T(2,128)}, f32[2,256,12]{1,0,2:T(2,128)S(1)}, u32[]{:S(2)}) copy-start(f32[2,256,12]{1,0,2:T(2,128)S(1)} %reshape.754) | copy-start | bytes 73732
  116.3 33.4 %copy-start.61 = (f32[2,256,12]{1,0,2:T(2,128)}, f32[2,256,12]{1,0,2:T(2,128)S(1)}, u32[]{:S(2)}) copy-start(f32[2,256,12]{1,0,2:T(2,128)S(1)} %reshape.763) | copy-start | bytes 73732
  118.6 40.6 %copy-start.93 = (f32[2,12,256]{2,1,0:T(8,128)}, f32[2,12,256]{2,1,0:T(8,128)S(1)}, u32[]{:S(2)}) copy-start(f32[2,12,256]{2,1,0:T(8,128)S(1)} %reshape.833) | copy-start | bytes 73732
  120.4 38.8 %copy-start.134 = (f32[2,12]{1,0:T(2,128)}, f32[2,12]{1,0:T(2,128)S(1)}, u32[]{:S(2)}) copy-start(f32[2,12]{1,0:T(2,128)S(1)} %slice_reduce_fusion.10) | copy-start | bytes 292
  122.0 37.3 %copy-start.59 = (f32[2,12,256]{2,1,0:T(8,128)}, f32[2,12,256]{2,1,0:T(8,128)S(1)}, u32[]{:S(2)}) copy-start(f32[2,12,256]{2,1,0:T(8,128)S(1)} %reshape.841) | copy-start | bytes 73732
  122.1 37.1 %copy-start.132 = (f32[2,12]{1,0:T(2,128)}, f32[2,12]{1,0:T(2,128)S(1)}, u32[]{:S(2)}) copy-start(f32[2,12]{1,0:T(2,128)S(1)} %slice_reduce_fusion.8) | copy-start | bytes 292
  123.7 35.6 %copy-start.94 = (f32[2,12,256]{2,1,0:T(8,128)}, f32[2,12,256]{2,1,0:T(8,128)S(1)}, u32[]{:S(2)}) copy-start(f32[2,12,256]{2,1,0:T(8,128)S(1)} %reshape.835) | copy-start | bytes 73732
  141.6 17.7 %copy-start.74 = (f32[512,12]{0,1:T(8,128)}, f32[512,12]{0,1:T(8,128)S(1)}, u32[]{:S(2)}) copy-start(f32[512,12]{0,1:T(8,128)S(1)} %multiply_bitcast_fusion.5) | copy-start | bytes 73732
  159.3 7.4 collective-permute-start.1
  164.6 15.9 %collective-permute-start = (bf16[3,3328]{1,0:T(4,128)(2,1)}, bf16[3,3328]{1,0:T(4,128)(2,1)S(1)}, u32[]{:S(2)}, u32[]{:S(2)}) collective-permute-start(bf16[3,3328]{1,0:T(4,128)(2,1)} %slice.380), channel_id=1, source_target_pairs={{0,1},{1,2},{2,3},{3,4},{4,5},{5,6},{6,7},{7,8},{8,9},{9,10},{10,1... | collective-permute-start | bytes 59912 | tf_op jit(solution)/shard_map/ppermute | solution.py:21
  173.7 50.4 %all-to-all-start.3 = ((bf16[128,4,768]{0,2,1:T(8,128)(2,1)}), bf16[128,4,768]{0,2,1:T(8,128)(2,1)}, u32[]{:S(2)}, u32[]{:S(2)}) async-start(bf16[128,4,768]{0,2,1:T(8,128)(2,1)} %bitcast.581), calls=%async_computation.3 | async-start | bytes 1572864 | tf_op jit(solution)/shard_map/all_to_all | solution.py:197
  206.4 16.7 %copy-start.54 = (bf16[512,256]{1,0:T(8,128)(2,1)}, bf16[512,256]{1,0:T(8,128)(2,1)S(1)}, u32[]{:S(2)}) copy-start(bf16[512,256]{1,0:T(8,128)(2,1)S(1)} %all_gather.74) | copy-start | bytes 786436
  224.1 64.9 %all-to-all-start = ((bf16[128,4,768]{0,2,1:T(8,128)(2,1)}), bf16[128,4,768]{0,2,1:T(8,128)(2,1)}, u32[]{:S(2)}, u32[]{:S(2)}) async-start(bf16[128,4,768]{0,2,1:T(8,128)(2,1)} %bitcast.579), calls=%async_computation | async-start | bytes 1572864 | tf_op jit(solution)/shard_map/all_to_all | solution.py:197
  289.1 80.1 %all-to-all-start.5 = ((bf16[4,128,768]{1,2,0:T(8,128)(2,1)}), bf16[4,128,768]{1,2,0:T(8,128)(2,1)}, u32[]{:S(2)}, u32[]{:S(2)}) async-start(bf16[4,128,768]{1,2,0:T(8,128)(2,1)} %copy.441), calls=%async_computation.5 | async-start | bytes 1572864 | tf_op jit(solution)/shard_map/all_to_all | solution.py:223
  369.2 18.9 %all-to-all-start.2 = ((bf16[4,128,768]{1,2,0:T(8,128)(2,1)}), bf16[4,128,768]{1,2,0:T(8,128)(2,1)}, u32[]{:S(2)}, u32[]{:S(2)}) async-start(bf16[4,128,768]{1,2,0:T(8,128)(2,1)} %copy.425), calls=%async_computation.2 | async-start | bytes 1572864 | tf_op jit(solution)/shard_map/all_to_all | solution.py:223
  401.5 16.5 %slice-start = ((s8[9437184]{0:T(1024)(128)(4,1)}), s8[4194304]{0:T(1024)(128)(4,1)S(1)}, s32[]{:S(2)}) async-start(s8[9437184]{0:T(1024)(128)(4,1)} %bitcast.551), calls=%async_computation.24 | async-start | bytes 8388608
  401.5 16.5 %slice-start.1 = ((s8[9437184]{0:T(1024)(128)(4,1)}), s8[4194304]{0:T(1024)(128)(4,1)S(1)}, s32[]{:S(2)}) async-start(s8[9437184]{0:T(1024)(128)(4,1)} %bitcast.551), calls=%async_computation.25 | async-start | bytes 8388608
  434.2 25.3 %all-to-all-start.9 = ((bf16[128,4,768]{0,2,1:T(8,128)(2,1)}), bf16[128,4,768]{0,2,1:T(8,128)(2,1)}, u32[]{:S(2)}, u32[]{:S(2)}) async-start(bf16[128,4,768]{0,2,1:T(8,128)(2,1)} %bitcast.580), calls=%async_computation.10 | async-start | bytes 1572864 | tf_op jit(solution)/shard_map/all_to_all | solution.py:284
  444.2 20.7 %copy-start.180 = (f32[2,12,1,1]{1,3,2,0:T(1,128)}, f32[2,12,1,1]{1,3,2,0:T(1,128)S(1)}, u32[]{:S(2)}) copy-start(f32[2,12,1,1]{1,3,2,0:T(1,128)S(1)} %get-tuple-element.1855) | copy-start | bytes 292
  459.5 56.3 %all-to-all-start.6 = ((bf16[128,4,768]{0,2,1:T(8,128)(2,1)}), bf16[128,4,768]{0,2,1:T(8,128)(2,1)}, u32[]{:S(2)}, u32[]{:S(2)}) async-start(bf16[128,4,768]{0,2,1:T(8,128)(2,1)} %bitcast.84), calls=%async_computation.6 | async-start | bytes 1572864 | tf_op jit(solution)/shard_map/all_to_all | solution.py:284
  571.6 65.6 %copy-start.22 = (bf16[2,256,12,64]{1,0,3,2:T(2,128)(2,1)S(1)}, bf16[2,256,12,64]{1,0,3,2:T(2,128)(2,1)}, u32[]{:S(2)}) copy-start(bf16[2,256,12,64]{1,0,3,2:T(2,128)(2,1)} %all_to_all.156) | copy-start | bytes 2359300
  620.8 12.0 all-to-all-start.11
  632.9 15.1 %all-to-all-start.8 = ((bf16[4,128,12]{1,2,0:T(8,128)(2,1)}), bf16[4,128,12]{1,2,0:T(8,128)(2,1)}, u32[]{:S(2)}, u32[]{:S(2)}) async-start(bf16[4,128,12]{1,2,0:T(8,128)(2,1)} %copy.470), calls=%async_computation.9 | async-start | bytes 32768 | tf_op jit(solution)/shard_map/all_to_all | solution.py:321
  648.0 27.4 %all-to-all-start.10 = ((bf16[4,128,768]{1,2,0:T(8,128)(2,1)}), bf16[4,128,768]{1,2,0:T(8,128)(2,1)}, u32[]{:S(2)}, u32[]{:S(2)}) async-start(bf16[4,128,768]{1,2,0:T(8,128)(2,1)} %copy.484), calls=%async_computation.11 | async-start | bytes 1572864 | tf_op jit(solution)/shard_map/all_to_all | solution.py:318
  675.4 21.7 %all-to-all-start.7 = ((bf16[4,128,768]{1,2,0:T(8,128)(2,1)}), bf16[4,128,768]{1,2,0:T(8,128)(2,1)}, u32[]{:S(2)}, u32[]{:S(2)}) async-start(bf16[4,128,768]{1,2,0:T(8,128)(2,1)} %copy.456), calls=%async_computation.7 | async-start | bytes 1572864 | tf_op jit(solution)/shard_map/all_to_all | solution.py:318
  680.6 23.5 %reduce-scatter.7.cloned.1.call-start = ((), (), s32[]{:S(2)}) async-start(), calls=%async_computation.20 | async-start | bytes 327680 | tf_op jit(solution)/shard_map/reduce_scatter | solution.py:325
  683.6 41.1 %reduce-scatter.5.cloned.1.call-start = ((), (), s32[]{:S(2)}) async-start(), calls=%async_computation.19 | async-start | bytes 327680 | tf_op jit(solution)/shard_map/reduce_scatter | solution.py:325
  692.4 437.6 %reduce-scatter.9.cloned.1.call-start = ((), (), s32[]{:S(2)}) async-start(), calls=%async_computation.21 | async-start | bytes 41361408 | tf_op jit(solution)/shard_map/reduce_scatter | solution.py:373
  733.4 5.8 collective-permute-start.3
  735.3 6.4 collective-permute-start.2
  761.8 498.5 %all-reduce.31.cloned.1.call-start = ((), (), s32[]{:S(2)}) async-start(), calls=%async_computation.23 | async-start | bytes 183296 | tf_op jit(solution)/shard_map/psum | solution.py:390
  809.9 665.2 %reduce-scatter.11.cloned.1.call-start = ((), (), s32[]{:S(2)}) async-start(), calls=%async_computation.22 | async-start | bytes 19464192 | tf_op jit(solution)/shard_map/reduce_scatter | solution.py:382
  (166 other events, 912.3 us)
Sparse Core Ops, SparseCore 0:
  10.8 90.7 all-gather.9
  104.4 90.3 all-gather.11
  197.6 94.1 all-gather.13
  683.9 20.1 reduce-scatter.6
  706.8 17.8 reduce-scatter.4
  761.9 368.0 reduce-scatter.8
  1137.6 122.5 all-reduce.30
  1267.2 207.8 reduce-scatter.10
where the time goes:
time: 1500 us; the launch traced here: 1490 us
  waiting for transfers between devices  684 us (46%)
  matrix products  216 us (14%)
  local copies, waits for them, and re-layouts  179 us (12%)
  blocking collectives  177 us (12%)
  other arithmetic  140 us (9%)
  starting transfers between devices  77 us (5%)
  between operations  17.4 us (1%)
    reduce_scatter x1, waiting for transfers between devices, shards(): lax.psum_scatter(lax.dot_general(part, proj_all, (((0,), (0,)), ((), ()))...  294 us
    reduce_scatter x1, waiting for transfers between devices, shards(): lax.psum_scatter(lax.dot_general(part, cot_all, (((0,), (0,)), ((), ())),...  215 us
    psum x1, waiting for transfers between devices, shards(): lax.psum((norm_total, taps_total, cbias_total, dtb_total, alog_total, ski...  125 us
    all_gather x1, blocking collectives, fetch(): lax.all_gather(dt_proj, ('dp', 'ctx', 'hd'), axis=0, tiled=True)  76.8 us
    all_gather x6, blocking collectives, carried_in(): lax.all_gather(part.astype(kind), axis)  67.1 us
    dot_general x8, matrix products, back_dot(): lax.dot_general(grad_val, weight, (((1,), (1,)), ((), ())), preferred_ele...  54.5 us
    dot_general x6, matrix products, block_ssd(): y_part = jnp.einsum('ctsh,cshp->cthp', mix_w, x_groups, precision=HIGH)  37.6 us
    all_gather x2, blocking collectives, shards(): bc_all = lax.all_gather(bc_low, 'hd', axis=0, tiled=True)  32.6 us
  transfers between devices with their start and end apart: 24, of which 10 were waited for; matrix products, arithmetic and copies ran while one was open for 24% of the time, Pallas kernels for 0%

commit v1 on v0

v1 whole, which is shorter than its diff:
```python
import jax
import jax.numpy as jnp
from jax import lax
from jax.experimental import pallas as pl
from jax.experimental.pallas import tpu as pltpu
from jax.sharding import Mesh, PartitionSpec as P

H = 48
PS = 64
N = 128
KW = 4
DI = 3072
GROUP = 4
HG = H // GROUP
XW = HG * PS
CW = XW + 2 * N
AW = CW + 128
QC = 128
EPS = 1e-05
NEG = -1e30
BF = jnp.bfloat16
F4 = jnp.float32
HIGH = lax.Precision.HIGHEST
LIMIT = 48 * 1024 * 1024
SUMS = ("dp", "ctx", "hh")
EVERY = ("dp", "ctx", "hh", "hl")


def swap(part, axis, k):
    count = lax.axis_size(axis)
    return lax.ppermute(part, axis, [(i, i ^ k) for i in range(count)])


def shift(part, axes, by):
    count = 1
    for axis in axes:
        count = count * lax.axis_size(axis)
    pairs = [(i, i + by) for i in range(count) if 0 <= i + by < count]
    return lax.ppermute(part, axes, pairs)


def mm(a, b):
    return jnp.dot(a, b, preferred_element_type=F4)


def mm_nt(a, b):
    return lax.dot_general(a, b, (((1,), (1,)), ((), ())), preferred_element_type=F4)


def mm_tn(a, b):
    return lax.dot_general(a, b, (((0,), (0,)), ((), ())), preferred_element_type=F4)


def spread(v, e):
    hi = v.astype(BF)
    lo = (v - hi.astype(F4)).astype(BF)
    return mm(hi, e) + mm(lo, e)


def gather_heads(w, e):
    hi = w.astype(BF)
    lo = (w - hi.astype(F4)).astype(BF)
    return mm_nt(hi, e) + mm_nt(lo, e)


def sigmoid(v):
    return 1.0 / (1.0 + jnp.exp(-v))


def tri():
    r = lax.broadcasted_iota(jnp.int32, (QC, QC), 0)
    c = lax.broadcasted_iota(jnp.int32, (QC, QC), 1)
    return r, c


def col_of(row):
    return jnp.transpose(jnp.broadcast_to(row, (QC, QC)))


def wide(col):
    return jnp.concatenate([col] * (XW // 128), axis=1)


def order_kernel(norm, place, own, r1, r2, r3, gain, out):
    here = place[0]
    for k, ref in enumerate((own, r1, r2, r3)):
        slot = jnp.bitwise_xor(here, k)
        rows = ref.shape[0]
        at = pl.ds(pl.multiple_of(slot * rows, rows), rows)
        if norm:
            v = ref[...].astype(F4)
            scale = lax.rsqrt(jnp.mean(v * v, axis=-1, keepdims=True) + EPS)
            out[at, :] = (v * scale * gain[...]).astype(BF)
        else:
            out[at, :] = ref[...]


def ordered(norm, place, pieces, gain):
    rows, width = pieces[0].shape
    vm = pl.BlockSpec(memory_space=pltpu.VMEM)
    return pl.pallas_call(
        lambda *refs: order_kernel(norm, *refs),
        out_shape=jax.ShapeDtypeStruct((GROUP * rows, width), BF),
        in_specs=[pl.BlockSpec(memory_space=pltpu.SMEM)] + [vm] * 5,
        out_specs=vm,
        compiler_params=pltpu.CompilerParams(vmem_limit_bytes=LIMIT),
        name="order_norm" if norm else "order_copy",
    )(place, *pieces, gain)


def rows_of(width):
    return pl.BlockSpec((QC, width), lambda i: (i, 0))


def fixed(*shape):
    return pl.BlockSpec(shape, lambda i: (0,) * len(shape))


META = pl.BlockSpec((1, 8, 128), lambda i: (i, 0, 0))


def front_kernel(raw, halo, meta, taps, hp, e, x_o, bc_o, cum_o, dt_o, st_o, dec_o, buf, act, st, dec):
    i = pl.program_id(0)

    @pl.when(i == 0)
    def _():
        buf[0:8, :] = halo[...].astype(F4)
        st[...] = jnp.zeros_like(st)
        dec[...] = jnp.ones_like(dec)

    @pl.when(i > 0)
    def _():
        buf[0:8, :] = buf[QC : QC + 8, :]

    buf[8 : QC + 8, :] = raw[:, :CW].astype(F4)
    mt = meta[0]
    masks = [col_of(mt[3 + k : 4 + k, :]) for k in range(3)]
    for j in range(CW // 128):
        c = slice(j * 128, j * 128 + 128)
        mixed = taps[4:5, c] + taps[3:4, c] * buf[8 : QC + 8, c]
        for k in range(3):
            mixed = mixed + taps[k : k + 1, c] * buf[5 + k : 5 + k + QC, c] * masks[k]
        act[:, c] = (mixed * sigmoid(mixed)).astype(BF)
    x = act[:, :XW]
    x_o[...] = x
    bc_o[...] = act[:, XW:]
    v = raw[:, CW:].astype(F4) + hp[0:1, :]
    dt = jnp.maximum(v, 0.0) + jnp.log1p(jnp.exp(-jnp.abs(v)))
    la = dt * hp[1:2, :]
    r, c = tri()
    cum = jnp.dot((r >= c).astype(F4), la, precision=HIGH, preferred_element_type=F4)
    cum_o[...] = cum
    dt_o[...] = dt
    same_last = col_of((mt[0:1, :] == mt[2:3, :]).astype(F4))
    last = cum[QC - 1 : QC, :]
    tail = jnp.exp(last - cum) * same_last * dt
    lead_last = jnp.exp(last) * (mt[1:2, :] == mt[2:3, :]).astype(F4)
    xw = (x.astype(F4) * spread(tail, e[...])).astype(BF)
    grow = spread(jnp.broadcast_to(lead_last, (8, 128)), e[...])[0:1, :]
    st[...] = st[...] * grow + mm_tn(act[:, XW : XW + N], xw)
    dec[...] = dec[...] * lead_last
    st_o[...] = st[...].astype(BF)
    dec_o[...] = dec[...]


def front(raw, halo, meta, taps, hp, e):
    length = raw.shape[0]
    sd = jax.ShapeDtypeStruct
    return pl.pallas_call(
        front_kernel,
        grid=(length // QC,),
        in_specs=[rows_of(AW), fixed(8, CW), META, fixed(8, CW), fixed(8, 128), fixed(128, XW)],
        out_specs=[rows_of(XW), rows_of(2 * N), rows_of(128), rows_of(128), fixed(N, XW), fixed(8, 128)],
        out_shape=[
            sd((length, XW), BF),
            sd((length, 2 * N), BF),
            sd((length, 128), F4),
            sd((length, 128), F4),
            sd((N, XW), BF),
            sd((8, 128), F4),
        ],
        scratch_shapes=[
            pltpu.VMEM((QC + 8, CW), F4),
            pltpu.VMEM((QC, CW), BF),
            pltpu.VMEM((N, XW), F4),
            pltpu.VMEM((8, 128), F4),
        ],
        compiler_params=pltpu.CompilerParams(vmem_limit_bytes=LIMIT),
        name="conv_state",
    )(raw, halo, meta, taps, hp, e)


def scan_kernel(x_r, bc, cum_r, dt_r, meta, s_in, z_r, dg_r, skip, gain, e, y_o, ent_o, sum_o, st, y_s):
    i = pl.program_id(0)

    @pl.when(i == 0)
    def _():
        st[...] = s_in[...].astype(F4)

    mt = meta[0]
    x = x_r[...]
    b = bc[:, :N]
    c = bc[:, N:]
    cum = cum_r[...]
    dt = dt_r[...]
    r, q = tri()
    keep = col_of((mt[0:1, :] == mt[1:2, :]).astype(F4))
    inside = (col_of(mt[0:1, :]) == mt[0:1, :]) & (r >= q)
    scores = mm_nt(c, b)
    before = st[...].astype(BF)
    ent_o[0] = before
    lead = jnp.exp(cum) * keep
    y_s[...] = spread(lead, e[...]) * mm(c, before) + skip[...] * x.astype(F4)
    cum_t = jnp.transpose(cum)
    dt_t = jnp.transpose(dt)
    lane = lax.broadcasted_iota(jnp.int32, (1, 128), 1)
    halves = [(lane < PS).astype(BF), (lane >= PS).astype(BF)]
    for j in range(HG // 2):
        at = slice(j * 128, j * 128 + 128)
        xp = x[:, at]
        part = jnp.zeros((QC, 128), F4)
        for half in range(2):
            h = 2 * j + half
            gap = jnp.where(inside, cum[:, h : h + 1] - cum_t[h : h + 1, :], NEG)
            w = (scores * jnp.exp(gap) * dt_t[h : h + 1, :]).astype(BF)
            part = part + mm(w, xp * halves[half])
        y_s[:, at] = y_s[:, at] + part
    same_last = col_of((mt[0:1, :] == mt[2:3, :]).astype(F4))
    last = cum[QC - 1 : QC, :]
    tail = jnp.exp(last - cum) * same_last * dt
    lead_last = jnp.exp(last) * (mt[1:2, :] == mt[2:3, :]).astype(F4)
    xw = (x.astype(F4) * spread(tail, e[...])).astype(BF)
    grow = spread(jnp.broadcast_to(lead_last, (8, 128)), e[...])[0:1, :]
    st[...] = st[...] * grow + mm_tn(b, xw)
    squares = jnp.zeros((QC, 128), F4)
    along = jnp.zeros((QC, 128), F4)
    for j in range(XW // 128):
        at = slice(j * 128, j * 128 + 128)
        low = y_s[:, at].astype(BF)
        y_o[:, at] = low
        z = z_r[:, at]
        s = low.astype(F4) * z * sigmoid(z)
        squares = squares + s * s
        along = along + s * gain[:, at] * dg_r[:, at]
    sum_o[0] = jnp.concatenate(
        [
            jnp.sum(jnp.transpose(squares), axis=0, keepdims=True),
            jnp.sum(jnp.transpose(along), axis=0, keepdims=True),
            jnp.zeros((6, QC), F4),
        ],
        axis=0,
    )


def scan(x, bc, cum, dt, meta, s_in, z, dg, skip, gain, e):
    length = x.shape[0]
    chunks = length // QC
    sd = jax.ShapeDtypeStruct
    return pl.pallas_call(
        scan_kernel,
        grid=(chunks,),
        in_specs=[
            rows_of(XW),
            rows_of(2 * N),
            rows_of(128),
            rows_of(128),
            META,
            fixed(N, XW),
            rows_of(XW),
            rows_of(XW),
            fixed(1, XW),
            fixed(1, XW),
            fixed(128, XW),
        ],
        out_specs=[rows_of(XW), pl.BlockSpec((1, N, XW), lambda i: (i, 0, 0)), META],
        out_shape=[sd((length, XW), BF), sd((chunks, N, XW), BF), sd((chunks, 8, 128), F4)],
        scratch_shapes=[pltpu.VMEM((N, XW), F4), pltpu.VMEM((QC, XW), F4)],
        compiler_params=pltpu.CompilerParams(vmem_limit_bytes=LIMIT),
        name="scan_gate",
    )(x, bc, cum, dt, meta, s_in, z, dg, skip, gain, e)


def gate_kernel(y_r, z_r, dg_r, tot, bc, cum_r, meta, gain, e, gated_o, dy_o, dz_o, gg_o, ds_o, ds, gg):
    i = pl.program_id(0)

    @pl.when(i == 0)
    def _():
        ds[...] = jnp.zeros_like(ds)
        gg[...] = jnp.zeros_like(gg)

    mt = meta[0]
    cum = cum_r[...]
    rstd = col_of(lax.rsqrt(tot[0, 0:1, :] * (1.0 / DI) + EPS))
    pull = col_of(tot[0, 1:2, :]) * (rstd * rstd * rstd) * (1.0 / DI)
    keep = col_of((mt[0:1, :] == mt[1:2, :]).astype(F4))
    lead = spread(jnp.exp(cum) * keep, e[...])
    for j in range(XW // 128):
        at = slice(j * 128, j * 128 + 128)
        y = y_r[:, at].astype(F4)
        z = z_r[:, at]
        sig = sigmoid(z)
        act = z * sig
        s = y * act
        n = s * rstd
        g = gain[:, at]
        dg = dg_r[:, at]
        gated_o[:, at] = (n * g).astype(BF)
        gg[0:1, at] = gg[0:1, at] + jnp.sum(dg * n, axis=0, keepdims=True)
        d_s = rstd * dg * g - s * pull
        dy_o[:, at] = (d_s * act).astype(BF)
        dz_o[:, at] = (d_s * y * sig * (1.0 + z * (1.0 - sig))).astype(BF)
    last = cum[QC - 1 : QC, :]
    lead_last = jnp.exp(last) * (mt[1:2, :] == mt[2:3, :]).astype(F4)
    grow = spread(jnp.broadcast_to(lead_last, (8, 128)), e[...])[0:1, :]
    led = (dy_o[...].astype(F4) * lead).astype(BF)
    ds[...] = ds[...] * grow + mm_tn(bc[:, N:], led)
    ds_o[...] = ds[...].astype(BF)
    gg_o[...] = gg[...]


def gate(y, z, dg, tot, bc, cum, meta, gain, e):
    length = y.shape[0]
    n = length // QC
    sd = jax.ShapeDtypeStruct

    def back(width):
        return pl.BlockSpec((QC, width), lambda i: (n - 1 - i, 0))

    bmeta = pl.BlockSpec((1, 8, 128), lambda i: (n - 1 - i, 0, 0))
    return pl.pallas_call(
        gate_kernel,
        grid=(n,),
        in_specs=[
            back(XW),
            back(XW),
            back(XW),
            bmeta,
            back(2 * N),
            back(128),
            bmeta,
            fixed(1, XW),
            fixed(128, XW),
        ],
        out_specs=[back(XW), back(XW), back(XW), fixed(8, XW), fixed(N, XW)],
        out_shape=[
            sd((length, XW), BF),
            sd((length, XW), BF),
            sd((length, XW), BF),
            sd((8, XW), F4),
            sd((N, XW), BF),
        ],
        scratch_shapes=[pltpu.VMEM((N, XW), F4), pltpu.VMEM((8, XW), F4)],
        compiler_params=pltpu.CompilerParams(vmem_limit_bytes=LIMIT),
        name="gate_back",
    )(y, z, dg, tot, bc, cum, meta, gain, e)


def back_kernel(
    x_r, bc, cum_r, dt_r, meta, ent, dy_r, d_end, raw, raw_before, halo, taps, hp, skip, e,
    draw_o, rim_o, cg_o, hg_o,
    ds, dx_s, act, buf, ebuf, carry, rowbuf, cg, hg,
):
    i = pl.program_id(0)
    n = pl.num_programs(0)
    first = i == n - 1

    @pl.when(i == 0)
    def _():
        ds[...] = d_end[...].astype(F4)
        carry[...] = jnp.zeros_like(carry)
        cg[...] = jnp.zeros_like(cg)
        hg[...] = jnp.zeros_like(hg)
        rowbuf[...] = jnp.zeros_like(rowbuf)

    mt = meta[0]
    ev = e[...]
    x = x_r[...]
    dy = dy_r[...]
    xf = x.astype(F4)
    dyf = dy.astype(F4)
    b = bc[:, :N]
    c = bc[:, N:]
    cum = cum_r[...]
    dt = dt_r[...]
    r, q = tri()
    keep = col_of((mt[0:1, :] == mt[1:2, :]).astype(F4))
    same_last = col_of((mt[0:1, :] == mt[2:3, :]).astype(F4))
    inside = (col_of(mt[0:1, :]) == mt[0:1, :]) & (r >= q)
    scores = mm_nt(c, b)
    before = ent[0]
    after = ds[...].astype(BF)
    last = cum[QC - 1 : QC, :]
    lead = spread(jnp.exp(cum) * keep, ev)
    tail0 = spread(jnp.exp(last - cum) * same_last, ev)
    dtw = spread(dt, ev)
    lead_last = jnp.exp(last) * (mt[1:2, :] == mt[2:3, :]).astype(F4)
    u = tail0 * mm(b, after)
    led = dyf * lead
    tq0 = gather_heads(xf * u, ev)
    lv = gather_heads(led * mm(c, before), ev)
    dx_s[...] = dtw * u + skip[...] * dyf
    xw = (xf * tail0 * dtw).astype(BF)
    ledb = led.astype(BF)
    d_b = mm_nt(xw, after)
    d_c = mm_nt(ledb, before)
    flow = jnp.sum(ds[...] * before.astype(F4), axis=0, keepdims=True)
    passed = jnp.sum(dyf * xf, axis=0, keepdims=True)
    heads2 = gather_heads(jnp.concatenate([flow, passed, jnp.zeros((6, XW), F4)], axis=0), ev)
    grow = spread(jnp.broadcast_to(lead_last, (8, 128)), ev)[0:1, :]
    ds[...] = ds[...] * grow + mm_tn(c, ledb)
    cum_t = jnp.transpose(cum)
    dt_t = jnp.transpose(dt)
    lane = lax.broadcasted_iota(jnp.int32, (1, 128), 1)
    halves = [(lane < PS).astype(BF), (lane >= PS).astype(BF)]
    d_sc = jnp.zeros((QC, QC), F4)
    rows = jnp.zeros((QC, 128), F4)
    for j in range(HG // 2):
        at = slice(j * 128, j * 128 + 128)
        xp = x[:, at]
        dyp = dy[:, at]
        part = jnp.zeros((QC, 128), F4)
        for half in range(2):
            h = 2 * j + half
            gap = jnp.where(inside, cum[:, h : h + 1] - cum_t[h : h + 1, :], NEG)
            dec = jnp.exp(gap)
            dtr = dt_t[h : h + 1, :]
            sl = scores * dec
            d_m = mm_nt(dyp, xp * halves[half])
            g = d_m * sl
            rowbuf[h : h + 1, :] = jnp.sum(g, axis=0, keepdims=True)
            rows = rows + jnp.where(lane == h, jnp.sum(g * dtr, axis=1, keepdims=True), 0.0)
            d_sc = d_sc + d_m * dec * dtr
            part = part + mm_tn((sl * dtr).astype(BF), dyp * halves[half])
        dx_s[:, at] = dx_s[:, at] + part
    d_scb = d_sc.astype(BF)
    d_c = d_c + mm(d_scb, b)
    d_b = d_b + mm_tn(d_scb, c)
    ecol = jnp.transpose(rowbuf[...])
    tq = tq0 * dt
    at_end = jnp.sum(tq, axis=0, keepdims=True) + lead_last * heads2[0:1, :]
    token = lax.broadcasted_iota(jnp.int32, (QC, 128), 0)
    d_cum = rows - dt * ecol - tq + lv + jnp.where(token == QC - 1, at_end, 0.0)
    d_la = jnp.dot((r <= q).astype(F4), d_cum, precision=HIGH, preferred_element_type=F4)
    neg = hp[1:2, :]
    v = raw[:, CW:].astype(F4) + hp[0:1, :]
    d_rate = (ecol + tq0 + d_la * neg) * sigmoid(v)
    draw_o[:, CW:] = d_rate.astype(BF)
    hg[0:1, :] = hg[0:1, :] + jnp.sum(d_rate, axis=0, keepdims=True)
    hg[1:2, :] = hg[1:2, :] + jnp.sum(d_la * dt * neg, axis=0, keepdims=True)
    hg[2:3, :] = hg[2:3, :] + heads2[1:2, :]
    act[:, :XW] = dx_s[...].astype(BF).astype(F4)
    act[:, XW : XW + N] = d_b
    act[:, XW + N :] = d_c

    @pl.when(first)
    def _():
        buf[0:8, :] = halo[...].astype(F4)

    @pl.when(jnp.logical_not(first))
    def _():
        buf[0:8, :] = raw_before[QC - 8 : QC, :CW].astype(F4)

    buf[8 : QC + 8, :] = raw[:, :CW].astype(F4)
    masks = [col_of(mt[3 + k : 4 + k, :]) for k in range(3)]
    ebuf[0:8, :] = jnp.zeros((8, 128), F4)
    for j in range(CW // 128):
        at = slice(j * 128, j * 128 + 128)
        own = buf[8 : QC + 8, at]
        shifted = [buf[5 + k : 5 + k + QC, at] * masks[k] for k in range(3)]
        mixed = taps[4:5, at] + taps[3:4, at] * own
        for k in range(3):
            mixed = mixed + taps[k : k + 1, at] * shifted[k]
        sig = sigmoid(mixed)
        dm = act[:, at] * (sig * (1.0 + mixed * (1.0 - sig)))
        sums = [jnp.sum(dm * s, axis=0, keepdims=True) for s in (*shifted, own)]
        sums.append(jnp.sum(dm, axis=0, keepdims=True))
        cg[0:5, at] = cg[0:5, at] + jnp.concatenate(sums, axis=0)
        d_raw = taps[3:4, at] * dm
        rim = jnp.zeros((8, 128), F4)
        for k in range(3):
            ek = taps[k : k + 1, at] * dm * masks[k]
            ebuf[8 : QC + 8, :] = ek
            ebuf[QC + 8 : QC + 16, :] = carry[8 * k : 8 * k + 8, at]
            d_raw = d_raw + ebuf[11 - k : 11 - k + QC, :]
            rim = rim + ebuf[3 - k : 11 - k, :]
            carry[8 * k : 8 * k + 8, at] = ek[0:8, :]
        draw_o[:, at] = d_raw.astype(BF)
        rim_o[:, at] = rim.astype(BF)
    cg_o[...] = cg[...]
    hg_o[...] = hg[...]


def scan_back(x, bc, cum, dt, meta, ent, dy, d_end, raw, halo, taps, hp, skip, e):
    length = x.shape[0]
    n = length // QC
    sd = jax.ShapeDtypeStruct

    def back(width):
        return pl.BlockSpec((QC, width), lambda i: (n - 1 - i, 0))

    bmeta = pl.BlockSpec((1, 8, 128), lambda i: (n - 1 - i, 0, 0))
    return pl.pallas_call(
        back_kernel,
        grid=(n,),
        in_specs=[
            back(XW),
            back(2 * N),
            back(128),
            back(128),
            bmeta,
            pl.BlockSpec((1, N, XW), lambda i: (n - 1 - i, 0, 0)),
            back(XW),
            fixed(N, XW),
            back(AW),
            pl.BlockSpec((QC, AW), lambda i: (jnp.maximum(n - 2 - i, 0), 0)),
            fixed(8, CW),
            fixed(8, CW),
            fixed(8, 128),
            fixed(1, XW),
            fixed(128, XW),
        ],
        out_specs=[back(AW), fixed(8, CW), fixed(8, CW), fixed(8, 128)],
        out_shape=[sd((length, AW), BF), sd((8, CW), BF), sd((8, CW), F4), sd((8, 128), F4)],
        scratch_shapes=[
            pltpu.VMEM((N, XW), F4),
            pltpu.VMEM((QC, XW), F4),
            pltpu.VMEM((QC, CW), F4),
            pltpu.VMEM((QC + 8, CW), F4),
            pltpu.VMEM((QC + 16, 128), F4),
            pltpu.VMEM((24, CW), F4),
            pltpu.VMEM((128, 128), F4),
            pltpu.VMEM((8, CW), F4),
            pltpu.VMEM((8, 128), F4),
        ],
        compiler_params=pltpu.CompilerParams(vmem_limit_bytes=LIMIT),
        name="scan_back",
    )(x, bc, cum, dt, meta, ent, dy, d_end, raw, raw, halo, taps, hp, skip, e)


def pad_lanes(v, width):
    return jnp.pad(v, [(0, 0)] * (v.ndim - 1) + [(0, width - v.shape[-1])])


def carried(state, decay, hops, by):
    chain = ("ctx", "hh")
    total = shift(state, chain, by)
    if hops == 1:
        return total
    far, fade = state, decay
    total, product = jnp.zeros(state.shape, F4), jnp.ones(decay.shape, F4)
    for _ in range(hops):
        far = shift(far, chain, by)
        total = total + product * far.astype(F4)
        fade = shift(fade, chain, by)
        product = product * fade
    return total.astype(BF)


def shards(
    tokens_in, seg_ids, in_norm, z_proj, xbc_proj, dt_proj, conv_taps, conv_bias,
    dt_bias, a_log, d_skip, gate_norm, out_proj, out_cotangent,
):
    seqs, rows, width = tokens_in.shape
    length = seg_ids.shape[1]
    block = rows * GROUP
    chunks = block // QC
    chain = ("ctx", "hh")
    n_blocks = length // block
    hops = min(-(-(length // 4 - 1) // block), n_blocks - 1)
    n_sums = lax.axis_size("dp") * n_blocks
    hl = lax.axis_index("hl")
    place = hl.astype(jnp.int32).reshape(1)
    own_rows = z_proj.shape[0]

    def quarters(w):
        return w.reshape(w.shape[0], GROUP, -1).transpose(1, 0, 2)

    bc_cols = jnp.broadcast_to(xbc_proj[None, :, DI:], (GROUP, own_rows, 2 * N))
    wx_parts = jnp.concatenate(
        [quarters(xbc_proj[:, :DI]), bc_cols, pad_lanes(quarters(dt_proj), 128)], axis=-1
    )
    wx_mine = lax.all_to_all(wx_parts, "hl", 0, 0, tiled=True).reshape(GROUP * own_rows, AW)
    wx = lax.all_gather(wx_mine, SUMS, axis=0, tiled=True)
    wz_mine = lax.all_to_all(quarters(z_proj), "hl", 0, 0, tiled=True).reshape(GROUP * own_rows, XW)
    wz = lax.all_gather(wz_mine, SUMS, axis=0, tiled=True)
    pairs = [(f, (f % n_sums) * GROUP + f // n_sums) for f in range(GROUP * n_sums)]
    wo_mine = lax.ppermute(out_proj, EVERY, pairs)
    wo = lax.all_gather(wo_mine, SUMS, axis=0, tiled=True)

    def mine(v, size):
        return lax.dynamic_slice_in_dim(v, hl * size, size, axis=-1)

    taps = jnp.concatenate([conv_taps, conv_bias[None]], axis=0)
    taps = jnp.concatenate([mine(taps[:, :DI], XW), taps[:, DI:]], axis=1)
    taps = jnp.pad(taps, ((0, 3), (0, 0)))
    hp = jnp.stack([mine(dt_bias, HG), -jnp.exp(mine(a_log, HG))])
    hp = jnp.pad(hp, ((0, 6), (0, 128 - HG)))
    skip = jnp.repeat(mine(d_skip, HG), PS)[None]
    gain = mine(gate_norm, XW)[None]
    e = (jnp.arange(128)[:, None] == jnp.arange(XW)[None, :] // PS).astype(BF)
    in_gain = in_norm[None]

    start = lax.axis_index(chain) * block
    seg_pad = jnp.concatenate([jnp.full((seqs, 8), -1, jnp.int32), seg_ids], axis=1)
    near = lax.dynamic_slice_in_dim(seg_pad, start, block + 8, axis=1)
    seg = near[:, 8:].reshape(seqs, chunks, QC)
    lines = [seg, jnp.broadcast_to(near[:, 7 : 7 + block : QC][:, :, None], seg.shape)]
    lines.append(jnp.broadcast_to(seg[:, :, QC - 1 :], seg.shape))
    for k in range(KW - 1):
        lines.append((near[:, 5 + k : 5 + k + block].reshape(seg.shape) == seg).astype(jnp.int32))
    lines.extend([jnp.zeros_like(seg)] * 2)
    meta = jnp.stack(lines, axis=2).astype(F4)

    def collected(part, norm):
        others = [swap(part, "hl", k) for k in range(1, GROUP)]
        return ordered(norm, place, [part, *others], in_gain)

    def spread_sum(part):
        def piece(k):
            at = jnp.bitwise_xor(hl, k) * rows
            return lax.dynamic_slice_in_dim(part, at, rows)

        total = piece(0).astype(F4)
        for k in range(1, GROUP):
            total = total + swap(piece(k), "hl", k).astype(F4)
        return total

    normed = [collected(tokens_in[s], True) for s in range(seqs)]
    cot = [collected(out_cotangent[s], False) for s in range(seqs)]
    kept = []
    for s in range(seqs):
        raw = mm(normed[s], wx).astype(BF)
        halo = shift(raw[block - 8 :, :CW], chain, 1)
        x, bc, cum, dt, state, decay = front(raw, halo, meta[s], taps, hp, e)
        decay_row = jnp.repeat(decay[0, :HG], PS)[None]
        kept.append((raw, halo, x, bc, cum, dt, carried(state, decay_row, hops, 1), decay_row))
    gates = [mm(normed[s], wz) for s in range(seqs)]
    d_gated = [mm_nt(cot[s], wo) for s in range(seqs)]
    outs = []
    middle = []
    out_grad = 0.0
    gate_total = 0.0
    for s in range(seqs):
        raw, halo, x, bc, cum, dt, s_in, decay_row = kept[s]
        y, ent, sums = scan(x, bc, cum, dt, meta[s], s_in, gates[s], d_gated[s], skip, gain, e)
        tot = sums
        for k in range(1, GROUP):
            tot = tot + swap(sums, "hl", k)
        gated, dy, dz, gg, d_state = gate(y, gates[s], d_gated[s], tot, bc, cum, meta[s], gain, e)
        d_end = carried(d_state, decay_row, hops, -1)
        gate_total = gate_total + gg[0]
        out_grad = out_grad + mm_tn(gated, cot[s])
        summed = spread_sum(mm(gated, wo).astype(BF))
        outs.append((tokens_in[s].astype(F4) + summed).astype(BF))
        middle.append((ent, dy, dz, d_end))
    out_part = lax.psum_scatter(out_grad.astype(BF), SUMS, scatter_dimension=0, tiled=True)
    back_pairs = [(b, a) for a, b in pairs]
    out_proj_grad = lax.ppermute(out_part, EVERY, back_pairs).astype(F4)
    z_grad = 0.0
    for s in range(seqs):
        z_grad = z_grad + mm_tn(normed[s], middle[s][2])

    def columns(grad, n_cols):
        part = lax.psum_scatter(grad.astype(BF), SUMS, scatter_dimension=0, tiled=True)
        parts = part.reshape(GROUP, own_rows, n_cols)
        return lax.all_to_all(parts, "hl", 0, 0, tiled=True).astype(F4)

    z_parts = columns(z_grad, XW)
    z_proj_grad = z_parts.transpose(1, 0, 2).reshape(own_rows, DI)
    x_grad = 0.0
    conv_total = 0.0
    head_total = 0.0
    norm_total = 0.0
    grads_tok = []
    for s in range(seqs):
        raw, halo, x, bc, cum, dt, _, _ = kept[s]
        ent, dy, dz, d_end = middle[s]
        draw, rim, cg, hg = scan_back(
            x, bc, cum, dt, meta[s], ent, dy, d_end, raw, halo, taps, hp, skip, e
        )
        conv_total = conv_total + cg
        head_total = head_total + hg
        rim = shift(rim, chain, -1)
        draw = draw.at[block - 8 :, :CW].add(rim)
        x_grad = x_grad + mm_tn(normed[s], draw)
        d_normed = mm_nt(dz, wz) + mm_nt(draw, wx)
        norm_total = norm_total + jnp.sum(d_normed * normed[s].astype(F4), axis=0)
        summed = spread_sum(d_normed.astype(BF))
        u = tokens_in[s].astype(F4)
        scale = lax.rsqrt(jnp.mean(u * u, axis=-1, keepdims=True) + EPS)
        hat = u * scale
        dh = summed * in_norm
        d_u = scale * (dh - hat * jnp.mean(dh * hat, axis=-1, keepdims=True))
        grads_tok.append(d_u + out_cotangent[s].astype(F4))
    x_parts = columns(x_grad, AW)
    xs = x_parts[:, :, :XW].transpose(1, 0, 2).reshape(own_rows, DI)
    xbc_proj_grad = jnp.concatenate([xs, jnp.sum(x_parts[:, :, XW:CW], axis=0)], axis=1)
    dt_proj_grad = x_parts[:, :, CW : CW + HG].transpose(1, 0, 2).reshape(own_rows, H)

    pieces = [
        conv_total[:5, :XW].reshape(-1),
        gate_total,
        head_total[:3].reshape(-1),
        conv_total[:5, XW:].reshape(-1),
        norm_total / in_norm,
    ]
    sizes = [p.shape[0] for p in pieces]
    pack = jnp.concatenate(pieces)
    lines_n = -(-pack.shape[0] // 1024) * 8
    pack = jnp.pad(pack, (0, lines_n * 128 - pack.shape[0])).reshape(lines_n, 128)
    for axis in SUMS:
        k = 1
        while k < lax.axis_size(axis):
            pack = pack + swap(pack, axis, k)
            k = 2 * k
    got = [pack] + [swap(pack, "hl", k) for k in range(1, GROUP)]
    for bit in (1, 2):
        odd = (hl & bit) > 0
        got = [jnp.where(odd, got[j ^ bit], got[j]) for j in range(GROUP)]
    flat = jnp.stack(got).reshape(GROUP, -1)
    cuts = []
    low = 0
    for size in sizes:
        cuts.append(flat[:, low : low + size])
        low = low + size
    conv_x = cuts[0].reshape(GROUP, 5, XW).transpose(1, 0, 2).reshape(5, DI)
    conv_all = jnp.concatenate([conv_x, jnp.sum(cuts[3], axis=0).reshape(5, 2 * N)], axis=1)
    per_head = cuts[2].reshape(GROUP, 3, 128)[:, :, :HG].transpose(1, 0, 2).reshape(3, H)
    return (
        jnp.stack(outs),
        jnp.stack(grads_tok),
        jnp.sum(cuts[4], axis=0),
        z_proj_grad,
        xbc_proj_grad,
        dt_proj_grad,
        conv_all[:4],
        conv_all[4],
        per_head[0],
        per_head[1],
        per_head[2],
        cuts[1].reshape(DI),
        out_proj_grad,
    )


def solution(mesh):
    sizes = dict(mesh.shape)
    grid = mesh.devices.reshape(sizes["dp"], sizes["ctx"], sizes["hd"] // GROUP, GROUP)
    fine = Mesh(grid, ("dp", "ctx", "hh", "hl"))
    tok = P("dp", ("ctx", "hh", "hl"), None)
    wgt = P(("dp", "ctx", "hh", "hl"), None)
    in_specs = (tok, P("dp", None), P(), wgt, wgt, wgt, P(), P(), P(), P(), P(), P(), wgt, tok)
    out_specs = (tok, tok, P(), wgt, wgt, wgt, P(), P(), P(), P(), P(), P(), wgt)
    return jax.shard_map(shards, mesh=fine, in_specs=in_specs, out_specs=out_specs, check_vma=False)
```

time: 1500 us -> 551 us (0.37)
  waiting for transfers between devices: 684 us -> 158 us
  matrix products: 216 us -> 56.1 us
  blocking collectives: 177 us -> 32 us
  local copies, waits for them, and re-layouts: 179 us -> 38.7 us
  other arithmetic: 140 us -> 22.1 us
  starting transfers between devices: 77 us -> 156 us
  Pallas kernels: 0 us -> 62.1 us
    reduce_scatter x4 -> x3, waiting for transfers between devices: 530 us -> 0.02 us  [the longest x1 0.01 us: shards(): lax.psum_scatter(out_grad.astype(BF), SUMS, scatter_dimension=0, tiled=True)]
    all_gather x9 -> x0, blocking collectives: 177 us -> none  [the longest x1 76.8 us: fetch(): lax.all_gather(dt_proj, ('dp', 'ctx', 'hd'), axis=0, tiled=True)]
    dot_general x50 -> x18, matrix products: 216 us -> 56.1 us  [the longest x6 19.8 us: mm_nt(): lax.dot_general(a, b, (((1,), (1,)), ((), ())), preferred_element_type=F4)]
    ppermute x4 -> x46, starting transfers between devices: 7.88 us -> 141 us  [the longest x36 121 us: swap(): return lax.ppermute(part, axis, [(i, i ^ k) for i in range(count)])]
    ppermute x4 -> x46, waiting for transfers between devices: 4.65 us -> 134 us  [the longest x36 130 us: swap(): return lax.ppermute(part, axis, [(i, i ^ k) for i in range(count)])]
    psum x1 -> x0, waiting for transfers between devices: 125 us -> none  [shards(): lax.psum((norm_total, taps_total, cbias_total, dtb_total, alog_total, ski...]
    pallas_call x0 -> x12, Pallas kernels: none -> 62.1 us  [the longest x2 28.3 us: scan_back(): pl.pallas_call(back_kernel, grid=(n,), in_specs=[back(XW), back(2 * N), b...]
    all_to_all x12 -> x3, starting transfers between devices: 68.7 us -> 14.3 us  [the longest x2 10.9 us: columns(): return lax.all_to_all(parts, 'hl', 0, 0, tiled=True).astype(F4)]
  transfers between devices with their start and end apart: 24 -> 55, of which waited for: 10 -> 18; matrix products, arithmetic and copies ran while one was open for 24% -> 17% of each run, Pallas kernels for 0% -> 11%
where the time goes in v1:
time: 551 us; the launch traced here: 541 us
  waiting for transfers between devices  158 us (29%)
  starting transfers between devices  156 us (28%)
  Pallas kernels  62.1 us (11%)
  matrix products  56.1 us (10%)
  local copies, waits for them, and re-layouts  38.7 us (7%)
  blocking collectives  32 us (6%)
  other arithmetic  22.1 us (4%)
  between operations  16 us (3%)
    ppermute x36, waiting for transfers between devices, swap(): return lax.ppermute(part, axis, [(i, i ^ k) for i in range(count)])  130 us
    ppermute x36, starting transfers between devices, swap(): return lax.ppermute(part, axis, [(i, i ^ k) for i in range(count)])  121 us
    all_to_all x1, blocking collectives, shards(): lax.all_to_all(wx_parts, 'hl', 0, 0, tiled=True)  32 us
    pallas_call x2, Pallas kernels, scan_back(): pl.pallas_call(back_kernel, grid=(n,), in_specs=[back(XW), back(2 * N), b...  28.3 us
    unnamed x217, local copies, waits for them, and re-layouts  23.5 us
    dot_general x6, matrix products, mm_nt(): lax.dot_general(a, b, (((1,), (1,)), ((), ())), preferred_element_type=F4)  19.8 us
    all_to_all x2, waiting for transfers between devices, columns(): return lax.all_to_all(parts, 'hl', 0, 0, tiled=True).astype(F4)  19.1 us
    dot_general x6, matrix products, mm(): return jnp.dot(a, b, preferred_element_type=F4)  19 us
  transfers between devices with their start and end apart: 55, of which 18 were waited for; matrix products, arithmetic and copies ran while one was open for 17% of the time, Pallas kernels for 11%

profile of v1, /device:TPU:0, one launch (start us, length us, event | category | flops | bytes accessed | tf_op | source)
XLA Modules:
  0.0 541.0 jit_solution(2856321914717001297)
XLA Ops:
  12.0 32.0 %all_to_all.20 = bf16[4,48,1152]{2,1,0:T(8,128)(2,1)} all-to-all(bf16[4,48,1152]{2,1,0:T(8,128)(2,1)S(1)} %copy.82), channel_id=1, replica_groups=mesh['dp'=2,'ctx'=4,'hd'=4] {'hd'}, dimensions={0} | all-to-all | bytes 884736 | tf_op jit(solution)/shard_map/all_to_all | solution.py:582
  45.0 3.5 all-to-all-start.1
  53.8 4.7 all-to-all-done.1
  62.4 11.4 %collective-permute-done.15.refs_2_ = bf16[128,1536]{1,0:T(8,128)(2,1)S(1)} collective-permute-done((bf16[128,1536]{1,0:T(8,128)(2,1)S(1)}, bf16[128,1536]{1,0:T(8,128)(2,1)S(1)}, u32[]{:S(2)}, u32[]{:S(2)}) %collective-permute-start.15) | collective-permute-done | bytes 393248 | tf_op jit(solution)/shard_map/ppermute | solution.py:31
  74.6 9.2 %collective-permute-done.16.refs_3_ = bf16[128,1536]{1,0:T(8,128)(2,1)S(1)} collective-permute-done((bf16[128,1536]{1,0:T(8,128)(2,1)S(1)}, bf16[128,1536]{1,0:T(8,128)(2,1)S(1)}, u32[]{:S(2)}, u32[]{:S(2)}) %collective-permute-start.16) | collective-permute-done | bytes 393248 | tf_op jit(solution)/shard_map/ppermute | solution.py:31
  85.8 24.4 %collective-permute-start.1 = (bf16[128,1536]{1,0:T(8,128)(2,1)}, bf16[128,1536]{1,0:T(8,128)(2,1)}, u32[]{:S(2)}, u32[]{:S(2)}) collective-permute-start(bf16[128,1536]{1,0:T(8,128)(2,1)} %get-tuple-element.209.refs_1_), channel_id=1, source_target_pairs={{0,2},{1,3},{2,0},{3,1},{4,6},{5,7},{6,4},{7,5},{8,10},{9,11},{10,... | collective-permute-start | bytes 1179656 | tf_op jit(solution)/shard_map/ppermute | solution.py:31
  113.4 21.1 %collective-permute-done.21.refs_3_ = bf16[128,1536]{1,0:T(8,128)(2,1)S(1)} collective-permute-done((bf16[128,1536]{1,0:T(8,128)(2,1)S(1)}, bf16[128,1536]{1,0:T(8,128)(2,1)S(1)}, u32[]{:S(2)}, u32[]{:S(2)}) %collective-permute-start.21) | collective-permute-done | bytes 393248 | tf_op jit(solution)/shard_map/ppermute | solution.py:31
  136.0 7.9 %collective-permute-start.6 = (bf16[128,1536]{1,0:T(8,128)(2,1)}, bf16[128,1536]{1,0:T(8,128)(2,1)}, u32[]{:S(2)}, u32[]{:S(2)}) collective-permute-start(bf16[128,1536]{1,0:T(8,128)(2,1)} %get-tuple-element.207.refs_1_), channel_id=1, source_target_pairs={{0,2},{1,3},{2,0},{3,1},{4,6},{5,7},{6,4},{7,5},{8,10},{9,11},{10,... | collective-permute-start | bytes 1179656 | tf_op jit(solution)/shard_map/ppermute | solution.py:31
  155.2 13.2 %collective-permute-done.1.refs_3_ = bf16[128,1536]{1,0:T(8,128)(2,1)} collective-permute-done((bf16[128,1536]{1,0:T(8,128)(2,1)}, bf16[128,1536]{1,0:T(8,128)(2,1)}, u32[]{:S(2)}, u32[]{:S(2)}) %collective-permute-start.1) | collective-permute-done | bytes 393248 | tf_op jit(solution)/shard_map/ppermute | solution.py:31
  170.3 15.0 %collective-permute-done.6.refs_3_ = bf16[128,1536]{1,0:T(8,128)(2,1)} collective-permute-done((bf16[128,1536]{1,0:T(8,128)(2,1)}, bf16[128,1536]{1,0:T(8,128)(2,1)}, u32[]{:S(2)}, u32[]{:S(2)}) %collective-permute-start.6) | collective-permute-done | bytes 393248 | tf_op jit(solution)/shard_map/ppermute | solution.py:31
  187.9 4.8 fusion.35.dg_r
  195.3 4.3 convolution_convert_fusion.raw.raw_before
  205.4 5.0 collective-permute-start.3
  210.4 5.2 conv_state.3
  218.6 2.8 collective-permute-start.19
  221.5 3.2 fusion.34.z_r
  224.7 5.0 conv_state.2
  231.1 5.4 scan_gate.3
  236.4 7.9 %collective-permute-start.23 = (f32[4,8,128]{2,1,0:T(8,128)S(1)}, f32[4,8,128]{2,1,0:T(8,128)S(1)}, u32[]{:S(2)}, u32[]{:S(2)}) collective-permute-start(f32[4,8,128]{2,1,0:T(8,128)S(1)} %get-tuple-element.85), channel_id=1, source_target_pairs={{0,1},{1,0},{2,3},{3,2},{4,5},{5,4},{6,7},{7,6},{8,9},{9,8},{10,11... | collective-permute-start | bytes 49160 | tf_op jit(solution)/shard_map/ppermute | solution.py:31
  248.2 5.1 scan_gate.2
  257.7 4.5 gate_back.3
  262.2 3.6 fusion.38
  265.9 4.6 gate_back.2
  273.9 2.8 add_convert_fusion.1
  279.8 3.3 convolution_convert_fusion.2
  287.9 2.9 add_convert_fusion
  291.0 4.6 convolution_convert_fusion.3
  295.7 14.1 %scan_back.3 = (bf16[512,1152]{1,0:T(8,128)(2,1)S(1)}, bf16[8,1024]{1,0:T(8,128)(2,1)S(1)}, f32[8,1024]{1,0:T(8,128)S(1)}, f32[8,128]{1,0:T(8,128)S(1)}) custom-call(bf16[512,768]{1,0:T(8,128)(2,1)S(1)} %copy-done.14, bf16[512,256]{1,0:T(8,128)(2,1)S(1)} %copy-done.25, f32[512,128]{1,0:T(8,128)S(1)} %copy-done.28, f32[512,128]{1,0:T(8,128)S(1)} %copy-done.37, ...), custom_call_target="tpu_custom_call" | custom-call | tf_op jit(solution)/shard_map/scan_back/pallas_call | solution.py:502
  310.0 14.2 %scan_back.2 = (bf16[512,1152]{1,0:T(8,128)(2,1)S(1)}, bf16[8,1024]{1,0:T(8,128)(2,1)S(1)}, f32[8,1024]{1,0:T(8,128)S(1)}, f32[8,128]{1,0:T(8,128)S(1)}) custom-call(bf16[512,768]{1,0:T(8,128)(2,1)S(1)} %copy-done.11, bf16[512,256]{1,0:T(8,128)(2,1)S(1)} %copy-done.20, f32[512,128]{1,0:T(8,128)S(1)} %copy-done.22, f32[512,128]{1,0:T(8,128)S(1)} %copy-done.34, ...), custom_call_target="tpu_custom_call" | custom-call | tf_op jit(solution)/shard_map/scan_back/pallas_call | solution.py:502
  328.1 4.0 collective-permute-done.35
  335.4 4.7 fusion.37
  342.5 2.7 multiply_reduce_fusion
  345.2 2.7 multiply_reduce_fusion.1
  350.3 4.3 fusion
  354.6 3.0 collective-permute-start.40
  373.4 6.9 %collective-permute-start.14 = (bf16[128,1536]{1,0:T(8,128)(2,1)}, bf16[128,1536]{1,0:T(8,128)(2,1)}, u32[]{:S(2)}, u32[]{:S(2)}) collective-permute-start(bf16[128,1536]{1,0:T(8,128)(2,1)} %get-tuple-element.200), channel_id=1, source_target_pairs={{0,3},{1,2},{2,1},{3,0},{4,7},{5,6},{6,5},{7,4},{8,11},{9,10},{10,... | collective-permute-start | bytes 1179656 | tf_op jit(solution)/shard_map/ppermute | solution.py:31
  381.8 5.2 collective-permute-done.12
  388.7 21.5 %collective-permute-done.13 = bf16[128,1536]{1,0:T(8,128)(2,1)} collective-permute-done((bf16[128,1536]{1,0:T(8,128)(2,1)S(1)}, bf16[128,1536]{1,0:T(8,128)(2,1)}, u32[]{:S(2)}, u32[]{:S(2)}) %collective-permute-start.13) | collective-permute-done | bytes 393248 | tf_op jit(solution)/shard_map/ppermute | solution.py:31
  413.3 15.0 %collective-permute-start.37 = (bf16[128,1536]{1,0:T(8,128)(2,1)}, bf16[128,1536]{1,0:T(8,128)(2,1)S(1)}, u32[]{:S(2)}, u32[]{:S(2)}) collective-permute-start(bf16[128,1536]{1,0:T(8,128)(2,1)} %get-tuple-element.195), channel_id=1, source_target_pairs={{0,2},{1,3},{2,0},{3,1},{4,6},{5,7},{6,4},{7,5},{8,10},{9,11},{10,... | collective-permute-start | bytes 1179656 | tf_op jit(solution)/shard_map/ppermute | solution.py:31
  432.6 21.0 %collective-permute-start.32 = (bf16[128,1536]{1,0:T(8,128)(2,1)S(1)}, bf16[128,1536]{1,0:T(8,128)(2,1)S(1)}, u32[]{:S(2)}, u32[]{:S(2)}) collective-permute-start(bf16[128,1536]{1,0:T(8,128)(2,1)S(1)} %copy-done.91), channel_id=1, source_target_pairs={{0,2},{1,3},{2,0},{3,1},{4,6},{5,7},{6,4},{7,5},{8,10},{9,11},{10,... | collective-permute-start | bytes 1179656 | tf_op jit(solution)/shard_map/ppermute | solution.py:31
  455.3 13.8 %collective-permute-done.37 = bf16[128,1536]{1,0:T(8,128)(2,1)S(1)} collective-permute-done((bf16[128,1536]{1,0:T(8,128)(2,1)}, bf16[128,1536]{1,0:T(8,128)(2,1)S(1)}, u32[]{:S(2)}, u32[]{:S(2)}) %collective-permute-start.37) | collective-permute-done | bytes 393248 | tf_op jit(solution)/shard_map/ppermute | solution.py:31
  469.1 16.8 %collective-permute-done.32 = bf16[128,1536]{1,0:T(8,128)(2,1)S(1)} collective-permute-done((bf16[128,1536]{1,0:T(8,128)(2,1)S(1)}, bf16[128,1536]{1,0:T(8,128)(2,1)S(1)}, u32[]{:S(2)}, u32[]{:S(2)}) %collective-permute-start.32) | collective-permute-done | bytes 393248 | tf_op jit(solution)/shard_map/ppermute | solution.py:31
  486.0 3.6 fusion.11
  490.7 7.4 %all-to-all-start.2 = ((bf16[4,48,768]{2,1,0:T(8,128)(2,1)}), bf16[4,48,768]{2,1,0:T(8,128)(2,1)}, u32[]{:S(2)}, u32[]{:S(2)}) async-start(bf16[4,48,768]{2,1,0:T(8,128)(2,1)} %bitcast.149), calls=%async_computation.3 | async-start | bytes 589824 | tf_op jit(solution)/shard_map/all_to_all | solution.py:666
  498.1 3.5 fusion.15
  503.4 9.6 %all-to-all-done.2 = bf16[4,48,768]{2,1,0:T(8,128)(2,1)} async-done(((bf16[4,48,768]{2,1,0:T(8,128)(2,1)}), bf16[4,48,768]{2,1,0:T(8,128)(2,1)}, u32[]{:S(2)}, u32[]{:S(2)}) %all-to-all-start.2) | async-done | bytes 294944 | tf_op jit(solution)/shard_map/all_to_all | solution.py:666
  513.0 3.5 all-to-all-start.3
  522.5 9.5 %all-to-all-done.3 = bf16[4,48,1152]{2,1,0:T(8,128)(2,1)S(1)} async-done(((bf16[4,48,1152]{2,1,0:T(8,128)(2,1)}), bf16[4,48,1152]{2,1,0:T(8,128)(2,1)S(1)}, u32[]{:S(2)}, u32[]{:S(2)}) %all-to-all-start.3) | async-done | bytes 442400 | tf_op jit(solution)/shard_map/all_to_all | solution.py:666
  (418 shorter events, 120.6 us)
Async XLA Ops:
  7.2 180.7 %all-gather.8.cloned.1.call-start = ((), (), s32[]{:S(2)}) async-start(), calls=%async_computation.9 | async-start | bytes 2654208 | tf_op jit(solution)/shard_map/all_gather | solution.py:588
  9.6 185.7 %all-gather.4.cloned.1.call-start = ((), (), s32[]{:S(2)}) async-start(), calls=%async_computation.7 | async-start | bytes 3981312 | tf_op jit(solution)/shard_map/all_gather | solution.py:583
  45.0 13.5 %all-to-all-start.1 = ((bf16[4,48,768]{2,1,0:T(8,128)(2,1)}), bf16[4,48,768]{2,1,0:T(8,128)(2,1)S(1)}, u32[]{:S(2)}, u32[]{:S(2)}) async-start(bf16[4,48,768]{2,1,0:T(8,128)(2,1)} %copy.84), calls=%async_computation.1 | async-start | bytes 589824 | tf_op jit(solution)/shard_map/all_to_all | solution.py:584
  48.5 173.0 %all-gather.6.cloned.1.call-start = ((), (), s32[]{:S(2)}) async-start(), calls=%async_computation.8 | async-start | bytes 2654208 | tf_op jit(solution)/shard_map/all_gather | solution.py:585
  49.4 24.4 %collective-permute-start.15 = (bf16[128,1536]{1,0:T(8,128)(2,1)S(1)}, bf16[128,1536]{1,0:T(8,128)(2,1)S(1)}, u32[]{:S(2)}, u32[]{:S(2)}) collective-permute-start(bf16[128,1536]{1,0:T(8,128)(2,1)S(1)} %get-tuple-element.210.refs_1_), channel_id=1, source_target_pairs={{0,1},{1,0},{2,3},{3,2},{4,5},{5,4},{6,7},{7,6},{8,9},{9,8},{10,11... | collective-permute-start | bytes 1179656 | tf_op jit(solution)/shard_map/ppermute | solution.py:31
  51.4 32.4 %collective-permute-start.16 = (bf16[128,1536]{1,0:T(8,128)(2,1)S(1)}, bf16[128,1536]{1,0:T(8,128)(2,1)S(1)}, u32[]{:S(2)}, u32[]{:S(2)}) collective-permute-start(bf16[128,1536]{1,0:T(8,128)(2,1)S(1)} %get-tuple-element.210.refs_1_), channel_id=1, source_target_pairs={{0,2},{1,3},{2,0},{3,1},{4,6},{5,7},{6,4},{7,5},{8,10},{9,11},{10,... | collective-permute-start | bytes 1179656 | tf_op jit(solution)/shard_map/ppermute | solution.py:31
  53.7 31.3 %collective-permute-start.17 = (bf16[128,1536]{1,0:T(8,128)(2,1)S(1)}, bf16[128,1536]{1,0:T(8,128)(2,1)S(1)}, u32[]{:S(2)}, u32[]{:S(2)}) collective-permute-start(bf16[128,1536]{1,0:T(8,128)(2,1)S(1)} %get-tuple-element.210.refs_1_), channel_id=1, source_target_pairs={{0,3},{1,2},{2,1},{3,0},{4,7},{5,6},{6,5},{7,4},{8,11},{9,10},{10,... | collective-permute-start | bytes 1179656 | tf_op jit(solution)/shard_map/ppermute | solution.py:31
  59.3 431.4 %reduce-scatter.4.cloned.1.call-start = ((), (), s32[]{:S(2)}) async-start(), calls=%async_computation.10 | async-start | bytes 2654208 | tf_op jit(solution)/shard_map/reduce_scatter | solution.py:664
  60.1 50.2 %collective-permute-start.20 = (bf16[128,1536]{1,0:T(8,128)(2,1)S(1)}, bf16[128,1536]{1,0:T(8,128)(2,1)S(1)}, u32[]{:S(2)}, u32[]{:S(2)}) collective-permute-start(bf16[128,1536]{1,0:T(8,128)(2,1)S(1)} %get-tuple-element.208.refs_1_), channel_id=1, source_target_pairs={{0,1},{1,0},{2,3},{3,2},{4,5},{5,4},{6,7},{7,6},{8,9},{9,8},{10,11... | collective-permute-start | bytes 1179656 | tf_op jit(solution)/shard_map/ppermute | solution.py:31
  61.0 73.5 %collective-permute-start.21 = (bf16[128,1536]{1,0:T(8,128)(2,1)S(1)}, bf16[128,1536]{1,0:T(8,128)(2,1)S(1)}, u32[]{:S(2)}, u32[]{:S(2)}) collective-permute-start(bf16[128,1536]{1,0:T(8,128)(2,1)S(1)} %get-tuple-element.208.refs_1_), channel_id=1, source_target_pairs={{0,2},{1,3},{2,0},{3,1},{4,6},{5,7},{6,4},{7,5},{8,10},{9,11},{10,... | collective-permute-start | bytes 1179656 | tf_op jit(solution)/shard_map/ppermute | solution.py:31
  73.8 61.5 %collective-permute-start.22 = (bf16[128,1536]{1,0:T(8,128)(2,1)S(1)}, bf16[128,1536]{1,0:T(8,128)(2,1)S(1)}, u32[]{:S(2)}, u32[]{:S(2)}) collective-permute-start(bf16[128,1536]{1,0:T(8,128)(2,1)S(1)} %get-tuple-element.208.refs_1_), channel_id=1, source_target_pairs={{0,3},{1,2},{2,1},{3,0},{4,7},{5,6},{6,5},{7,4},{8,11},{9,10},{10,... | collective-permute-start | bytes 1179656 | tf_op jit(solution)/shard_map/ppermute | solution.py:31
  84.5 59.5 %collective-permute-start = (bf16[128,1536]{1,0:T(8,128)(2,1)}, bf16[128,1536]{1,0:T(8,128)(2,1)S(1)}, u32[]{:S(2)}, u32[]{:S(2)}) collective-permute-start(bf16[128,1536]{1,0:T(8,128)(2,1)} %get-tuple-element.209.refs_1_), channel_id=1, source_target_pairs={{0,1},{1,0},{2,3},{3,2},{4,5},{5,4},{6,7},{7,6},{8,9},{9,8},{10,11... | collective-permute-start | bytes 1179656 | tf_op jit(solution)/shard_map/ppermute | solution.py:31
  85.8 82.6 %collective-permute-start.1 = (bf16[128,1536]{1,0:T(8,128)(2,1)}, bf16[128,1536]{1,0:T(8,128)(2,1)}, u32[]{:S(2)}, u32[]{:S(2)}) collective-permute-start(bf16[128,1536]{1,0:T(8,128)(2,1)} %get-tuple-element.209.refs_1_), channel_id=1, source_target_pairs={{0,2},{1,3},{2,0},{3,1},{4,6},{5,7},{6,4},{7,5},{8,10},{9,11},{10,... | collective-permute-start | bytes 1179656 | tf_op jit(solution)/shard_map/ppermute | solution.py:31
  111.0 57.4 %collective-permute-start.2 = (bf16[128,1536]{1,0:T(8,128)(2,1)}, bf16[128,1536]{1,0:T(8,128)(2,1)}, u32[]{:S(2)}, u32[]{:S(2)}) collective-permute-start(bf16[128,1536]{1,0:T(8,128)(2,1)} %get-tuple-element.209.refs_1_), channel_id=1, source_target_pairs={{0,3},{1,2},{2,1},{3,0},{4,7},{5,6},{6,5},{7,4},{8,11},{9,10},{10,... | collective-permute-start | bytes 1179656 | tf_op jit(solution)/shard_map/ppermute | solution.py:31
  135.3 35.0 %collective-permute-start.5 = (bf16[128,1536]{1,0:T(8,128)(2,1)}, bf16[128,1536]{1,0:T(8,128)(2,1)}, u32[]{:S(2)}, u32[]{:S(2)}) collective-permute-start(bf16[128,1536]{1,0:T(8,128)(2,1)} %get-tuple-element.207.refs_1_), channel_id=1, source_target_pairs={{0,1},{1,0},{2,3},{3,2},{4,5},{5,4},{6,7},{7,6},{8,9},{9,8},{10,11... | collective-permute-start | bytes 1179656 | tf_op jit(solution)/shard_map/ppermute | solution.py:31
  136.0 49.2 %collective-permute-start.6 = (bf16[128,1536]{1,0:T(8,128)(2,1)}, bf16[128,1536]{1,0:T(8,128)(2,1)}, u32[]{:S(2)}, u32[]{:S(2)}) collective-permute-start(bf16[128,1536]{1,0:T(8,128)(2,1)} %get-tuple-element.207.refs_1_), channel_id=1, source_target_pairs={{0,2},{1,3},{2,0},{3,1},{4,6},{5,7},{6,4},{7,5},{8,10},{9,11},{10,... | collective-permute-start | bytes 1179656 | tf_op jit(solution)/shard_map/ppermute | solution.py:31
  144.7 40.5 %collective-permute-start.7 = (bf16[128,1536]{1,0:T(8,128)(2,1)}, bf16[128,1536]{1,0:T(8,128)(2,1)}, u32[]{:S(2)}, u32[]{:S(2)}) collective-permute-start(bf16[128,1536]{1,0:T(8,128)(2,1)} %get-tuple-element.207.refs_1_), channel_id=1, source_target_pairs={{0,3},{1,2},{2,1},{3,0},{4,7},{5,6},{6,5},{7,4},{8,11},{9,10},{10,... | collective-permute-start | bytes 1179656 | tf_op jit(solution)/shard_map/ppermute | solution.py:31
  199.6 10.7 %collective-permute-start.18 = (bf16[8,1024]{1,0:T(8,128)(2,1)S(1)}, bf16[8,1024]{1,0:T(8,128)(2,1)S(1)}, u32[]{:S(2)}, u32[]{:S(2)}) collective-permute-start(bf16[8,1024]{1,0:T(8,128)(2,1)S(1)} %slice.221), channel_id=1, source_target_pairs={{0,4},{4,8},{8,12},{1,5},{5,9},{9,13},{2,6},{6,10},{10,14},{3,7},{... | collective-permute-start | bytes 49160 | tf_op jit(solution)/shard_map/ppermute | solution.py:39
  205.4 19.3 %collective-permute-start.3 = (bf16[8,1024]{1,0:T(8,128)(2,1)S(1)}, bf16[8,1024]{1,0:T(8,128)(2,1)S(1)}, u32[]{:S(2)}, u32[]{:S(2)}) collective-permute-start(bf16[8,1024]{1,0:T(8,128)(2,1)S(1)} %slice.216), channel_id=1, source_target_pairs={{0,4},{4,8},{8,12},{1,5},{5,9},{9,13},{2,6},{6,10},{10,14},{3,7},{... | collective-permute-start | bytes 49160 | tf_op jit(solution)/shard_map/ppermute | solution.py:39
  218.6 12.4 %collective-permute-start.19 = (bf16[128,768]{1,0:T(8,128)(2,1)}, bf16[128,768]{1,0:T(8,128)(2,1)}, u32[]{:S(2)}, u32[]{:S(2)}) collective-permute-start(bf16[128,768]{1,0:T(8,128)(2,1)} %get-tuple-element.83), channel_id=1, source_target_pairs={{0,4},{4,8},{8,12},{1,5},{5,9},{9,13},{2,6},{6,10},{10,14},{3,7},{... | collective-permute-start | bytes 589832 | tf_op jit(solution)/shard_map/ppermute | solution.py:39
  229.7 18.4 %collective-permute-start.4 = (bf16[128,768]{1,0:T(8,128)(2,1)S(1)}, bf16[128,768]{1,0:T(8,128)(2,1)S(1)}, u32[]{:S(2)}, u32[]{:S(2)}) collective-permute-start(bf16[128,768]{1,0:T(8,128)(2,1)S(1)} %get-tuple-element.75), channel_id=1, source_target_pairs={{0,4},{4,8},{8,12},{1,5},{5,9},{9,13},{2,6},{6,10},{10,14},{3,7},{... | collective-permute-start | bytes 589832 | tf_op jit(solution)/shard_map/ppermute | solution.py:39
  236.4 21.2 %collective-permute-start.23 = (f32[4,8,128]{2,1,0:T(8,128)S(1)}, f32[4,8,128]{2,1,0:T(8,128)S(1)}, u32[]{:S(2)}, u32[]{:S(2)}) collective-permute-start(f32[4,8,128]{2,1,0:T(8,128)S(1)} %get-tuple-element.85), channel_id=1, source_target_pairs={{0,1},{1,0},{2,3},{3,2},{4,5},{5,4},{6,7},{7,6},{8,9},{9,8},{10,11... | collective-permute-start | bytes 49160 | tf_op jit(solution)/shard_map/ppermute | solution.py:31
  244.3 13.4 %collective-permute-start.24 = (f32[4,8,128]{2,1,0:T(8,128)S(1)}, f32[4,8,128]{2,1,0:T(8,128)S(1)}, u32[]{:S(2)}, u32[]{:S(2)}) collective-permute-start(f32[4,8,128]{2,1,0:T(8,128)S(1)} %get-tuple-element.85), channel_id=1, source_target_pairs={{0,2},{1,3},{2,0},{3,1},{4,6},{5,7},{6,4},{7,5},{8,10},{9,11},{10,... | collective-permute-start | bytes 49160 | tf_op jit(solution)/shard_map/ppermute | solution.py:31
  244.3 13.4 %collective-permute-start.25 = (f32[4,8,128]{2,1,0:T(8,128)S(1)}, f32[4,8,128]{2,1,0:T(8,128)S(1)}, u32[]{:S(2)}, u32[]{:S(2)}) collective-permute-start(f32[4,8,128]{2,1,0:T(8,128)S(1)} %get-tuple-element.85), channel_id=1, source_target_pairs={{0,3},{1,2},{2,1},{3,0},{4,7},{5,6},{6,5},{7,4},{8,11},{9,10},{10,... | collective-permute-start | bytes 49160 | tf_op jit(solution)/shard_map/ppermute | solution.py:31
  254.2 11.6 %collective-permute-start.10 = (f32[4,8,128]{2,1,0:T(8,128)S(1)}, f32[4,8,128]{2,1,0:T(8,128)S(1)}, u32[]{:S(2)}, u32[]{:S(2)}) collective-permute-start(f32[4,8,128]{2,1,0:T(8,128)S(1)} %get-tuple-element.77), channel_id=1, source_target_pairs={{0,2},{1,3},{2,0},{3,1},{4,6},{5,7},{6,4},{7,5},{8,10},{9,11},{10,... | collective-permute-start | bytes 49160 | tf_op jit(solution)/shard_map/ppermute | solution.py:31
  255.2 10.6 %collective-permute-start.11 = (f32[4,8,128]{2,1,0:T(8,128)S(1)}, f32[4,8,128]{2,1,0:T(8,128)S(1)}, u32[]{:S(2)}, u32[]{:S(2)}) collective-permute-start(f32[4,8,128]{2,1,0:T(8,128)S(1)} %get-tuple-element.77), channel_id=1, source_target_pairs={{0,3},{1,2},{2,1},{3,0},{4,7},{5,6},{6,5},{7,4},{8,11},{9,10},{10,... | collective-permute-start | bytes 49160 | tf_op jit(solution)/shard_map/ppermute | solution.py:31
  257.6 8.2 %collective-permute-start.9 = (f32[4,8,128]{2,1,0:T(8,128)S(1)}, f32[4,8,128]{2,1,0:T(8,128)S(1)}, u32[]{:S(2)}, u32[]{:S(2)}) collective-permute-start(f32[4,8,128]{2,1,0:T(8,128)S(1)} %get-tuple-element.77), channel_id=1, source_target_pairs={{0,1},{1,0},{2,3},{3,2},{4,5},{5,4},{6,7},{7,6},{8,9},{9,8},{10,11... | collective-permute-start | bytes 49160 | tf_op jit(solution)/shard_map/ppermute | solution.py:31
  276.7 224.9 %reduce-scatter.8.cloned.1.call-start = ((), (), s32[]{:S(2)}) async-start(), calls=%async_computation.12 | async-start | bytes 2654208 | tf_op jit(solution)/shard_map/reduce_scatter | solution.py:656
  276.8 18.8 %collective-permute-start.34 = (bf16[128,768]{1,0:T(8,128)(2,1)}, bf16[128,768]{1,0:T(8,128)(2,1)}, u32[]{:S(2)}, u32[]{:S(2)}) collective-permute-start(bf16[128,768]{1,0:T(8,128)(2,1)} %copy-done.68), channel_id=1, source_target_pairs={{4,0},{8,4},{12,8},{5,1},{9,5},{13,9},{6,2},{10,6},{14,10},{7,3},{... | collective-permute-start | bytes 589832 | tf_op jit(solution)/shard_map/ppermute | solution.py:39
  278.1 31.8 %collective-permute-start.29 = (bf16[128,768]{1,0:T(8,128)(2,1)}, bf16[128,768]{1,0:T(8,128)(2,1)}, u32[]{:S(2)}, u32[]{:S(2)}) collective-permute-start(bf16[128,768]{1,0:T(8,128)(2,1)} %copy-done.69), channel_id=1, source_target_pairs={{4,0},{8,4},{12,8},{5,1},{9,5},{13,9},{6,2},{10,6},{14,10},{7,3},{... | collective-permute-start | bytes 589832 | tf_op jit(solution)/shard_map/ppermute | solution.py:39
  284.2 146.6 %collective-permute-start.26 = (bf16[128,1536]{1,0:T(8,128)(2,1)}, bf16[128,1536]{1,0:T(8,128)(2,1)}, u32[]{:S(2)}, u32[]{:S(2)}) collective-permute-start(bf16[128,1536]{1,0:T(8,128)(2,1)} %get-tuple-element.202), channel_id=1, source_target_pairs={{0,1},{1,0},{2,3},{3,2},{4,5},{5,4},{6,7},{7,6},{8,9},{9,8},{10,11... | collective-permute-start | bytes 1179656 | tf_op jit(solution)/shard_map/ppermute | solution.py:31
  286.2 146.3 %collective-permute-start.27 = (bf16[128,1536]{1,0:T(8,128)(2,1)}, bf16[128,1536]{1,0:T(8,128)(2,1)}, u32[]{:S(2)}, u32[]{:S(2)}) collective-permute-start(bf16[128,1536]{1,0:T(8,128)(2,1)} %get-tuple-element.204), channel_id=1, source_target_pairs={{0,2},{1,3},{2,0},{3,1},{4,6},{5,7},{6,4},{7,5},{8,10},{9,11},{10,... | collective-permute-start | bytes 1179656 | tf_op jit(solution)/shard_map/ppermute | solution.py:31
  290.9 222.1 %reduce-scatter.6.cloned.1.call-start = ((), (), s32[]{:S(2)}) async-start(), calls=%async_computation.11 | async-start | bytes 3981312 | tf_op jit(solution)/shard_map/reduce_scatter | solution.py:664
  325.3 6.9 %collective-permute-start.35 = (bf16[8,1024]{1,0:T(8,128)(2,1)S(1)}, bf16[8,1024]{1,0:T(8,128)(2,1)S(1)}, u32[]{:S(2)}, u32[]{:S(2)}) collective-permute-start(bf16[8,1024]{1,0:T(8,128)(2,1)S(1)} %get-tuple-element.98), channel_id=1, source_target_pairs={{4,0},{8,4},{12,8},{5,1},{9,5},{13,9},{6,2},{10,6},{14,10},{7,3},{... | collective-permute-start | bytes 49160 | tf_op jit(solution)/shard_map/ppermute | solution.py:39
  326.6 7.5 %collective-permute-start.30 = (bf16[8,1024]{1,0:T(8,128)(2,1)S(1)}, bf16[8,1024]{1,0:T(8,128)(2,1)S(1)}, u32[]{:S(2)}, u32[]{:S(2)}) collective-permute-start(bf16[8,1024]{1,0:T(8,128)(2,1)S(1)} %get-tuple-element.92), channel_id=1, source_target_pairs={{4,0},{8,4},{12,8},{5,1},{9,5},{13,9},{6,2},{10,6},{14,10},{7,3},{... | collective-permute-start | bytes 49160 | tf_op jit(solution)/shard_map/ppermute | solution.py:39
  370.7 16.3 %collective-permute-start.12 = (bf16[128,1536]{1,0:T(8,128)(2,1)}, bf16[128,1536]{1,0:T(8,128)(2,1)}, u32[]{:S(2)}, u32[]{:S(2)}) collective-permute-start(bf16[128,1536]{1,0:T(8,128)(2,1)} %get-tuple-element.199), channel_id=1, source_target_pairs={{0,1},{1,0},{2,3},{3,2},{4,5},{5,4},{6,7},{7,6},{8,9},{9,8},{10,11... | collective-permute-start | bytes 1179656 | tf_op jit(solution)/shard_map/ppermute | solution.py:31
  371.9 38.4 %collective-permute-start.13 = (bf16[128,1536]{1,0:T(8,128)(2,1)S(1)}, bf16[128,1536]{1,0:T(8,128)(2,1)}, u32[]{:S(2)}, u32[]{:S(2)}) collective-permute-start(bf16[128,1536]{1,0:T(8,128)(2,1)S(1)} %get-tuple-element.201), channel_id=1, source_target_pairs={{0,2},{1,3},{2,0},{3,1},{4,6},{5,7},{6,4},{7,5},{8,10},{9,11},{10,... | collective-permute-start | bytes 1179656 | tf_op jit(solution)/shard_map/ppermute | solution.py:31
  373.4 39.9 %collective-permute-start.14 = (bf16[128,1536]{1,0:T(8,128)(2,1)}, bf16[128,1536]{1,0:T(8,128)(2,1)}, u32[]{:S(2)}, u32[]{:S(2)}) collective-permute-start(bf16[128,1536]{1,0:T(8,128)(2,1)} %get-tuple-element.200), channel_id=1, source_target_pairs={{0,3},{1,2},{2,1},{3,0},{4,7},{5,6},{6,5},{7,4},{8,11},{9,10},{10,... | collective-permute-start | bytes 1179656 | tf_op jit(solution)/shard_map/ppermute | solution.py:31
  387.0 45.6 %collective-permute-start.28 = (bf16[128,1536]{1,0:T(8,128)(2,1)S(1)}, bf16[128,1536]{1,0:T(8,128)(2,1)}, u32[]{:S(2)}, u32[]{:S(2)}) collective-permute-start(bf16[128,1536]{1,0:T(8,128)(2,1)S(1)} %copy-done.88), channel_id=1, source_target_pairs={{0,3},{1,2},{2,1},{3,0},{4,7},{5,6},{6,5},{7,4},{8,11},{9,10},{10,... | collective-permute-start | bytes 1179656 | tf_op jit(solution)/shard_map/ppermute | solution.py:31
  410.2 43.4 %collective-permute-start.36 = (bf16[128,1536]{1,0:T(8,128)(2,1)}, bf16[128,1536]{1,0:T(8,128)(2,1)S(1)}, u32[]{:S(2)}, u32[]{:S(2)}) collective-permute-start(bf16[128,1536]{1,0:T(8,128)(2,1)} %get-tuple-element.193), channel_id=1, source_target_pairs={{0,1},{1,0},{2,3},{3,2},{4,5},{5,4},{6,7},{7,6},{8,9},{9,8},{10,11... | collective-permute-start | bytes 1179656 | tf_op jit(solution)/shard_map/ppermute | solution.py:31
  413.3 55.8 %collective-permute-start.37 = (bf16[128,1536]{1,0:T(8,128)(2,1)}, bf16[128,1536]{1,0:T(8,128)(2,1)S(1)}, u32[]{:S(2)}, u32[]{:S(2)}) collective-permute-start(bf16[128,1536]{1,0:T(8,128)(2,1)} %get-tuple-element.195), channel_id=1, source_target_pairs={{0,2},{1,3},{2,0},{3,1},{4,6},{5,7},{6,4},{7,5},{8,10},{9,11},{10,... | collective-permute-start | bytes 1179656 | tf_op jit(solution)/shard_map/ppermute | solution.py:31
  430.8 38.3 %collective-permute-start.38 = (bf16[128,1536]{1,0:T(8,128)(2,1)S(1)}, bf16[128,1536]{1,0:T(8,128)(2,1)S(1)}, u32[]{:S(2)}, u32[]{:S(2)}) collective-permute-start(bf16[128,1536]{1,0:T(8,128)(2,1)S(1)} %copy-done.89), channel_id=1, source_target_pairs={{0,3},{1,2},{2,1},{3,0},{4,7},{5,6},{6,5},{7,4},{8,11},{9,10},{10,... | collective-permute-start | bytes 1179656 | tf_op jit(solution)/shard_map/ppermute | solution.py:31
  432.6 36.6 %collective-permute-start.31 = (bf16[128,1536]{1,0:T(8,128)(2,1)S(1)}, bf16[128,1536]{1,0:T(8,128)(2,1)S(1)}, u32[]{:S(2)}, u32[]{:S(2)}) collective-permute-start(bf16[128,1536]{1,0:T(8,128)(2,1)S(1)} %copy-done.92), channel_id=1, source_target_pairs={{0,1},{1,0},{2,3},{3,2},{4,5},{5,4},{6,7},{7,6},{8,9},{9,8},{10,11... | collective-permute-start | bytes 1179656 | tf_op jit(solution)/shard_map/ppermute | solution.py:31
  432.6 53.4 %collective-permute-start.32 = (bf16[128,1536]{1,0:T(8,128)(2,1)S(1)}, bf16[128,1536]{1,0:T(8,128)(2,1)S(1)}, u32[]{:S(2)}, u32[]{:S(2)}) collective-permute-start(bf16[128,1536]{1,0:T(8,128)(2,1)S(1)} %copy-done.91), channel_id=1, source_target_pairs={{0,2},{1,3},{2,0},{3,1},{4,6},{5,7},{6,4},{7,5},{8,10},{9,11},{10,... | collective-permute-start | bytes 1179656 | tf_op jit(solution)/shard_map/ppermute | solution.py:31
  453.6 32.4 %collective-permute-start.33 = (bf16[128,1536]{1,0:T(8,128)(2,1)S(1)}, bf16[128,1536]{1,0:T(8,128)(2,1)S(1)}, u32[]{:S(2)}, u32[]{:S(2)}) collective-permute-start(bf16[128,1536]{1,0:T(8,128)(2,1)S(1)} %copy-done.90), channel_id=1, source_target_pairs={{0,3},{1,2},{2,1},{3,0},{4,7},{5,6},{6,5},{7,4},{8,11},{9,10},{10,... | collective-permute-start | bytes 1179656 | tf_op jit(solution)/shard_map/ppermute | solution.py:31
  490.7 22.3 %all-to-all-start.2 = ((bf16[4,48,768]{2,1,0:T(8,128)(2,1)}), bf16[4,48,768]{2,1,0:T(8,128)(2,1)}, u32[]{:S(2)}, u32[]{:S(2)}) async-start(bf16[4,48,768]{2,1,0:T(8,128)(2,1)} %bitcast.149), calls=%async_computation.3 | async-start | bytes 589824 | tf_op jit(solution)/shard_map/all_to_all | solution.py:666
  501.6 18.1 %collective-permute-start.45 = (bf16[96,1536]{1,0:T(8,128)(2,1)}, bf16[96,1536]{1,0:T(8,128)(2,1)S(1)}, u32[]{:S(2)}, u32[]{:S(2)}) collective-permute-start(bf16[96,1536]{1,0:T(8,128)(2,1)} %reduce-scatter.8.cloned.1.call-done), channel_id=1, source_target_pairs={{0,0},{4,1},{8,2},{12,3},{16,4},{20,5},{24,6},{28,7},{1,8},{5,9},{... | collective-permute-start | bytes 884744 | tf_op jit(solution)/shard_map/ppermute | solution.py:658
  513.0 19.0 %all-to-all-start.3 = ((bf16[4,48,1152]{2,1,0:T(8,128)(2,1)}), bf16[4,48,1152]{2,1,0:T(8,128)(2,1)S(1)}, u32[]{:S(2)}, u32[]{:S(2)}) async-start(bf16[4,48,1152]{2,1,0:T(8,128)(2,1)} %bitcast.148), calls=%async_computation.5 | async-start | bytes 884736 | tf_op jit(solution)/shard_map/all_to_all | solution.py:666
  (113 other events, 1599.5 us)
Sparse Core Ops, SparseCore 0:
  9.9 43.5 all-gather.7
  55.4 33.9 all-gather.3
  91.3 28.9 all-gather.5
  276.9 40.2 reduce-scatter.3
  320.7 43.1 reduce-scatter.7
  367.2 47.9 reduce-scatter.5

commit v2 on v1

v2 whole, which is shorter than its diff:
```python
import jax
import jax.numpy as jnp
from jax import lax
from jax.experimental import pallas as pl
from jax.experimental.pallas import tpu as pltpu
from jax.sharding import Mesh, PartitionSpec as P

H = 48
PS = 64
N = 128
KW = 4
DI = 3072
GROUP = 4
HG = H // GROUP
HP = 16
XW = HG * PS
CW = XW + 2 * N
AW = CW + 128
QC = 128
EPS = 1e-05
NEG = -1e30
BF = jnp.bfloat16
F4 = jnp.float32
LIMIT = 48 * 1024 * 1024
SUMS = ("dp", "ctx", "hh")
CHAIN = ("ctx", "hh")
EVERY = ("dp", "ctx", "hh", "hl")


def swap(part, axis, k):
    count = lax.axis_size(axis)
    return lax.ppermute(part, axis, [(i, i ^ k) for i in range(count)])


def shift(part, axes, by):
    count = 1
    for axis in axes:
        count = count * lax.axis_size(axis)
    pairs = [(i, i + by) for i in range(count) if 0 <= i + by < count]
    return lax.ppermute(part, axes, pairs)


def mm(a, b):
    return jnp.dot(a, b, preferred_element_type=F4)


def mm_nt(a, b):
    return lax.dot_general(a, b, (((1,), (1,)), ((), ())), preferred_element_type=F4)


def mm_tn(a, b):
    return lax.dot_general(a, b, (((0,), (0,)), ((), ())), preferred_element_type=F4)


def spread(v, e):
    return mm_tn(v.astype(BF), e)


def spread_fine(v, e):
    hi = v.astype(BF)
    lo = (v - hi.astype(F4)).astype(BF)
    return mm_tn(hi, e) + mm_tn(lo, e)


def gather_heads(w, e):
    return mm_nt(e, w.astype(BF))


def gather_fine(w, e):
    hi = w.astype(BF)
    lo = (w - hi.astype(F4)).astype(BF)
    return mm_nt(e, hi) + mm_nt(e, lo)


def sigmoid(v):
    return 0.5 * jnp.tanh(0.5 * v) + 0.5


def norm_rows(values, gain):
    return values * lax.rsqrt(jnp.mean(values * values, axis=-1, keepdims=True) + EPS) * gain


def running(v, back):
    r = lax.broadcasted_iota(jnp.int32, (QC, QC), 0)
    q = lax.broadcasted_iota(jnp.int32, (QC, QC), 1)
    ones = ((r >= q) if back else (r <= q)).astype(BF)
    hi = v.astype(BF)
    rest = v - hi.astype(F4)
    mid = rest.astype(BF)
    lo = (rest - mid.astype(F4)).astype(BF)
    got = mm(jnp.concatenate([hi, mid, lo], axis=0), ones)
    n = v.shape[0]
    return got[:n] + got[n : 2 * n] + got[2 * n :]


def lines_of(mt):
    return jnp.transpose(jnp.concatenate([mt, jnp.zeros((QC - 8, QC), F4)], axis=0))


def tiles(count):
    return [slice(j * 128, j * 128 + 128) for j in range(count)]


def col_of(row):
    return jnp.transpose(jnp.broadcast_to(row, (QC, QC)))


def cols_of(v):
    return jnp.transpose(jnp.concatenate([v, jnp.zeros((QC - HP, QC), F4)], axis=0))


def place_kernel(place, *refs):
    out = refs[-1]
    rows = refs[0].shape[0]
    for k, ref in enumerate(refs[:-1]):
        slot = jnp.bitwise_xor(place[0], k)
        out[pl.ds(pl.multiple_of(slot * rows, rows), rows), :] = ref[...]


def placed(place, pieces):
    rows, width = pieces[0].shape
    vm = pl.BlockSpec(memory_space=pltpu.VMEM)
    return pl.pallas_call(
        place_kernel,
        out_shape=jax.ShapeDtypeStruct((len(pieces) * rows, width), BF),
        in_specs=[pl.BlockSpec(memory_space=pltpu.SMEM)] + [vm] * len(pieces),
        out_specs=vm,
        compiler_params=pltpu.CompilerParams(vmem_limit_bytes=LIMIT),
        name="place_rows",
    )(place, *pieces)


def joined(cur, got, side):
    low = jnp.where(side == 0, cur, got)
    high = jnp.where(side == 0, got, cur)
    return jnp.concatenate([low, high], axis=0)


def sums_gather(mine, cuts):
    rows = mine.shape[0]
    if lax.axis_size("hh") > 1 or rows % 16:
        whole = lax.all_gather(mine, SUMS, axis=0, tiled=True)
        return [whole[:, a:b] for a, b in cuts]
    place = lax.axis_index("ctx").astype(jnp.int32).reshape(1)
    others = [swap(mine, "ctx", k) for k in range(1, lax.axis_size("ctx"))]
    stack = placed(place, [mine, *others])
    got = swap(stack, "dp", 1)
    side = lax.axis_index("dp")
    return [joined(stack[:, a:b], got[:, a:b], side) for a, b in cuts]


def team_halves(total):
    if lax.axis_size("hh") > 1:
        return total
    parts = total.reshape(2, -1, total.shape[1])
    dp = lax.axis_index("dp")
    give = lax.dynamic_index_in_dim(parts, 1 - dp, 0, keepdims=False)
    keep = lax.dynamic_index_in_dim(parts, dp, 0, keepdims=False)
    return (keep.astype(F4) + swap(give, "dp", 1).astype(F4)).astype(BF)


def chain_sum(cur):
    if lax.axis_size("hh") > 1:
        return lax.psum_scatter(cur, SUMS, scatter_dimension=0, tiled=True).astype(BF)
    count = lax.axis_size("ctx")
    parts = cur.reshape(count, -1, cur.shape[1])
    ctx = lax.axis_index("ctx")

    def piece(k):
        return lax.dynamic_index_in_dim(parts, jnp.bitwise_xor(ctx, k), 0, keepdims=False)

    out = piece(0).astype(F4)
    for k in range(1, count):
        out = out + swap(piece(k), "ctx", k).astype(F4)
    return out.astype(BF)


def work(length, us):
    flops = int(us * 1e9) * length // 1024
    return pl.CostEstimate(flops=flops, transcendentals=0, bytes_accessed=length * 8192)


def fixed(*shape):
    return pl.BlockSpec(shape, lambda i: (0,) * len(shape))


def ahead(rows, width, at=0):
    return pl.BlockSpec((rows, width), lambda i: (i, at))


def ahead3(seqs, *shape):
    return pl.BlockSpec((seqs, *shape), lambda i: (i, 0, 0))


def behind(n, rows, width, at=0):
    return pl.BlockSpec((rows, width), lambda i: (n - 1 - i, at))


def behind3(n, seqs, *shape):
    return pl.BlockSpec((seqs, *shape), lambda i: (n - 1 - i, 0, 0))


def decays(cum, mt):
    last = cum[:, QC - 1 : QC]
    same_last = (mt[0:1, :] == mt[2:3, :]).astype(F4)
    follows = (mt[1:2, :] == mt[2:3, :]).astype(F4)
    tail0 = jnp.exp(last - cum) * same_last
    lead_last = jnp.exp(last) * follows
    return tail0, lead_last


def front_kernel(
    xr, br, rr, halo, meta, taps, hp, e, x_o, bc_o, sl_o, sc_o, st_o, dec_o, buf, st, dec
):
    i = pl.program_id(0)
    seqs = halo.shape[0]

    @pl.when(i == 0)
    def _():
        buf[:, 0:8, :] = halo[...].astype(F4)
        st[...] = jnp.zeros_like(st)
        dec[...] = jnp.ones_like(dec)

    @pl.when(i > 0)
    def _():
        buf[:, 0:8, :] = buf[:, QC : QC + 8, :]

    every = range(seqs)
    rows = [slice(s * QC, s * QC + QC) for s in every]
    tails, lasts = [], []
    for s in every:
        v = jnp.transpose(rr[rows[s], :].astype(F4))[:HP] + hp[0]
        dt = jnp.maximum(v, 0.0) + jnp.log1p(jnp.exp(-jnp.abs(v)))
        cum = running(dt * hp[1], False)
        sc_o[s, 0:HP, :] = cum
        sc_o[s, HP:, :] = dt
        tail0, lead_last = decays(cum, meta[s])
        dec[s] = dec[s] * lead_last
        tails.append((tail0 * dt).astype(BF))
        lasts.append(lead_last[:, :8])
    order = tiles(CW // 128)
    n_x = XW // 128
    for s in every:
        turned = lines_of(meta[s])
        for j in [*range(n_x, len(order)), *range(n_x)]:
            c = order[j]
            if j < n_x:
                own = xr[rows[s], c].astype(F4)
            else:
                own = br[rows[s], j * 128 - XW : j * 128 - XW + 128].astype(F4)
            buf[s, 8 : QC + 8, c] = own
            mixed = taps[4:5, c] + taps[3:4, c] * own
            for k in range(3):
                mixed = mixed + taps[k : k + 1, c] * (
                    buf[s, 5 + k : 5 + k + QC, c] * turned[:, 3 + k : 4 + k]
                )
            sig = sigmoid(mixed)
            act = (mixed * sig).astype(BF)
            sl_o[rows[s], c] = (sig + mixed * sig * (1.0 - sig)).astype(BF)
            if j < n_x:
                x_o[rows[s], c] = act
                xw = (act.astype(F4) * spread(tails[s], e[:, c])).astype(BF)
                grow = spread_fine(lasts[s], e[:, c])[0:1, :]
                st[s, :, c] = st[s, :, c] * grow + mm_tn(bc_o[rows[s], :N], xw)
            else:
                bc_o[rows[s], j * 128 - XW : j * 128 - XW + 128] = act
    st_o[...] = st[...].astype(BF)
    dec_o[...] = dec[...]


def front(seqs, raw, halo, meta, taps, hp, e):
    length = raw.shape[0]
    span = seqs * QC
    sd = jax.ShapeDtypeStruct
    return pl.pallas_call(
        front_kernel,
        grid=(length // span,),
        in_specs=[
            ahead(span, XW),
            ahead(span, 2 * N, XW // (2 * N)),
            ahead(span, 128, CW // 128),
            fixed(seqs, 8, CW),
            ahead3(seqs, 8, 128),
            fixed(8, CW),
            fixed(2, HP, 128),
            fixed(HP, XW),
        ],
        out_specs=[
            ahead(span, XW),
            ahead(span, 2 * N),
            ahead(span, CW),
            ahead3(seqs, 2 * HP, 128),
            fixed(seqs, N, XW),
            fixed(seqs, HP, 128),
        ],
        out_shape=[
            sd((length, XW), BF),
            sd((length, 2 * N), BF),
            sd((length, CW), BF),
            sd((length // QC, 2 * HP, 128), F4),
            sd((seqs, N, XW), BF),
            sd((seqs, HP, 128), F4),
        ],
        scratch_shapes=[
            pltpu.VMEM((seqs, QC + 8, CW), F4),
            pltpu.VMEM((seqs, N, XW), F4),
            pltpu.VMEM((seqs, HP, 128), F4),
        ],
        compiler_params=pltpu.CompilerParams(vmem_limit_bytes=LIMIT),
        cost_estimate=work(length, 1),
        name="conv_state",
    )(raw, raw, raw, halo, meta, taps, hp, e)


def lane_halves():
    lane = lax.broadcasted_iota(jnp.int32, (1, 128), 1)
    return [(lane < PS).astype(BF), (lane >= PS).astype(BF)]


def inside_of(mt):
    r = lax.broadcasted_iota(jnp.int32, (QC, QC), 0)
    q = lax.broadcasted_iota(jnp.int32, (QC, QC), 1)
    return (col_of(mt[0:1, :]) == mt[0:1, :]) & (r >= q)


def scan_kernel(x_r, bc, sc, meta, s_in, z_r, skip, e, y_o, ent_o, sum_o, st):
    i = pl.program_id(0)
    seqs = s_in.shape[0]
    every = range(seqs)
    rows = [slice(s * QC, s * QC + QC) for s in every]

    @pl.when(i == 0)
    def _():
        st[...] = s_in[...].astype(F4)

    halves = lane_halves()
    for s in every:
        mt = meta[s]
        cum, dt = sc[s, 0:HP, :], sc[s, HP:, :]
        b, c = bc[rows[s], :N], bc[rows[s], N:]
        lead = (jnp.exp(cum) * (mt[0:1, :] == mt[1:2, :]).astype(F4)).astype(BF)
        tail0, lead_last = decays(cum, mt)
        tail = (tail0 * dt).astype(BF)
        scores = mm_nt(c, b)
        inside = inside_of(mt)
        cum_cols = cols_of(cum)
        squares = jnp.zeros((QC, 128), F4)
        for j, at in enumerate(tiles(XW // 128)):
            ej = e[:, at]
            xp = x_r[rows[s], at]
            xf = xp.astype(F4)
            now = st[s, :, at]
            before = now.astype(BF)
            ent_o[s, :, at] = before
            y = spread(lead, ej) * mm(c, before) + skip[:, at] * xf
            xw = (xf * spread(tail, ej)).astype(BF)
            st[s, :, at] = now * spread_fine(lead_last[:, :8], ej)[0:1, :] + mm_tn(b, xw)
            for half in range(2):
                h = 2 * j + half
                gap = jnp.where(inside, cum_cols[:, h : h + 1] - sc[s, h : h + 1, :], NEG)
                w = (scores * jnp.exp(gap) * sc[s, HP + h : HP + h + 1, :]).astype(BF)
                y = y + mm(w, xp * halves[half])
            low = y.astype(BF)
            y_o[rows[s], at] = low
            z = z_r[rows[s], at]
            v = low.astype(F4) * z * sigmoid(z)
            squares = squares + v * v
        sum_o[s] = jnp.sum(jnp.transpose(squares), axis=0, keepdims=True)


def scan(seqs, x, bc, sc, meta, s_in, z, skip, e):
    length = x.shape[0]
    span = seqs * QC
    chunks = length // QC
    sd = jax.ShapeDtypeStruct
    return pl.pallas_call(
        scan_kernel,
        grid=(length // span,),
        in_specs=[
            ahead(span, XW),
            ahead(span, 2 * N),
            ahead3(seqs, 2 * HP, 128),
            ahead3(seqs, 8, 128),
            fixed(seqs, N, XW),
            ahead(span, XW),
            fixed(1, XW),
            fixed(HP, XW),
        ],
        out_specs=[ahead(span, XW), ahead3(seqs, N, XW), ahead3(seqs, 1, QC)],
        out_shape=[sd((length, XW), BF), sd((chunks, N, XW), BF), sd((chunks, 1, QC), F4)],
        scratch_shapes=[pltpu.VMEM((seqs, N, XW), F4)],
        compiler_params=pltpu.CompilerParams(vmem_limit_bytes=LIMIT),
        cost_estimate=work(length, 1),
        name="scan_gate",
    )(x, bc, sc, meta, s_in, z, skip, e)


def gate_kernel(y_r, z_r, dg_r, sq, al, bc, sc, meta, gain, e, dy_o, dz_o, gg_o, ds_o, ds, gg):
    i = pl.program_id(0)
    seqs = ds.shape[0]
    every = range(seqs)
    rows = [slice(s * QC, s * QC + QC) for s in every]

    @pl.when(i == 0)
    def _():
        gg[...] = jnp.zeros_like(gg)
        ds[...] = jnp.zeros_like(ds)

    for s in every:
        mt = meta[s]
        cum = sc[s, 0:HP, :]
        c = bc[rows[s], N:]
        scale = lax.rsqrt(sq[s] * (1.0 / DI) + EPS)
        rstd = col_of(scale)
        pull = col_of(al[s] * (scale * scale * scale) * (1.0 / DI))
        lead = (jnp.exp(cum) * (mt[0:1, :] == mt[1:2, :]).astype(F4)).astype(BF)
        _, lead_last = decays(cum, mt)
        for at in tiles(XW // 128):
            ej = e[:, at]
            y = y_r[rows[s], at].astype(F4)
            z = z_r[rows[s], at]
            sig = sigmoid(z)
            act = z * sig
            v = y * act
            dg = dg_r[rows[s], at] * rstd
            gg[0:1, at] = gg[0:1, at] + jnp.sum(dg * v, axis=0, keepdims=True)
            d_v = dg * gain[:, at] - v * pull
            dy = (d_v * act).astype(BF)
            dy_o[rows[s], at] = dy
            dz_o[rows[s], at] = (d_v * y * (sig + act * (1.0 - sig))).astype(BF)
            led = (dy.astype(F4) * spread(lead, ej)).astype(BF)
            grow = spread_fine(lead_last[:, :8], ej)[0:1, :]
            ds[s, :, at] = ds[s, :, at] * grow + mm_tn(c, led)
    ds_o[...] = ds[...].astype(BF)
    gg_o[...] = gg[...]


def gate(seqs, y, z, dg, sq, al, bc, sc, meta, gain, e):
    length = y.shape[0]
    span = seqs * QC
    n = length // span
    sd = jax.ShapeDtypeStruct
    wide = behind(n, span, XW)
    line = behind3(n, seqs, 1, QC)
    return pl.pallas_call(
        gate_kernel,
        grid=(n,),
        in_specs=[
            wide,
            wide,
            wide,
            line,
            line,
            behind(n, span, 2 * N),
            behind3(n, seqs, 2 * HP, 128),
            behind3(n, seqs, 8, 128),
            fixed(1, XW),
            fixed(HP, XW),
        ],
        out_specs=[wide, wide, fixed(8, XW), fixed(seqs, N, XW)],
        out_shape=[
            sd((length, XW), BF),
            sd((length, XW), BF),
            sd((8, XW), F4),
            sd((seqs, N, XW), BF),
        ],
        scratch_shapes=[pltpu.VMEM((seqs, N, XW), F4), pltpu.VMEM((8, XW), F4)],
        compiler_params=pltpu.CompilerParams(vmem_limit_bytes=LIMIT),
        cost_estimate=work(length, 1),
        name="gate_back",
    )(y, z, dg, sq, al, bc, sc, meta, gain, e)


def back_kernel(
    x_r, bc, sl, sc, meta, ent, dy_r, d_end, xr, br, rr, halo, taps, hp, skip, e,
    draw_o, rim_o, cg_o, hg_o,
    ds, carry, colbuf, rowbuf, cg, hg,
):
    i = pl.program_id(0)
    seqs = ds.shape[0]
    every = range(seqs)
    rows = [slice(s * QC, s * QC + QC) for s in every]
    first = (i == pl.num_programs(0) - 1).astype(F4)

    @pl.when(i == 0)
    def _():
        ds[...] = d_end[...].astype(F4)
        carry[...] = jnp.zeros_like(carry)
        cg[...] = jnp.zeros_like(cg)
        hg[...] = jnp.zeros_like(hg)
        colbuf[...] = jnp.zeros_like(colbuf)
        rowbuf[...] = jnp.zeros_like(rowbuf)

    halves = lane_halves()
    lane = lax.broadcasted_iota(jnp.int32, (1, 128), 1)
    token = lax.broadcasted_iota(jnp.int32, (QC, 128), 0)
    edge = lax.broadcasted_iota(jnp.int32, (8, 128), 0)
    place = lax.broadcasted_iota(jnp.int32, (HP, QC), 1)

    def conv_back(s, c, own, d_act, turned):
        dm = d_act * sl[rows[s], c].astype(F4)
        near = turned[:, 5:6]
        shifted = [dm]
        for k in range(3):
            ready = shifted[-1] * near
            moved = pltpu.roll(ready, QC - 1, 0)
            shifted.append(jnp.where(token == QC - 1, carry[s, k : k + 1, c], moved))
            carry[s, k : k + 1, c] = ready[0:1, :]
        d_raw = taps[3:4, c] * shifted[0]
        for k in range(3):
            d_raw = d_raw + taps[2 - k : 3 - k, c] * shifted[k + 1]
        draw_o[rows[s], c] = d_raw.astype(BF)
        parts = [jnp.sum(own * v, axis=0, keepdims=True) for v in shifted[::-1]]
        parts.append(jnp.sum(dm, axis=0, keepdims=True))
        head = dm[0:8, :]
        outside = halo[s, :, c].astype(F4) * first
        rim = jnp.zeros((8, 128), F4)
        for k in range(3):
            held = jnp.where(edge < 3 - k, head * turned[0:8, 3 + k : 4 + k], 0.0)
            held = pltpu.roll(held, 5 + k, 0)
            rim = rim + taps[k : k + 1, c] * held
            parts[k] = parts[k] + jnp.sum(outside * held, axis=0, keepdims=True)
        rim_o[s, :, c] = rim.astype(BF)
        cg[0:5, c] = cg[0:5, c] + jnp.concatenate(parts, axis=0)

    for s in every:
        mt = meta[s]
        turned = lines_of(mt)
        cum, dt = sc[s, 0:HP, :], sc[s, HP:, :]
        b, c = bc[rows[s], :N], bc[rows[s], N:]
        lead = (jnp.exp(cum) * (mt[0:1, :] == mt[1:2, :]).astype(F4)).astype(BF)
        tail0, lead_last = decays(cum, mt)
        tail = (tail0 * dt).astype(BF)
        scores = mm_nt(c, b)
        inside = inside_of(mt)
        cum_cols = cols_of(cum)
        d_sc = jnp.zeros((QC, QC), F4)
        sums = jnp.zeros((QC, 128), F4)
        tq = jnp.zeros((HP, QC), F4)
        lv = jnp.zeros((HP, QC), F4)
        d_b = jnp.zeros((QC, N), F4)
        d_c = jnp.zeros((QC, N), F4)
        for j, at in enumerate(tiles(XW // 128)):
            ej = e[:, at]
            xp = x_r[rows[s], at]
            dyp = dy_r[rows[s], at]
            xf = xp.astype(F4)
            dyf = dyp.astype(F4)
            before = ent[s, :, at]
            now = ds[s, :, at]
            after = now.astype(BF)
            tailj = spread(tail, ej)
            u = tailj * mm(b, after)
            led = dyf * spread(lead, ej)
            tq = tq + gather_heads(xf * u, ej)
            lv = lv + gather_heads(led * mm(c, before), ej)
            ledb = led.astype(BF)
            d_b = d_b + mm_nt((xf * tailj).astype(BF), after)
            d_c = d_c + mm_nt(ledb, before)
            colbuf[s, 0:1, at] = jnp.sum(now * before.astype(F4), axis=0, keepdims=True)
            colbuf[s, 1:2, at] = jnp.sum(dyf * xf, axis=0, keepdims=True)
            ds[s, :, at] = now * spread_fine(lead_last[:, :8], ej)[0:1, :] + mm_tn(c, ledb)
            dx = u + skip[:, at] * dyf
            for half in range(2):
                h = 2 * j + half
                gap = jnp.where(inside, cum_cols[:, h : h + 1] - sc[s, h : h + 1, :], NEG)
                dec = jnp.exp(gap)
                dtr = sc[s, HP + h : HP + h + 1, :]
                sl_h = scores * dec
                d_m = mm_nt(dyp, xp * halves[half])
                g = d_m * sl_h
                rowbuf[s, h : h + 1, :] = jnp.sum(g, axis=0, keepdims=True)
                sums = jnp.where(lane == h, jnp.sum(g * dtr, axis=1, keepdims=True), sums)
                d_sc = d_sc + d_m * (dec * dtr)
                dx = dx + mm_tn((sl_h * dtr).astype(BF), dyp * halves[half])
            conv_back(s, at, xr[rows[s], at].astype(F4), dx.astype(BF).astype(F4), turned)
        d_scb = d_sc.astype(BF)
        d_b = d_b + mm_tn(d_scb, c)
        d_c = d_c + mm(d_scb, b)
        conv_back(s, slice(XW, XW + N), br[rows[s], :N].astype(F4), d_b, turned)
        conv_back(s, slice(XW + N, CW), br[rows[s], N:].astype(F4), d_c, turned)
        ecol = rowbuf[s]
        both = gather_fine(colbuf[s], e[...])
        at_end = jnp.sum(tq, axis=1, keepdims=True) + lead_last * both[:, 0:1]
        d_cum = jnp.transpose(sums)[:HP] - dt * ecol - tq + lv
        d_la = running(d_cum + jnp.where(place == QC - 1, at_end, 0.0), True)
        v = jnp.transpose(rr[rows[s], :].astype(F4))[:HP] + hp[0]
        d_rate = (ecol + tq / jnp.maximum(dt, 1e-30) + d_la * hp[1]) * sigmoid(v)
        draw_o[rows[s], CW:] = cols_of(d_rate).astype(BF)
        hg[0] = hg[0] + d_rate
        hg[1] = hg[1] + d_la * dt * hp[1]
        hg[2] = hg[2] + jnp.where(place == 0, both[:, 1:2], 0.0)
    cg_o[...] = cg[...]
    hg_o[...] = hg[...]


def scan_back(seqs, x, bc, sl, sc, meta, ent, dy, d_end, raw, halo, taps, hp, skip, e):
    length = x.shape[0]
    span = seqs * QC
    n = length // span
    sd = jax.ShapeDtypeStruct
    return pl.pallas_call(
        back_kernel,
        grid=(n,),
        in_specs=[
            behind(n, span, XW),
            behind(n, span, 2 * N),
            behind(n, span, CW),
            behind3(n, seqs, 2 * HP, 128),
            behind3(n, seqs, 8, 128),
            behind3(n, seqs, N, XW),
            behind(n, span, XW),
            fixed(seqs, N, XW),
            behind(n, span, XW),
            behind(n, span, 2 * N, XW // (2 * N)),
            behind(n, span, 128, CW // 128),
            fixed(seqs, 8, CW),
            fixed(8, CW),
            fixed(2, HP, 128),
            fixed(1, XW),
            fixed(HP, XW),
        ],
        out_specs=[behind(n, span, AW), fixed(seqs, 8, CW), fixed(8, CW), fixed(3, HP, 128)],
        out_shape=[
            sd((length, AW), BF),
            sd((seqs, 8, CW), BF),
            sd((8, CW), F4),
            sd((3, HP, 128), F4),
        ],
        scratch_shapes=[
            pltpu.VMEM((seqs, N, XW), F4),
            pltpu.VMEM((seqs, 8, CW), F4),
            pltpu.VMEM((seqs, 8, XW), F4),
            pltpu.VMEM((seqs, HP, 128), F4),
            pltpu.VMEM((8, CW), F4),
            pltpu.VMEM((3, HP, 128), F4),
        ],
        compiler_params=pltpu.CompilerParams(vmem_limit_bytes=LIMIT),
        cost_estimate=work(length, 2),
        name="scan_back",
    )(x, bc, sl, sc, meta, ent, dy, d_end, raw, raw, raw, halo, taps, hp, skip, e)


def pad_lanes(v, width):
    return jnp.pad(v, [(0, 0)] * (v.ndim - 1) + [(0, width - v.shape[-1])])


def carried(state, decay, hops, by):
    total = shift(state, CHAIN, by)
    if hops == 1:
        return total
    total, product = total.astype(F4), 1.0
    for j in range(2, hops + 1):
        product = product * shift(decay, CHAIN, by * (j - 1))
        total = total + product * shift(state, CHAIN, by * j).astype(F4)
    return total.astype(BF)


def shards(
    tokens_in, seg_ids, in_norm, z_proj, xbc_proj, dt_proj, conv_taps, conv_bias,
    dt_bias, a_log, d_skip, gate_norm, out_proj, out_cotangent,
):
    seqs, rows, width = tokens_in.shape
    length = seg_ids.shape[1]
    block = rows * GROUP
    n_blocks = length // block
    hops = min(-(-(length // 4 - 1) // block), n_blocks - 1)
    n_sums = lax.axis_size("dp") * n_blocks
    hl = lax.axis_index("hl")
    own_rows = z_proj.shape[0]

    def collected(part):
        return lax.all_gather(part, "hl", axis=0).reshape(GROUP * seqs * rows, width)

    def quarters(w):
        return w.reshape(w.shape[0], GROUP, -1).transpose(1, 0, 2)

    bc_cols = jnp.broadcast_to(xbc_proj[None, :, DI:], (GROUP, own_rows, 2 * N))
    parts = [quarters(xbc_proj[:, :DI]), bc_cols, pad_lanes(quarters(dt_proj), 128), quarters(z_proj)]
    in_mine = lax.all_to_all(jnp.concatenate(parts, axis=-1), "hl", 0, 0, tiled=True)
    in_mine = in_mine.reshape(GROUP * own_rows, AW + XW)
    pairs = [(f, (f % n_sums) * GROUP + f // n_sums) for f in range(GROUP * n_sums)]
    wo_mine = lax.ppermute(out_proj, EVERY, pairs)
    in_mine, wo_mine, tokens_now = lax.optimization_barrier((in_mine, wo_mine, tokens_in))
    tokens = collected(tokens_now)
    cot = collected(out_cotangent)
    wx, wz = sums_gather(in_mine, [(0, AW), (AW, AW + XW)])
    [wo] = sums_gather(wo_mine, [(0, width)])

    def mine(v, size):
        return lax.dynamic_slice_in_dim(v, hl * size, size, axis=-1)

    taps = jnp.concatenate([conv_taps, conv_bias[None]], axis=0)
    taps = jnp.concatenate([mine(taps[:, :DI], XW), taps[:, DI:]], axis=1)
    taps = jnp.pad(taps, ((0, 3), (0, 0)))
    hp = jnp.stack([mine(dt_bias, HG), -jnp.exp(mine(a_log, HG))])
    hp = jnp.broadcast_to(jnp.pad(hp, ((0, 0), (0, HP - HG)))[:, :, None], (2, HP, 128))
    skip = jnp.repeat(mine(d_skip, HG), PS)[None]
    gain = mine(gate_norm, XW)[None]
    e = (jnp.arange(HP)[:, None] == jnp.arange(XW)[None, :] // PS).astype(BF)

    start = lax.axis_index(CHAIN) * block
    seg_pad = jnp.concatenate([jnp.full((seqs, 8), -1, jnp.int32), seg_ids], axis=1)
    near = lax.dynamic_slice_in_dim(seg_pad, start, block + 8, axis=1)
    seg = near[:, 8:].reshape(seqs, GROUP, QC)
    lines = [seg, jnp.broadcast_to(near[:, 7 : 7 + block : QC][:, :, None], seg.shape)]
    lines.append(jnp.broadcast_to(seg[:, :, QC - 1 :], seg.shape))
    for k in range(KW - 1):
        lines.append((near[:, 5 + k : 5 + k + block].reshape(seg.shape) == seg).astype(jnp.int32))
    lines.extend([jnp.zeros_like(seg)] * 2)
    meta = jnp.stack(lines, axis=2).astype(F4)
    meta = meta.transpose(1, 0, 2, 3).reshape(GROUP * seqs, 8, QC)

    tokens, wx, wz, wo, meta, taps, hp, skip, gain, e = lax.optimization_barrier(
        (tokens, wx, wz, wo, meta, taps, hp, skip, gain, e)
    )
    normed = norm_rows(tokens.astype(F4), in_norm).astype(BF)
    raw = mm(normed, wx).astype(BF)
    last = raw.reshape(GROUP, seqs, rows, AW)[GROUP - 1, :, rows - 8 :, :CW]
    halo = shift(last, CHAIN, 1)
    x, bc, sl, sc, state, decay = front(seqs, raw, halo, meta, taps, hp, e)
    decay_row = jnp.repeat(decay[:, :HG, 0], PS, axis=-1)[:, None]
    s_in = carried(state, decay_row, hops, 1)
    gates = mm(normed, wz)
    y, ent, squares = scan(seqs, x, bc, sc, meta, s_in, gates, skip, e)

    def team_sum(part):
        total = part
        for k in range(1, GROUP):
            total = total + swap(part, "hl", k)
        return total

    def spread_sum(part):
        total = lax.psum_scatter(part, "hl", scatter_dimension=0, tiled=True)
        return total.reshape(seqs, rows, width).astype(F4)

    squares = team_sum(squares)
    scale = lax.rsqrt(squares.reshape(-1, 1) * (1.0 / DI) + EPS)
    s_val = y.astype(F4) * jax.nn.silu(gates)
    gated = (s_val * scale * gain).astype(BF)
    out_rows = mm(gated, wo).astype(BF)
    cot, out_rows = lax.optimization_barrier((cot, out_rows))
    d_gated = mm_nt(cot, wo)
    along = team_sum(jnp.sum(d_gated * gain * s_val, axis=1).reshape(squares.shape))
    out_sum = spread_sum(out_rows)
    o_grad = mm_tn(gated, cot).astype(BF)
    dy, dz, gg, d_state = gate(seqs, y, gates, d_gated, squares, along, bc, sc, meta, gain, e)
    d_end = carried(d_state, decay_row, hops, -1)
    z_grad = mm_tn(normed, dz).astype(BF)
    from_z = mm_nt(dz, wz)
    dy, o_grad, z_grad, from_z = lax.optimization_barrier((dy, o_grad, z_grad, from_z))
    draw, rim, conv_total, head_total = scan_back(
        seqs, x, bc, sl, sc, meta, ent, dy, d_end, raw, halo, taps, hp, skip, e
    )
    rim = shift(rim, CHAIN, -1)
    o_half = team_halves(o_grad)
    z_half = team_halves(z_grad)
    rim, o_half, z_half, out_sum = lax.optimization_barrier((rim, o_half, z_half, out_sum))
    for s in range(seqs):
        at = ((GROUP - 1) * seqs + s) * rows + rows - 8
        edge = draw[at : at + 8, :CW].astype(F4) + rim[s].astype(F4)
        draw = lax.dynamic_update_slice(draw, edge.astype(BF), (at, 0))
    d_low = (from_z + mm_nt(draw, wx)).astype(BF)
    d_low, o_half, z_half, draw = lax.optimization_barrier((d_low, o_half, z_half, draw))
    d_sum = spread_sum(d_low)
    x_grad = mm_tn(normed, draw).astype(BF)
    norm_total = jnp.sum(x_grad.astype(F4) * wx.astype(F4), axis=1)
    norm_total = norm_total + jnp.sum(z_grad.astype(F4) * wz.astype(F4), axis=1)
    x_own = chain_sum(team_halves(x_grad)).reshape(GROUP, own_rows, AW)
    z_own = chain_sum(z_half).reshape(GROUP, own_rows, XW)
    o_own = chain_sum(o_half)
    out_proj_grad = lax.ppermute(o_own, EVERY, [(b, a) for a, b in pairs]).astype(F4)
    z_all = lax.all_to_all(z_own, "hl", 0, 0, tiled=True)

    pieces = [
        conv_total[:5, :XW].reshape(-1),
        gg[0],
        jnp.sum(head_total, axis=2).reshape(-1),
        conv_total[:5, XW:].reshape(-1),
        norm_total / in_norm,
    ]
    sizes = [p.shape[0] for p in pieces]
    pack = jnp.concatenate(pieces)
    lines_n = -(-pack.shape[0] // 1024) * 8
    total = lines_n * 128
    pack = jnp.pad(pack, (0, total - pack.shape[0])).reshape(lines_n, 128)
    for axis in SUMS:
        pack = pack + sum(swap(pack, axis, k) for k in range(1, lax.axis_size(axis)))
    high = pack.astype(BF)
    rest = (pack - high.astype(F4)).astype(BF)
    extra = -(-2 * total // (AW * 16)) * 16
    small = jnp.concatenate([high.reshape(-1), rest.reshape(-1)])
    small = jnp.pad(small, (0, extra * AW - 2 * total)).reshape(1, extra, AW)
    x_own = jnp.concatenate([x_own, jnp.broadcast_to(small, (GROUP, extra, AW))], axis=1)
    x_all = lax.all_to_all(x_own, "hl", 0, 0, tiled=True)
    x_all, d_sum = lax.optimization_barrier((x_all, d_sum))

    u = tokens_in.astype(F4)
    scale = lax.rsqrt(jnp.mean(u * u, axis=-1, keepdims=True) + EPS)
    hat = u * scale
    dh = d_sum * in_norm
    d_u = scale * (dh - hat * jnp.mean(dh * hat, axis=-1, keepdims=True))
    tokens_grad = d_u + out_cotangent.astype(F4)
    layer_out = (tokens_in.astype(F4) + out_sum).astype(BF)
    z_proj_grad = z_all.transpose(1, 0, 2).reshape(own_rows, DI).astype(F4)
    x_parts = x_all[:, :own_rows]
    xs = x_parts[:, :, :XW].transpose(1, 0, 2).reshape(own_rows, DI).astype(F4)
    bc_grad = jnp.sum(x_parts[:, :, XW:CW].astype(F4), axis=0)
    xbc_proj_grad = jnp.concatenate([xs, bc_grad], axis=1)
    dt_parts = x_parts[:, :, CW : CW + HG].transpose(1, 0, 2)
    dt_proj_grad = dt_parts.reshape(own_rows, H).astype(F4)
    got = x_all[:, own_rows:].astype(F4).reshape(GROUP, -1)
    flat = got[:, :total] + got[:, total : 2 * total]
    cuts = []
    low = 0
    for size in sizes:
        cuts.append(flat[:, low : low + size])
        low = low + size
    conv_x = cuts[0].reshape(GROUP, 5, XW).transpose(1, 0, 2).reshape(5, DI)
    conv_all = jnp.concatenate([conv_x, jnp.sum(cuts[3], axis=0).reshape(5, 2 * N)], axis=1)
    per_head = cuts[2].reshape(GROUP, 3, HP)[:, :, :HG].transpose(1, 0, 2).reshape(3, H)
    return (
        layer_out,
        tokens_grad,
        jnp.sum(cuts[4], axis=0),
        z_proj_grad,
        xbc_proj_grad,
        dt_proj_grad,
        conv_all[:4],
        conv_all[4],
        per_head[0],
        per_head[1],
        per_head[2],
        cuts[1].reshape(DI),
        out_proj_grad,
    )


def solution(mesh):
    sizes = dict(mesh.shape)
    grid = mesh.devices.reshape(sizes["dp"], sizes["ctx"], sizes["hd"] // GROUP, GROUP)
    fine = Mesh(grid, ("dp", "ctx", "hh", "hl"))
    tok = P("dp", ("ctx", "hh", "hl"), None)
    wgt = P(("dp", "ctx", "hh", "hl"), None)
    in_specs = (tok, P("dp", None), P(), wgt, wgt, wgt, P(), P(), P(), P(), P(), P(), wgt, tok)
    out_specs = (tok, tok, P(), wgt, wgt, wgt, P(), P(), P(), P(), P(), P(), wgt)
    return jax.shard_map(shards, mesh=fine, in_specs=in_specs, out_specs=out_specs, check_vma=False)
```

time: 551 us -> 411 us (0.75)
  the two profiles are of different devices: /device:TPU:0 before, /device:TPU:6 now
where the time goes in v2:
time: 411 us; the launch traced here: 404 us
  waiting for transfers between devices  137 us (33%)
  starting transfers between devices  66.6 us (16%)
  matrix products  55.6 us (14%)
  Pallas kernels  52.6 us (13%)
  other arithmetic  40.2 us (10%)
  local copies, waits for them, and re-layouts  36.6 us (9%)
  between operations  15.1 us (4%)
    ppermute x30, waiting for transfers between devices, swap(): return lax.ppermute(part, axis, [(i, i ^ k) for i in range(count)])  70.5 us
    ppermute x30, starting transfers between devices, swap(): return lax.ppermute(part, axis, [(i, i ^ k) for i in range(count)])  34.2 us
    pallas_call x1, Pallas kernels, scan_back(): pl.pallas_call(back_kernel, grid=(n,), in_specs=[behind(n, span, XW), beh...  24.8 us
    ppermute x1, waiting for transfers between devices, shards(): lax.ppermute(o_own, EVERY, [(b, a) for a, b in pairs]).astype(F4)  22.1 us
    dot_general x3, matrix products, mm_nt(): lax.dot_general(a, b, (((1,), (1,)), ((), ())), preferred_element_type=F4)  21.9 us
    ppermute x1, waiting for transfers between devices, shards(): wo_mine = lax.ppermute(out_proj, EVERY, pairs)  21 us
    ppermute x4, waiting for transfers between devices, shift(): return lax.ppermute(part, axes, pairs)  20.2 us
    dot_general x3, matrix products, mm(): return jnp.dot(a, b, preferred_element_type=F4)  18.9 us
  transfers between devices with their start and end apart: 43, of which 21 were waited for; matrix products, arithmetic and copies ran while one was open for 22% of the time, Pallas kernels for 13%

profile of v2, /device:TPU:6, one launch (start us, length us, event | category | flops | bytes accessed | tf_op | source)
XLA Modules:
  0.0 403.5 jit_solution(7128275357095295919)
XLA Ops:
  11.8 4.9 %all-to-all-start = ((bf16[4,48,1920]{2,1,0:T(8,128)(2,1)}), bf16[4,48,1920]{2,1,0:T(8,128)(2,1)S(1)}, u32[]{:S(2)}, u32[]{:S(2)}) async-start(bf16[4,48,1920]{2,1,0:T(8,128)(2,1)} %fusion.20), calls=%async_computation | async-start | bytes 1474560 | tf_op jit(solution)/shard_map/all_to_all | solution.py:680
  16.7 2.7 collective-permute-start
  19.4 21.0 %collective-permute-done.refs_0_ = bf16[96,1536]{1,0:T(8,128)(2,1)S(1)} collective-permute-done((bf16[96,1536]{1,0:T(8,128)(2,1)S(1)}, bf16[96,1536]{1,0:T(8,128)(2,1)S(1)}, u32[]{:S(2)}, u32[]{:S(2)}) %collective-permute-start) | collective-permute-done | bytes 294944 | tf_op jit(solution)/shard_map/ppermute | solution.py:683
  40.6 5.3 %collective-permute-start.2 = (bf16[192,1920]{1,0:T(8,128)(2,1)S(1)}, bf16[192,1920]{1,0:T(8,128)(2,1)S(1)}, u32[]{:S(2)}, u32[]{:S(2)}) collective-permute-start(bf16[192,1920]{1,0:T(8,128)(2,1)S(1)} %bitcast.145), channel_id=1, source_target_pairs={{0,8},{4,12},{8,0},{12,4},{1,9},{5,13},{9,1},{13,5},{2,10},{6,14},... | collective-permute-start | bytes 2211848 | tf_op jit(solution)/shard_map/ppermute | solution.py:32
  45.9 15.0 %collective-permute-done.3.refs_3_ = bf16[192,1920]{1,0:T(8,128)(2,1)S(1)} collective-permute-done((bf16[192,1920]{1,0:T(8,128)(2,1)S(1)}, bf16[192,1920]{1,0:T(8,128)(2,1)S(1)}, u32[]{:S(2)}, u32[]{:S(2)}) %collective-permute-start.3) | collective-permute-done | bytes 737312 | tf_op jit(solution)/shard_map/ppermute | solution.py:32
  61.8 14.8 %collective-permute-done.2.refs_2_ = bf16[192,1920]{1,0:T(8,128)(2,1)S(1)} collective-permute-done((bf16[192,1920]{1,0:T(8,128)(2,1)S(1)}, bf16[192,1920]{1,0:T(8,128)(2,1)S(1)}, u32[]{:S(2)}, u32[]{:S(2)}) %collective-permute-start.2) | collective-permute-done | bytes 737312 | tf_op jit(solution)/shard_map/ppermute | solution.py:32
  83.6 3.0 collective-permute-start.7
  88.2 6.2 %collective-permute-done.7.refs_3_ = bf16[96,1536]{1,0:T(8,128)(2,1)S(1)} collective-permute-done((bf16[96,1536]{1,0:T(8,128)(2,1)S(1)}, bf16[96,1536]{1,0:T(8,128)(2,1)S(1)}, u32[]{:S(2)}, u32[]{:S(2)}) %collective-permute-start.7) | collective-permute-done | bytes 294944 | tf_op jit(solution)/shard_map/ppermute | solution.py:32
  94.4 5.8 %collective-permute-done.6.refs_2_ = bf16[96,1536]{1,0:T(8,128)(2,1)S(1)} collective-permute-done((bf16[96,1536]{1,0:T(8,128)(2,1)S(1)}, bf16[96,1536]{1,0:T(8,128)(2,1)S(1)}, u32[]{:S(2)}, u32[]{:S(2)}) %collective-permute-start.6) | collective-permute-done | bytes 294944 | tf_op jit(solution)/shard_map/ppermute | solution.py:32
  115.7 2.8 fusion
  118.7 6.7 %convolution_convert_fusion.2.xr.br.rr = bf16[1024,1152]{1,0:T(8,128)(2,1)S(1)} fusion(bf16[1536,1152]{1,0:T(8,128)(2,1)} %pad_maximum_fusion, bf16[1024,1536]{1,0:T(8,128)(2,1)S(1)} %bitcast.166, f32[1536]{0:T(1024)S(1)} %copy-done.33, f32[1024]{0:T(1024)S(1)} %add_rsqrt_fusion.1), kind=kOutput, calls=%fused_computation.10 | convolution fusion | flops 3631349760 | bytes 9054208 | tf_op jit(solution)/shard_map/dot_general | solution.py:44
  127.0 4.5 %collective-permute-done.9.halo = bf16[2,8,1024]{2,1,0:T(8,128)(2,1)S(1)} collective-permute-done((bf16[2,8,1024]{2,1,0:T(8,128)(2,1)S(1)}, bf16[2,8,1024]{2,1,0:T(8,128)(2,1)S(1)}, u32[]{:S(2)}, u32[]{:S(2)}) %collective-permute-start.9) | collective-permute-done | bytes 32800 | tf_op jit(solution)/shard_map/ppermute | solution.py:40
  131.5 10.1 %conv_state.1 = (bf16[1024,768]{1,0:T(8,128)(2,1)S(1)}, bf16[1024,256]{1,0:T(8,128)(2,1)S(1)}, bf16[1024,1024]{1,0:T(8,128)(2,1)S(1)}, f32[8,32,128]{2,1,0:T(8,1...) custom-call(bf16[1024,1152]{1,0:T(8,128)(2,1)} %copy-done.15, bf16[1024,1152]{1,0:T(8,128)(2,1)} %copy-done.15, ...), custom_call_target="tpu_custom_call" | custom-call | flops 1000000000 | bytes 8388608 | tf_op jit(solution)/shard_map/conv_state/pallas_call | solution.py:275
  143.1 4.3 %fusion.45.z_r = f32[1024,768]{1,0:T(8,128)} fusion(bf16[1536,768]{1,0:T(8,128)(2,1)S(1)} %copy-done.18, bf16[1024,1536]{1,0:T(8,128)(2,1)S(1)} %bitcast.167, f32[1536]{0:T(1024)S(1)} %copy-done.33, f32[1024]{0:T(1024)S(1)} %add_rsqrt_fusion.1), kind=kOutput, calls=%fused_computation.144 | convolution fusion | flops 2422210560 | bytes 8660992 | tf_op jit(solution)/shard_map/dot_general | solution.py:44
  147.5 7.2 %collective-permute-done.10.s_in = bf16[2,128,768]{2,1,0:T(8,128)(2,1)S(1)} collective-permute-done((bf16[2,128,768]{2,1,0:T(8,128)(2,1)S(1)}, bf16[2,128,768]{2,1,0:T(8,128)(2,1)S(1)}, u32[]{:S(2)}, u32[]{:S(2)}) %collective-permute-start.10) | collective-permute-done | bytes 393248 | tf_op jit(solution)/shard_map/ppermute | solution.py:40
  154.6 9.5 %scan_gate.1 = (bf16[1024,768]{1,0:T(8,128)(2,1)S(1)}, bf16[8,128,768]{2,1,0:T(8,128)(2,1)S(1)}, f32[8,1,128]{2,1,0:T(1,128)S(1)}) custom-call(bf16[1024,768]{1,0:T(8,128)(2,1)S(1)} %get-tuple-element.67.x_r, bf16[1024,256]{1,0:T(8,128)(2,1)S(1)} %get-tuple-element.68.bc, f32[8,32,128]{2,1,0:T(8,128)S(1)} %get-tuple-element.70.sc, ...), custom_call_target="tpu_custom_call" | custom-call | flops 1000000000 | bytes 8388608 | tf_op jit(solution)/shard_map/scan_gate/pallas_call | solution.py:376
  168.0 2.8 collective-permute-start.11
  172.5 7.9 %convolution_convert_fusion.1 = bf16[1024,1536]{1,0:T(8,128)(2,1)} fusion(bf16[768,1536]{1,0:T(8,128)(2,1)} %pad_maximum_fusion.2, f32[768]{0:T(1024)S(1)} %reduce, f32[1024]{0:T(1024)S(1)} %bitcast.195, f32[1024,768]{1,0:T(8,128)} %fusion.45.z_r, bf16[1024,768]{1,0:T(8,128)(2,1)} %copy-done.3), kind=kOutput, calls=%fused_computation.9 | convolution fusion | flops 2424569856 | bytes 10230784 | tf_op jit(solution)/shard_map/dot_general | solution.py:44
  180.7 8.7 %multiply_reduce_fusion.2 = (f32[1024]{0:T(1024)S(1)}, f32[1024,768]{1,0:T(8,128)}) fusion(f32[768]{0:T(1024)S(1)} %reduce, f32[1024,768]{1,0:T(8,128)} %fusion.45.z_r, bf16[1024,768]{1,0:T(8,128)(2,1)} %copy-done.3, bf16[1024,1536]{1,0:T(8,128)(2,1)} %bitcast.197, bf16[768,1536]{1,0:T(8,128)(2,1)} %pad_maximum_fusion.2), kind=kOutput, calls=%fused_computation.16 | convolution fusion | flops 2422995968 | bytes 13376512 | tf_op jit(solution)/shard_map/dot_general | solution.py:48
  193.8 3.2 convolution_convert_fusion.4
  198.3 6.9 %gate_back.1 = (bf16[1024,768]{1,0:T(8,128)(2,1)S(1)}, bf16[1024,768]{1,0:T(8,128)(2,1)S(1)}, f32[8,768]{1,0:T(8,128)S(1)}, bf16[2,128,768]{2,1,0:T(8,128)(2,1)S(1)}) custom-call(bf16[1024,768]{1,0:T(8,128)(2,1)S(1)} %copy-done.4, f32[1024,768]{1,0:T(8,128)} %fusion.45.z_r, f32[1024,768]{1,0:T(8,128)} %get-tuple-element.174.dg_r, ...), custom_call_target="tpu_custom_call" | custom-call | flops 1000000000 | bytes 8388608 | tf_op jit(solution)/shard_map/gate_back/pallas_call | solution.py:445
  205.3 4.7 %fusion.48 = f32[1024,1536]{1,0:T(8,128)} fusion(bf16[1024,768]{1,0:T(8,128)(2,1)S(1)} %get-tuple-element.81, bf16[1536,768]{1,0:T(8,128)(2,1)S(1)} %copy-done.19), kind=kOutput, calls=%fused_computation.145 | convolution fusion | flops 2415919104 | bytes 10223616 | tf_op jit(solution)/shard_map/dot_general | solution.py:48
  209.9 3.3 convolution_convert_fusion.3
  216.1 4.1 %collective-permute-start.17 = (bf16[2,128,768]{2,1,0:T(8,128)(2,1)S(1)}, bf16[2,128,768]{2,1,0:T(8,128)(2,1)S(1)}, u32[]{:S(2)}, u32[]{:S(2)}) collective-permute-start(bf16[2,128,768]{2,1,0:T(8,128)(2,1)S(1)} %get-tuple-element.83), channel_id=1, source_target_pairs={{4,0},{8,4},{12,8},{5,1},{9,5},{13,9},{6,2},{10,6},{14,10},{7,3},{... | collective-permute-start | bytes 1179656 | tf_op jit(solution)/shard_map/ppermute | solution.py:40
  220.2 8.5 %collective-permute-done.17.d_end = bf16[2,128,768]{2,1,0:T(8,128)(2,1)S(1)} collective-permute-done((bf16[2,128,768]{2,1,0:T(8,128)(2,1)S(1)}, bf16[2,128,768]{2,1,0:T(8,128)(2,1)S(1)}, u32[]{:S(2)}, u32[]{:S(2)}) %collective-permute-start.17) | collective-permute-done | bytes 393248 | tf_op jit(solution)/shard_map/ppermute | solution.py:40
  231.6 24.8 %scan_back.1 = (bf16[1024,1152]{1,0:T(8,128)(2,1)}, bf16[2,8,1024]{2,1,0:T(8,128)(2,1)S(1)}, f32[8,1024]{1,0:T(8,128)S(1)}, f32[3,16,128]{2,1,0:T(8,128)S(1)}) custom-call(bf16[1024,768]{1,0:T(8,128)(2,1)S(1)} %get-tuple-element.67.x_r, bf16[1024,256]{1,0:T(8,128)(2,1)S(1)} %get-tuple-element.68.bc, bf16[1024,1024]{1,0:T(8,128)(2,1)} %copy-done.2, ...), custom_call_target="tpu_custom_call" | custom-call | flops 2000000000 | bytes 8388608 | tf_op jit(solution)/shard_map/scan_back/pallas_call | solution.py:602
  256.3 4.7 %collective-permute-start.18 = (bf16[2,8,1024]{2,1,0:T(8,128)(2,1)S(1)}, bf16[2,8,1024]{2,1,0:T(8,128)(2,1)S(1)}, u32[]{:S(2)}, u32[]{:S(2)}) collective-permute-start(bf16[2,8,1024]{2,1,0:T(8,128)(2,1)S(1)} %get-tuple-element.84), channel_id=1, source_target_pairs={{4,0},{8,4},{12,8},{5,1},{9,5},{13,9},{6,2},{10,6},{14,10},{7,3},{... | collective-permute-start | bytes 98312 | tf_op jit(solution)/shard_map/ppermute | solution.py:40
  261.1 2.6 fusion.5
  263.7 2.6 fusion.4
  266.2 2.6 convert.19
  270.3 8.6 %add_convert_fusion = bf16[1024,1536]{1,0:T(8,128)(2,1)} fusion(f32[1024,1536]{1,0:T(8,128)} %fusion.48, bf16[1024,1152]{1,0:T(8,128)(2,1)S(1)} %fusion.37, bf16[1536,1152]{1,0:T(8,128)(2,1)} %pad_maximum_fusion), kind=kOutput, calls=%fused_computation.7 | convolution fusion | flops 3627024384 | bytes 15335424 | tf_op jit(solution)/shard_map/dot_general | solution.py:48
  278.9 8.2 %multiply_reduce_fusion = (f32[1536]{0:T(1024)S(1)}, bf16[1536,1152]{1,0:T(8,128)(2,1)S(1)}) fusion(bf16[1536,1152]{1,0:T(8,128)(2,1)} %pad_maximum_fusion, bf16[1024,1152]{1,0:T(8,128)(2,1)} %copy-done.39, bf16[1024,1536]{1,0:T(8,128)(2,1)} %bitcast.165, f32[1536]{0:T(1024)S(1)} %copy-done.33, f32[1024]{0:T(1024)S(1)} %add_rsqrt_fusion.1), kind=kOutput, calls=%fused_computation.3 | convolution fusion | flops 3639015936 | bytes 12599296 | tf_op jit(solution)/shard_map/dot_general | solution.py:52
  294.9 2.3 collective-permute-start.27
  299.4 3.9 collective-permute-done.28
  303.3 2.9 collective-permute-start.31
  306.2 2.5 fusion.3
  310.7 2.6 collective-permute-start.24
  315.1 4.3 %collective-permute-done.30 = bf16[192,768]{1,0:T(8,128)(2,1)} collective-permute-done((bf16[192,768]{1,0:T(8,128)(2,1)S(1)}, bf16[192,768]{1,0:T(8,128)(2,1)}, u32[]{:S(2)}, u32[]{:S(2)}) %collective-permute-start.30) | collective-permute-done | bytes 294944 | tf_op jit(solution)/shard_map/ppermute | solution.py:32
  319.3 2.5 collective-permute-start.34
  323.9 3.5 all-to-all-start.2
  327.5 6.6 %collective-permute-done.24 = bf16[192,1152]{1,0:T(8,128)(2,1)S(1)} collective-permute-done((bf16[192,1152]{1,0:T(8,128)(2,1)}, bf16[192,1152]{1,0:T(8,128)(2,1)S(1)}, u32[]{:S(2)}, u32[]{:S(2)}) %collective-permute-start.24) | collective-permute-done | bytes 442400 | tf_op jit(solution)/shard_map/ppermute | solution.py:32
  334.1 6.3 %collective-permute-done.23 = bf16[192,1152]{1,0:T(8,128)(2,1)S(1)} collective-permute-done((bf16[192,1152]{1,0:T(8,128)(2,1)}, bf16[192,1152]{1,0:T(8,128)(2,1)S(1)}, u32[]{:S(2)}, u32[]{:S(2)}) %collective-permute-start.23) | collective-permute-done | bytes 442400 | tf_op jit(solution)/shard_map/ppermute | solution.py:32
  341.5 3.0 all-to-all-done.2
  344.5 3.5 all-to-all-start.1
  348.0 2.8 collective-permute-done.33
  352.2 5.7 %collective-permute-start.35 = (bf16[96,1536]{1,0:T(8,128)(2,1)S(1)}, bf16[96,1536]{1,0:T(8,128)(2,1)S(1)}, u32[]{:S(2)}, u32[]{:S(2)}) collective-permute-start(bf16[96,1536]{1,0:T(8,128)(2,1)S(1)} %fusion.23), channel_id=1, source_target_pairs={{0,0},{4,1},{8,2},{12,3},{16,4},{20,5},{24,6},{28,7},{1,8},{5,9},{... | collective-permute-start | bytes 884744 | tf_op jit(solution)/shard_map/ppermute | solution.py:772
  358.1 22.1 %collective-permute-done.35 = bf16[96,1536]{1,0:T(8,128)(2,1)S(1)} collective-permute-done((bf16[96,1536]{1,0:T(8,128)(2,1)S(1)}, bf16[96,1536]{1,0:T(8,128)(2,1)S(1)}, u32[]{:S(2)}, u32[]{:S(2)}) %collective-permute-start.35) | collective-permute-done | bytes 294944 | tf_op jit(solution)/shard_map/ppermute | solution.py:772
  392.2 3.4 fusion.11
  (261 shorter events, 82.6 us)
Async XLA Ops:
  11.8 28.6 %all-to-all-start = ((bf16[4,48,1920]{2,1,0:T(8,128)(2,1)}), bf16[4,48,1920]{2,1,0:T(8,128)(2,1)S(1)}, u32[]{:S(2)}, u32[]{:S(2)}) async-start(bf16[4,48,1920]{2,1,0:T(8,128)(2,1)} %fusion.20), calls=%async_computation | async-start | bytes 1474560 | tf_op jit(solution)/shard_map/all_to_all | solution.py:680
  16.7 98.9 %all-gather.5.cloned.1.call-start = ((), (), s32[]{:S(2)}) async-start(), calls=%async_computation.7 | async-start | bytes 3932160 | tf_op jit(solution)/shard_map/all_gather | solution.py:673
  16.7 23.7 %collective-permute-start = (bf16[96,1536]{1,0:T(8,128)(2,1)S(1)}, bf16[96,1536]{1,0:T(8,128)(2,1)S(1)}, u32[]{:S(2)}, u32[]{:S(2)}) collective-permute-start(bf16[96,1536]{1,0:T(8,128)(2,1)S(1)} %copy-done.41), channel_id=1, source_target_pairs={{0,0},{1,4},{2,8},{3,12},{4,16},{5,20},{6,24},{7,28},{8,1},{9,5},{... | collective-permute-start | bytes 884744 | tf_op jit(solution)/shard_map/ppermute | solution.py:683
  40.4 37.0 %copy-start = (bf16[4,48,1920]{2,1,0:T(8,128)(2,1)}, bf16[4,48,1920]{2,1,0:T(8,128)(2,1)S(1)}, u32[]{:S(2)}) copy-start(bf16[4,48,1920]{2,1,0:T(8,128)(2,1)S(1)} %all-to-all-done) | copy-start | bytes 2211844
  40.5 140.0 %all-gather.7.cloned.1.call-start = ((), (), s32[]{:S(2)}) async-start(), calls=%async_computation.8 | async-start | bytes 3932160 | tf_op jit(solution)/shard_map/all_gather | solution.py:673
  40.5 20.4 %collective-permute-start.3 = (bf16[192,1920]{1,0:T(8,128)(2,1)S(1)}, bf16[192,1920]{1,0:T(8,128)(2,1)S(1)}, u32[]{:S(2)}, u32[]{:S(2)}) collective-permute-start(bf16[192,1920]{1,0:T(8,128)(2,1)S(1)} %bitcast.144), channel_id=1, source_target_pairs={{0,12},{4,8},{8,4},{12,0},{1,13},{5,9},{9,5},{13,1},{2,14},{6,10},... | collective-permute-start | bytes 2211848 | tf_op jit(solution)/shard_map/ppermute | solution.py:32
  40.6 35.9 %collective-permute-start.2 = (bf16[192,1920]{1,0:T(8,128)(2,1)S(1)}, bf16[192,1920]{1,0:T(8,128)(2,1)S(1)}, u32[]{:S(2)}, u32[]{:S(2)}) collective-permute-start(bf16[192,1920]{1,0:T(8,128)(2,1)S(1)} %bitcast.145), channel_id=1, source_target_pairs={{0,8},{4,12},{8,0},{12,4},{1,9},{5,13},{9,1},{13,5},{2,10},{6,14},... | collective-permute-start | bytes 2211848 | tf_op jit(solution)/shard_map/ppermute | solution.py:32
  45.9 31.6 %collective-permute-start.1 = (bf16[192,1920]{1,0:T(8,128)(2,1)S(1)}, bf16[192,1920]{1,0:T(8,128)(2,1)S(1)}, u32[]{:S(2)}, u32[]{:S(2)}) collective-permute-start(bf16[192,1920]{1,0:T(8,128)(2,1)S(1)} %bitcast.146), channel_id=1, source_target_pairs={{0,4},{4,0},{8,12},{12,8},{1,5},{5,1},{9,13},{13,9},{2,6},{6,2},{1... | collective-permute-start | bytes 2211848 | tf_op jit(solution)/shard_map/ppermute | solution.py:32
  83.0 20.9 %copy-start.32 = (f32[4,3328]{1,0:T(4,128)S(1)}, f32[4,3328]{1,0:T(4,128)}, u32[]{:S(2)}) copy-start(f32[4,3328]{1,0:T(4,128)} %param.20) | copy-start | bytes 159748
  83.0 20.9 %copy-start.36 = (f32[48]{0:T(128)S(1)}, f32[48]{0:T(128)}, u32[]{:S(2)}) copy-start(f32[48]{0:T(128)} %param.23) | copy-start | bytes 580
  83.1 20.9 %copy-start.37 = (f32[48]{0:T(128)S(1)}, f32[48]{0:T(128)}, u32[]{:S(2)}) copy-start(f32[48]{0:T(128)} %param.22) | copy-start | bytes 580
  83.1 25.6 %collective-permute-start.4 = (bf16[768,1920]{1,0:T(8,128)(2,1)S(1)}, bf16[768,1920]{1,0:T(8,128)(2,1)}, u32[]{:S(2)}, u32[]{:S(2)}) collective-permute-start(bf16[768,1920]{1,0:T(8,128)(2,1)S(1)} %place_rows.2), channel_id=1, source_target_pairs={{0,16},{16,0},{1,17},{17,1},{2,18},{18,2},{3,19},{19,3},{4,20},{20... | collective-permute-start | bytes 8847368 | tf_op jit(solution)/shard_map/ppermute | solution.py:32
  83.5 182.7 %reduce-scatter.3.cloned.1.call-start = ((), (), s32[]{:S(2)}) async-start(), calls=%async_computation.5 | async-start | bytes 3932160 | tf_op jit(solution)/shard_map/reduce_scatter | solution.py:734
  83.6 10.8 %collective-permute-start.7 = (bf16[96,1536]{1,0:T(8,128)(2,1)S(1)}, bf16[96,1536]{1,0:T(8,128)(2,1)S(1)}, u32[]{:S(2)}, u32[]{:S(2)}) collective-permute-start(bf16[96,1536]{1,0:T(8,128)(2,1)S(1)} %collective-permute-done.refs_0_), channel_id=1, source_target_pairs={{0,12},{4,8},{8,4},{12,0},{1,13},{5,9},{9,5},{13,1},{2,14},{6,10},... | collective-permute-start | bytes 884744 | tf_op jit(solution)/shard_map/ppermute | solution.py:32
  86.6 13.7 %collective-permute-start.6 = (bf16[96,1536]{1,0:T(8,128)(2,1)S(1)}, bf16[96,1536]{1,0:T(8,128)(2,1)S(1)}, u32[]{:S(2)}, u32[]{:S(2)}) collective-permute-start(bf16[96,1536]{1,0:T(8,128)(2,1)S(1)} %collective-permute-done.refs_0_), channel_id=1, source_target_pairs={{0,8},{4,12},{8,0},{12,4},{1,9},{5,13},{9,1},{13,5},{2,10},{6,14},... | collective-permute-start | bytes 884744 | tf_op jit(solution)/shard_map/ppermute | solution.py:32
  88.1 12.9 %collective-permute-start.5 = (bf16[96,1536]{1,0:T(8,128)(2,1)S(1)}, bf16[96,1536]{1,0:T(8,128)(2,1)S(1)}, u32[]{:S(2)}, u32[]{:S(2)}) collective-permute-start(bf16[96,1536]{1,0:T(8,128)(2,1)S(1)} %collective-permute-done.refs_0_), channel_id=1, source_target_pairs={{0,4},{4,0},{8,12},{12,8},{1,5},{5,1},{9,13},{13,9},{2,6},{6,2},{1... | collective-permute-start | bytes 884744 | tf_op jit(solution)/shard_map/ppermute | solution.py:32
  102.1 3.2 collective-permute-start.8
  125.4 6.1 %collective-permute-start.9 = (bf16[2,8,1024]{2,1,0:T(8,128)(2,1)S(1)}, bf16[2,8,1024]{2,1,0:T(8,128)(2,1)S(1)}, u32[]{:S(2)}, u32[]{:S(2)}) collective-permute-start(bf16[2,8,1024]{2,1,0:T(8,128)(2,1)S(1)} %slice_bitcast_fusion), channel_id=1, source_target_pairs={{0,4},{4,8},{8,12},{1,5},{5,9},{9,13},{2,6},{6,10},{10,14},{3,7},{... | collective-permute-start | bytes 98312 | tf_op jit(solution)/shard_map/ppermute | solution.py:40
  141.6 13.0 %collective-permute-start.10 = (bf16[2,128,768]{2,1,0:T(8,128)(2,1)S(1)}, bf16[2,128,768]{2,1,0:T(8,128)(2,1)S(1)}, u32[]{:S(2)}, u32[]{:S(2)}) collective-permute-start(bf16[2,128,768]{2,1,0:T(8,128)(2,1)S(1)} %get-tuple-element.71), channel_id=1, source_target_pairs={{0,4},{4,8},{8,12},{1,5},{5,9},{9,13},{2,6},{6,10},{10,14},{3,7},{... | collective-permute-start | bytes 1179656 | tf_op jit(solution)/shard_map/ppermute | solution.py:40
  166.4 5.4 %collective-permute-start.13 = (f32[8,1,128]{2,1,0:T(1,128)S(1)}, f32[8,1,128]{2,1,0:T(1,128)S(1)}, u32[]{:S(2)}, u32[]{:S(2)}) collective-permute-start(f32[8,1,128]{2,1,0:T(1,128)S(1)} %get-tuple-element.76), channel_id=1, source_target_pairs={{0,3},{1,2},{2,1},{3,0},{4,7},{5,6},{6,5},{7,4},{8,11},{9,10},{10,... | collective-permute-start | bytes 12296 | tf_op jit(solution)/shard_map/ppermute | solution.py:32
  168.0 4.5 %collective-permute-start.12 = (f32[8,1,128]{2,1,0:T(1,128)S(1)}, f32[8,1,128]{2,1,0:T(1,128)S(1)}, u32[]{:S(2)}, u32[]{:S(2)}) collective-permute-start(f32[8,1,128]{2,1,0:T(1,128)S(1)} %get-tuple-element.76), channel_id=1, source_target_pairs={{0,2},{1,3},{2,0},{3,1},{4,6},{5,7},{6,4},{7,5},{8,10},{9,11},{10,... | collective-permute-start | bytes 12296 | tf_op jit(solution)/shard_map/ppermute | solution.py:32
  168.0 4.5 %collective-permute-start.11 = (f32[8,1,128]{2,1,0:T(1,128)S(1)}, f32[8,1,128]{2,1,0:T(1,128)S(1)}, u32[]{:S(2)}, u32[]{:S(2)}) collective-permute-start(f32[8,1,128]{2,1,0:T(1,128)S(1)} %get-tuple-element.76), channel_id=1, source_target_pairs={{0,1},{1,0},{2,3},{3,2},{4,5},{5,4},{6,7},{7,6},{8,9},{9,8},{10,11... | collective-permute-start | bytes 12296 | tf_op jit(solution)/shard_map/ppermute | solution.py:32
  180.5 201.5 %reduce-scatter.5.cloned.1.call-start = ((), (), s32[]{:S(2)}) async-start(), calls=%async_computation.6 | async-start | bytes 3932160 | tf_op jit(solution)/shard_map/reduce_scatter | solution.py:734
  189.4 7.6 %collective-permute-start.16 = (f32[8,1,128]{2,1,0:T(1,128)S(1)}, f32[8,1,128]{2,1,0:T(1,128)S(1)}, u32[]{:S(2)}, u32[]{:S(2)}) collective-permute-start(f32[8,1,128]{2,1,0:T(1,128)S(1)} %bitcast.187), channel_id=1, source_target_pairs={{0,3},{1,2},{2,1},{3,0},{4,7},{5,6},{6,5},{7,4},{8,11},{9,10},{10,... | collective-permute-start | bytes 12296 | tf_op jit(solution)/shard_map/ppermute | solution.py:32
  191.7 6.6 %collective-permute-start.15 = (f32[8,1,128]{2,1,0:T(1,128)S(1)}, f32[8,1,128]{2,1,0:T(1,128)S(1)}, u32[]{:S(2)}, u32[]{:S(2)}) collective-permute-start(f32[8,1,128]{2,1,0:T(1,128)S(1)} %bitcast.188), channel_id=1, source_target_pairs={{0,2},{1,3},{2,0},{3,1},{4,6},{5,7},{6,4},{7,5},{8,10},{9,11},{10,... | collective-permute-start | bytes 12296 | tf_op jit(solution)/shard_map/ppermute | solution.py:32
  192.8 5.5 %collective-permute-start.14 = (f32[8,1,128]{2,1,0:T(1,128)S(1)}, f32[8,1,128]{2,1,0:T(1,128)S(1)}, u32[]{:S(2)}, u32[]{:S(2)}) collective-permute-start(f32[8,1,128]{2,1,0:T(1,128)S(1)} %bitcast.189), channel_id=1, source_target_pairs={{0,1},{1,0},{2,3},{3,2},{4,5},{5,4},{6,7},{7,6},{8,9},{9,8},{10,11... | collective-permute-start | bytes 12296 | tf_op jit(solution)/shard_map/ppermute | solution.py:32
  214.5 46.6 %collective-permute-start.19 = (bf16[384,1536]{1,0:T(8,128)(2,1)}, bf16[384,1536]{1,0:T(8,128)(2,1)}, u32[]{:S(2)}, u32[]{:S(2)}) collective-permute-start(bf16[384,1536]{1,0:T(8,128)(2,1)} %dynamic-slice_bitcast_fusion.2), channel_id=1, source_target_pairs={{0,16},{16,0},{1,17},{17,1},{2,18},{18,2},{3,19},{19,3},{4,20},{20... | collective-permute-start | bytes 3538952 | tf_op jit(solution)/shard_map/ppermute | solution.py:32
  215.6 48.1 %collective-permute-start.20 = (bf16[768,768]{1,0:T(8,128)(2,1)}, bf16[768,768]{1,0:T(8,128)(2,1)}, u32[]{:S(2)}, u32[]{:S(2)}) collective-permute-start(bf16[768,768]{1,0:T(8,128)(2,1)} %dynamic-slice_bitcast_fusion.1), channel_id=1, source_target_pairs={{0,16},{16,0},{1,17},{17,1},{2,18},{18,2},{3,19},{19,3},{4,20},{20... | collective-permute-start | bytes 3538952 | tf_op jit(solution)/shard_map/ppermute | solution.py:32
  216.1 12.6 %collective-permute-start.17 = (bf16[2,128,768]{2,1,0:T(8,128)(2,1)S(1)}, bf16[2,128,768]{2,1,0:T(8,128)(2,1)S(1)}, u32[]{:S(2)}, u32[]{:S(2)}) collective-permute-start(bf16[2,128,768]{2,1,0:T(8,128)(2,1)S(1)} %get-tuple-element.83), channel_id=1, source_target_pairs={{4,0},{8,4},{12,8},{5,1},{9,5},{13,9},{6,2},{10,6},{14,10},{7,3},{... | collective-permute-start | bytes 1179656 | tf_op jit(solution)/shard_map/ppermute | solution.py:40
  231.6 29.5 %copy-start.30 = (bf16[768,1536]{1,0:T(8,128)(2,1)S(1)}, bf16[768,1536]{1,0:T(8,128)(2,1)}, u32[]{:S(2)}) copy-start(bf16[768,1536]{1,0:T(8,128)(2,1)} %copy-done.29) | copy-start | bytes 7077892
  256.3 12.5 %collective-permute-start.18 = (bf16[2,8,1024]{2,1,0:T(8,128)(2,1)S(1)}, bf16[2,8,1024]{2,1,0:T(8,128)(2,1)S(1)}, u32[]{:S(2)}, u32[]{:S(2)}) collective-permute-start(bf16[2,8,1024]{2,1,0:T(8,128)(2,1)S(1)} %get-tuple-element.84), channel_id=1, source_target_pairs={{4,0},{8,4},{12,8},{5,1},{9,5},{13,9},{6,2},{10,6},{14,10},{7,3},{... | collective-permute-start | bytes 98312 | tf_op jit(solution)/shard_map/ppermute | solution.py:40
  288.5 17.7 %collective-permute-start.21 = (bf16[768,1152]{1,0:T(8,128)(2,1)}, bf16[768,1152]{1,0:T(8,128)(2,1)}, u32[]{:S(2)}, u32[]{:S(2)}) collective-permute-start(bf16[768,1152]{1,0:T(8,128)(2,1)} %dynamic-slice_bitcast_fusion), channel_id=1, source_target_pairs={{0,16},{16,0},{1,17},{17,1},{2,18},{18,2},{3,19},{19,3},{4,20},{20... | collective-permute-start | bytes 5308424 | tf_op jit(solution)/shard_map/ppermute | solution.py:32
  291.6 3.2 collective-permute-start.25
  293.6 19.6 %collective-permute-start.29 = (bf16[192,768]{1,0:T(8,128)(2,1)S(1)}, bf16[192,768]{1,0:T(8,128)(2,1)S(1)}, u32[]{:S(2)}, u32[]{:S(2)}) collective-permute-start(bf16[192,768]{1,0:T(8,128)(2,1)S(1)} %get-tuple-element.161), channel_id=1, source_target_pairs={{0,4},{4,0},{8,12},{12,8},{1,5},{5,1},{9,13},{13,9},{2,6},{6,2},{1... | collective-permute-start | bytes 884744 | tf_op jit(solution)/shard_map/ppermute | solution.py:32
  294.9 8.4 %collective-permute-start.28 = (f32[64,128]{1,0:T(8,128)S(1)}, f32[64,128]{1,0:T(8,128)S(1)}, u32[]{:S(2)}, u32[]{:S(2)}) collective-permute-start(f32[64,128]{1,0:T(8,128)S(1)} %fusion.42), channel_id=1, source_target_pairs={{0,12},{4,8},{8,4},{12,0},{1,13},{5,9},{9,5},{13,1},{2,14},{6,10},... | collective-permute-start | bytes 98312 | tf_op jit(solution)/shard_map/ppermute | solution.py:32
  294.9 11.2 %collective-permute-start.27 = (f32[64,128]{1,0:T(8,128)S(1)}, f32[64,128]{1,0:T(8,128)S(1)}, u32[]{:S(2)}, u32[]{:S(2)}) collective-permute-start(f32[64,128]{1,0:T(8,128)S(1)} %fusion.42), channel_id=1, source_target_pairs={{0,8},{4,12},{8,0},{12,4},{1,9},{5,13},{9,1},{13,5},{2,10},{6,14},... | collective-permute-start | bytes 98312 | tf_op jit(solution)/shard_map/ppermute | solution.py:32
  297.2 9.0 %collective-permute-start.26 = (f32[64,128]{1,0:T(8,128)S(1)}, f32[64,128]{1,0:T(8,128)S(1)}, u32[]{:S(2)}, u32[]{:S(2)}) collective-permute-start(f32[64,128]{1,0:T(8,128)S(1)} %fusion.42), channel_id=1, source_target_pairs={{0,4},{4,0},{8,12},{12,8},{1,5},{5,1},{9,13},{13,9},{2,6},{6,2},{1... | collective-permute-start | bytes 98312 | tf_op jit(solution)/shard_map/ppermute | solution.py:32
  303.3 10.9 %collective-permute-start.31 = (bf16[192,768]{1,0:T(8,128)(2,1)}, bf16[192,768]{1,0:T(8,128)(2,1)}, u32[]{:S(2)}, u32[]{:S(2)}) collective-permute-start(bf16[192,768]{1,0:T(8,128)(2,1)} %get-tuple-element.162), channel_id=1, source_target_pairs={{0,12},{4,8},{8,4},{12,0},{1,13},{5,9},{9,5},{13,1},{2,14},{6,10},... | collective-permute-start | bytes 884744 | tf_op jit(solution)/shard_map/ppermute | solution.py:32
  306.2 13.1 %collective-permute-start.30 = (bf16[192,768]{1,0:T(8,128)(2,1)S(1)}, bf16[192,768]{1,0:T(8,128)(2,1)}, u32[]{:S(2)}, u32[]{:S(2)}) collective-permute-start(bf16[192,768]{1,0:T(8,128)(2,1)S(1)} %get-tuple-element.163), channel_id=1, source_target_pairs={{0,8},{4,12},{8,0},{12,4},{1,9},{5,13},{9,1},{13,5},{2,10},{6,14},... | collective-permute-start | bytes 884744 | tf_op jit(solution)/shard_map/ppermute | solution.py:32
  309.9 17.6 %collective-permute-start.22 = (bf16[192,1152]{1,0:T(8,128)(2,1)}, bf16[192,1152]{1,0:T(8,128)(2,1)S(1)}, u32[]{:S(2)}, u32[]{:S(2)}) collective-permute-start(bf16[192,1152]{1,0:T(8,128)(2,1)} %get-tuple-element.155), channel_id=1, source_target_pairs={{0,4},{4,0},{8,12},{12,8},{1,5},{5,1},{9,13},{13,9},{2,6},{6,2},{1... | collective-permute-start | bytes 1327112 | tf_op jit(solution)/shard_map/ppermute | solution.py:32
  310.7 23.4 %collective-permute-start.24 = (bf16[192,1152]{1,0:T(8,128)(2,1)}, bf16[192,1152]{1,0:T(8,128)(2,1)S(1)}, u32[]{:S(2)}, u32[]{:S(2)}) collective-permute-start(bf16[192,1152]{1,0:T(8,128)(2,1)} %get-tuple-element.156), channel_id=1, source_target_pairs={{0,12},{4,8},{8,4},{12,0},{1,13},{5,9},{9,5},{13,1},{2,14},{6,10},... | collective-permute-start | bytes 1327112 | tf_op jit(solution)/shard_map/ppermute | solution.py:32
  314.0 26.4 %collective-permute-start.23 = (bf16[192,1152]{1,0:T(8,128)(2,1)}, bf16[192,1152]{1,0:T(8,128)(2,1)S(1)}, u32[]{:S(2)}, u32[]{:S(2)}) collective-permute-start(bf16[192,1152]{1,0:T(8,128)(2,1)} %get-tuple-element.157), channel_id=1, source_target_pairs={{0,8},{4,12},{8,0},{12,4},{1,9},{5,13},{9,1},{13,5},{2,10},{6,14},... | collective-permute-start | bytes 1327112 | tf_op jit(solution)/shard_map/ppermute | solution.py:32
  314.2 33.9 %collective-permute-start.32 = (bf16[96,1536]{1,0:T(8,128)(2,1)}, bf16[96,1536]{1,0:T(8,128)(2,1)}, u32[]{:S(2)}, u32[]{:S(2)}) collective-permute-start(bf16[96,1536]{1,0:T(8,128)(2,1)} %get-tuple-element.158), channel_id=1, source_target_pairs={{0,4},{4,0},{8,12},{12,8},{1,5},{5,1},{9,13},{13,9},{2,6},{6,2},{1... | collective-permute-start | bytes 884744 | tf_op jit(solution)/shard_map/ppermute | solution.py:32
  319.3 28.7 %collective-permute-start.34 = (bf16[96,1536]{1,0:T(8,128)(2,1)}, bf16[96,1536]{1,0:T(8,128)(2,1)}, u32[]{:S(2)}, u32[]{:S(2)}) collective-permute-start(bf16[96,1536]{1,0:T(8,128)(2,1)} %get-tuple-element.159), channel_id=1, source_target_pairs={{0,12},{4,8},{8,4},{12,0},{1,13},{5,9},{9,5},{13,1},{2,14},{6,10},... | collective-permute-start | bytes 884744 | tf_op jit(solution)/shard_map/ppermute | solution.py:32
  323.9 20.6 %all-to-all-start.2 = ((bf16[4,48,768]{2,1,0:T(8,128)(2,1)}), bf16[4,48,768]{2,1,0:T(8,128)(2,1)S(1)}, u32[]{:S(2)}, u32[]{:S(2)}) async-start(bf16[4,48,768]{2,1,0:T(8,128)(2,1)} %bitcast.50), calls=%async_computation.4 | async-start | bytes 589824 | tf_op jit(solution)/shard_map/all_to_all | solution.py:773
  327.4 23.4 %collective-permute-start.33 = (bf16[96,1536]{1,0:T(8,128)(2,1)}, bf16[96,1536]{1,0:T(8,128)(2,1)}, u32[]{:S(2)}, u32[]{:S(2)}) collective-permute-start(bf16[96,1536]{1,0:T(8,128)(2,1)} %get-tuple-element.160), channel_id=1, source_target_pairs={{0,8},{4,12},{8,0},{12,4},{1,9},{5,13},{9,1},{13,5},{2,10},{6,14},... | collective-permute-start | bytes 884744 | tf_op jit(solution)/shard_map/ppermute | solution.py:32
  344.5 38.8 %all-to-all-start.1 = ((bf16[4,64,1152]{2,1,0:T(8,128)(2,1)}), bf16[4,64,1152]{2,1,0:T(8,128)(2,1)S(1)}, u32[]{:S(2)}, u32[]{:S(2)}) async-start(bf16[4,64,1152]{2,1,0:T(8,128)(2,1)} %pad_maximum_fusion.4), calls=%async_computation.2 | async-start | bytes 1179648 | tf_op jit(solution)/shard_map/all_to_all | solution.py:795
  352.2 28.0 %collective-permute-start.35 = (bf16[96,1536]{1,0:T(8,128)(2,1)S(1)}, bf16[96,1536]{1,0:T(8,128)(2,1)S(1)}, u32[]{:S(2)}, u32[]{:S(2)}) collective-permute-start(bf16[96,1536]{1,0:T(8,128)(2,1)S(1)} %fusion.23), channel_id=1, source_target_pairs={{0,0},{4,1},{8,2},{12,3},{16,4},{20,5},{24,6},{28,7},{1,8},{5,9},{... | collective-permute-start | bytes 884744 | tf_op jit(solution)/shard_map/ppermute | solution.py:772
  (38 other events, 231.8 us)
Sparse Core Ops, SparseCore 0:
  40.6 65.8 all-gather.4
  108.0 62.3 all-gather.6
  180.6 61.3 reduce-scatter.2
  279.0 64.7 reduce-scatter.4

commit v3 on v2

--- a/solution.py
+++ b/solution.py
@@ -52,14 +52,11 @@
     return lax.dot_general(a, b, (((0,), (0,)), ((), ())), preferred_element_type=F4)
 
 
-def spread(v, e):
-    return mm_tn(v.astype(BF), e)
-
-
-def spread_fine(v, e):
+def grown(lead_last, e):
+    v = lead_last[:, :8]
     hi = v.astype(BF)
     lo = (v - hi.astype(F4)).astype(BF)
-    return mm_tn(hi, e) + mm_tn(lo, e)
+    return (mm_tn(hi, e[:HP, :]) + mm_tn(lo, e[:HP, :]))[0:1, :]
 
 
 def gather_heads(w, e):
@@ -70,6 +67,10 @@
     hi = w.astype(BF)
     lo = (w - hi.astype(F4)).astype(BF)
     return mm_nt(e, hi) + mm_nt(e, lo)
+
+
+def turn(v):
+    return jnp.transpose(v.astype(F4)).astype(BF)
 
 
 def sigmoid(v):
@@ -97,8 +98,19 @@
     return jnp.transpose(jnp.concatenate([mt, jnp.zeros((QC - 8, QC), F4)], axis=0))
 
 
-def tiles(count):
-    return [slice(j * 128, j * 128 + 128) for j in range(count)]
+def full(col):
+    return jnp.broadcast_to(col, (QC, 128))
+
+
+def tiles(count, width=128):
+    return [slice(j * width, j * width + width) for j in range(count)]
+
+
+WIDE = 256
+
+
+def stacked(v, halves):
+    return jnp.concatenate([v * halves[0], v * halves[1]], axis=0)
 
 
 def col_of(row):
@@ -136,42 +148,47 @@
     return jnp.concatenate([low, high], axis=0)
 
 
-def sums_gather(mine, cuts):
-    rows = mine.shape[0]
-    if lax.axis_size("hh") > 1 or rows % 16:
-        whole = lax.all_gather(mine, SUMS, axis=0, tiled=True)
+def plain():
+    return lax.axis_size("hh") == 1
+
+
+def near_rows(mine):
+    if not plain() or mine.shape[0] % 16:
+        return [mine]
+    return [mine] + [swap(mine, "ctx", k) for k in range(1, lax.axis_size("ctx"))]
+
+
+def all_rows(pieces, cuts):
+    if len(pieces) == 1:
+        whole = lax.all_gather(pieces[0], SUMS, axis=0, tiled=True)
         return [whole[:, a:b] for a, b in cuts]
-    place = lax.axis_index("ctx").astype(jnp.int32).reshape(1)
-    others = [swap(mine, "ctx", k) for k in range(1, lax.axis_size("ctx"))]
-    stack = placed(place, [mine, *others])
+    stack = placed(lax.axis_index("ctx").astype(jnp.int32).reshape(1), pieces)
     got = swap(stack, "dp", 1)
     side = lax.axis_index("dp")
     return [joined(stack[:, a:b], got[:, a:b], side) for a, b in cuts]
 
 
-def team_halves(total):
-    if lax.axis_size("hh") > 1:
-        return total
-    parts = total.reshape(2, -1, total.shape[1])
-    dp = lax.axis_index("dp")
-    give = lax.dynamic_index_in_dim(parts, 1 - dp, 0, keepdims=False)
-    keep = lax.dynamic_index_in_dim(parts, dp, 0, keepdims=False)
-    return (keep.astype(F4) + swap(give, "dp", 1).astype(F4)).astype(BF)
-
-
-def chain_sum(cur):
-    if lax.axis_size("hh") > 1:
-        return lax.psum_scatter(cur, SUMS, scatter_dimension=0, tiled=True).astype(BF)
+def half_of(v, side):
+    return lax.dynamic_slice_in_dim(v, side * (v.shape[1] // 2), v.shape[1] // 2, axis=1)
+
+
+def chain_pieces(keep, got):
     count = lax.axis_size("ctx")
-    parts = cur.reshape(count, -1, cur.shape[1])
     ctx = lax.axis_index("ctx")
-
-    def piece(k):
-        return lax.dynamic_index_in_dim(parts, jnp.bitwise_xor(ctx, k), 0, keepdims=False)
-
-    out = piece(0).astype(F4)
-    for k in range(1, count):
-        out = out + swap(piece(k), "ctx", k).astype(F4)
+    keep = keep.reshape(count, -1, keep.shape[-1])
+    got = got.reshape(keep.shape)
+    pieces = []
+    for k in range(count):
+        at = jnp.bitwise_xor(ctx, k)
+        parts = [lax.dynamic_index_in_dim(v, at, 0, keepdims=False) for v in (keep, got)]
+        pieces.append((parts[0].astype(F4) + parts[1].astype(F4)).astype(BF))
+    return pieces
+
+
+def chain_sum(pieces):
+    out = pieces[0].astype(F4)
+    for k in range(1, len(pieces)):
+        out = out + swap(pieces[k], "ctx", k).astype(F4)
     return out.astype(BF)
 
 
@@ -236,12 +253,13 @@
         sc_o[s, HP:, :] = dt
         tail0, lead_last = decays(cum, meta[s])
         dec[s] = dec[s] * lead_last
-        tails.append((tail0 * dt).astype(BF))
-        lasts.append(lead_last[:, :8])
+        tails.append(cols_of(tail0 * dt).astype(BF))
+        lasts.append(grown(lead_last, e))
     order = tiles(CW // 128)
     n_x = XW // 128
     for s in every:
         turned = lines_of(meta[s])
+        masks = [full(turned[:, 3 + k : 4 + k]) for k in range(3)]
         for j in [*range(n_x, len(order)), *range(n_x)]:
             c = order[j]
             if j < n_x:
@@ -252,18 +270,23 @@
             mixed = taps[4:5, c] + taps[3:4, c] * own
             for k in range(3):
                 mixed = mixed + taps[k : k + 1, c] * (
-                    buf[s, 5 + k : 5 + k + QC, c] * turned[:, 3 + k : 4 + k]
+                    buf[s, 5 + k : 5 + k + QC, c] * masks[k]
                 )
             sig = sigmoid(mixed)
             act = (mixed * sig).astype(BF)
             sl_o[rows[s], c] = (sig + mixed * sig * (1.0 - sig)).astype(BF)
             if j < n_x:
                 x_o[rows[s], c] = act
-                xw = (act.astype(F4) * spread(tails[s], e[:, c])).astype(BF)
-                grow = spread_fine(lasts[s], e[:, c])[0:1, :]
-                st[s, :, c] = st[s, :, c] * grow + mm_tn(bc_o[rows[s], :N], xw)
+                if j % 2:
+                    c2 = slice(j * 128 - 128, j * 128 + 128)
+                    pair = jnp.concatenate([held, act], axis=1).astype(F4)
+                    xw = (pair * mm(tails[s], e[:, c2])).astype(BF)
+                    st[s, :, c2] = st[s, :, c2] * lasts[s][:, c2] + mm(b_t, xw)
+                held = act
             else:
                 bc_o[rows[s], j * 128 - XW : j * 128 - XW + 128] = act
+                if j == n_x:
+                    b_t = turn(act)
     st_o[...] = st[...].astype(BF)
     dec_o[...] = dec[...]
 
@@ -283,7 +306,7 @@
             ahead3(seqs, 8, 128),
             fixed(8, CW),
             fixed(2, HP, 128),
-            fixed(HP, XW),
+            fixed(128, XW),
         ],
         out_specs=[
             ahead(span, XW),
@@ -323,7 +346,7 @@
     return (col_of(mt[0:1, :]) == mt[0:1, :]) & (r >= q)
 
 
-def scan_kernel(x_r, bc, sc, meta, s_in, z_r, skip, e, y_o, ent_o, sum_o, st):
+def scan_kernel(x_r, bc, sc, meta, s_in, z_r, skip, gain, e, y_o, sg_o, ent_o, sum_o, st):
     i = pl.program_id(0)
     seqs = s_in.shape[0]
     every = range(seqs)
@@ -338,37 +361,43 @@
         mt = meta[s]
         cum, dt = sc[s, 0:HP, :], sc[s, HP:, :]
         b, c = bc[rows[s], :N], bc[rows[s], N:]
-        lead = (jnp.exp(cum) * (mt[0:1, :] == mt[1:2, :]).astype(F4)).astype(BF)
+        lead = cols_of(jnp.exp(cum) * (mt[0:1, :] == mt[1:2, :]).astype(F4)).astype(BF)
         tail0, lead_last = decays(cum, mt)
-        tail = (tail0 * dt).astype(BF)
+        tail = cols_of(tail0 * dt).astype(BF)
+        b_t = turn(b)
         scores = mm_nt(c, b)
         inside = inside_of(mt)
         cum_cols = cols_of(cum)
         squares = jnp.zeros((QC, 128), F4)
-        for j, at in enumerate(tiles(XW // 128)):
+        grow = grown(lead_last, e)
+        for j, at in enumerate(tiles(XW // WIDE, WIDE)):
             ej = e[:, at]
-            xp = x_r[rows[s], at]
-            xf = xp.astype(F4)
+            xf = x_r[rows[s], at].astype(F4)
             now = st[s, :, at]
             before = now.astype(BF)
             ent_o[s, :, at] = before
-            y = spread(lead, ej) * mm(c, before) + skip[:, at] * xf
-            xw = (xf * spread(tail, ej)).astype(BF)
-            st[s, :, at] = now * spread_fine(lead_last[:, :8], ej)[0:1, :] + mm_tn(b, xw)
-            for half in range(2):
-                h = 2 * j + half
-                gap = jnp.where(inside, cum_cols[:, h : h + 1] - sc[s, h : h + 1, :], NEG)
-                w = (scores * jnp.exp(gap) * sc[s, HP + h : HP + h + 1, :]).astype(BF)
-                y = y + mm(w, xp * halves[half])
-            low = y.astype(BF)
-            y_o[rows[s], at] = low
-            z = z_r[rows[s], at]
-            v = low.astype(F4) * z * sigmoid(z)
-            squares = squares + v * v
+            wide = mm(lead, ej) * mm(c, before) + skip[:, at] * xf
+            xw = (xf * mm(tail, ej)).astype(BF)
+            st[s, :, at] = now * grow[:, at] + mm(b_t, xw)
+            for k in range(WIDE // 128):
+                here = slice(j * WIDE + k * 128, j * WIDE + k * 128 + 128)
+                xp = x_r[rows[s], here]
+                ws = []
+                for half in range(2):
+                    h = (j * WIDE + k * 128) // PS + half
+                    gap = jnp.where(inside, cum_cols[:, h : h + 1] - sc[s, h : h + 1, :], NEG)
+                    ws.append((scores * jnp.exp(gap) * sc[s, HP + h : HP + h + 1, :]).astype(BF))
+                y = wide[:, k * 128 : k * 128 + 128] + mm(jnp.concatenate(ws, axis=1), stacked(xp, halves))
+                low = y.astype(BF)
+                y_o[rows[s], here] = low
+                z = z_r[rows[s], here]
+                v = low.astype(F4) * z * sigmoid(z)
+                squares = squares + v * v
+                sg_o[rows[s], here] = (v * gain[:, here]).astype(BF)
         sum_o[s] = jnp.sum(jnp.transpose(squares), axis=0, keepdims=True)
 
 
-def scan(seqs, x, bc, sc, meta, s_in, z, skip, e):
+def scan(seqs, x, bc, sc, meta, s_in, z, skip, gain, e):
     length = x.shape[0]
     span = seqs * QC
     chunks = length // QC
@@ -384,15 +413,21 @@
             fixed(seqs, N, XW),
             ahead(span, XW),
             fixed(1, XW),
-            fixed(HP, XW),
-        ],
-        out_specs=[ahead(span, XW), ahead3(seqs, N, XW), ahead3(seqs, 1, QC)],
-        out_shape=[sd((length, XW), BF), sd((chunks, N, XW), BF), sd((chunks, 1, QC), F4)],
+            fixed(1, XW),
+            fixed(128, XW),
+        ],
+        out_specs=[ahead(span, XW), ahead(span, XW), ahead3(seqs, N, XW), ahead3(seqs, 1, QC)],
+        out_shape=[
+            sd((length, XW), BF),
+            sd((length, XW), BF),
+            sd((chunks, N, XW), BF),
+            sd((chunks, 1, QC), F4),
+        ],
         scratch_shapes=[pltpu.VMEM((seqs, N, XW), F4)],
         compiler_params=pltpu.CompilerParams(vmem_limit_bytes=LIMIT),
         cost_estimate=work(length, 1),
         name="scan_gate",
-    )(x, bc, sc, meta, s_in, z, skip, e)
+    )(x, bc, sc, meta, s_in, z, skip, gain, e)
 
 
 def gate_kernel(y_r, z_r, dg_r, sq, al, bc, sc, meta, gain, e, dy_o, dz_o, gg_o, ds_o, ds, gg):
@@ -411,11 +446,14 @@
         cum = sc[s, 0:HP, :]
         c = bc[rows[s], N:]
         scale = lax.rsqrt(sq[s] * (1.0 / DI) + EPS)
-        rstd = col_of(scale)
+        rstd = jnp.concatenate([col_of(scale)] * (WIDE // 128), axis=1)
         pull = col_of(al[s] * (scale * scale * scale) * (1.0 / DI))
-        lead = (jnp.exp(cum) * (mt[0:1, :] == mt[1:2, :]).astype(F4)).astype(BF)
+        pull = jnp.concatenate([pull] * (WIDE // 128), axis=1)
+        lead = cols_of(jnp.exp(cum) * (mt[0:1, :] == mt[1:2, :]).astype(F4)).astype(BF)
         _, lead_last = decays(cum, mt)
-        for at in tiles(XW // 128):
+        c_t = turn(c)
+        grow = grown(lead_last, e)
+        for at in tiles(XW // WIDE, WIDE):
             ej = e[:, at]
             y = y_r[rows[s], at].astype(F4)
             z = z_r[rows[s], at]
@@ -428,9 +466,8 @@
             dy = (d_v * act).astype(BF)
             dy_o[rows[s], at] = dy
             dz_o[rows[s], at] = (d_v * y * (sig + act * (1.0 - sig))).astype(BF)
-            led = (dy.astype(F4) * spread(lead, ej)).astype(BF)
-            grow = spread_fine(lead_last[:, :8], ej)[0:1, :]
-            ds[s, :, at] = ds[s, :, at] * grow + mm_tn(c, led)
+            led = (dy.astype(F4) * mm(lead, ej)).astype(BF)
+            ds[s, :, at] = ds[s, :, at] * grow[:, at] + mm(c_t, led)
     ds_o[...] = ds[...].astype(BF)
     gg_o[...] = gg[...]
 
@@ -455,7 +492,7 @@
             behind3(n, seqs, 2 * HP, 128),
             behind3(n, seqs, 8, 128),
             fixed(1, XW),
-            fixed(HP, XW),
+            fixed(128, XW),
         ],
         out_specs=[wide, wide, fixed(8, XW), fixed(seqs, N, XW)],
         out_shape=[
@@ -497,9 +534,11 @@
     edge = lax.broadcasted_iota(jnp.int32, (8, 128), 0)
     place = lax.broadcasted_iota(jnp.int32, (HP, QC), 1)
 
+    near_of = {}
+
     def conv_back(s, c, own, d_act, turned):
         dm = d_act * sl[rows[s], c].astype(F4)
-        near = turned[:, 5:6]
+        near = near_of[s]
         shifted = [dm]
         for k in range(3):
             ready = shifted[-1] * near
@@ -526,11 +565,13 @@
     for s in every:
         mt = meta[s]
         turned = lines_of(mt)
+        near_of[s] = full(turned[:, 5:6])
         cum, dt = sc[s, 0:HP, :], sc[s, HP:, :]
         b, c = bc[rows[s], :N], bc[rows[s], N:]
-        lead = (jnp.exp(cum) * (mt[0:1, :] == mt[1:2, :]).astype(F4)).astype(BF)
+        lead = cols_of(jnp.exp(cum) * (mt[0:1, :] == mt[1:2, :]).astype(F4)).astype(BF)
         tail0, lead_last = decays(cum, mt)
-        tail = (tail0 * dt).astype(BF)
+        tail = cols_of(tail0 * dt).astype(BF)
+        c_t = turn(c)
         scores = mm_nt(c, b)
         inside = inside_of(mt)
         cum_cols = cols_of(cum)
@@ -540,47 +581,56 @@
         lv = jnp.zeros((HP, QC), F4)
         d_b = jnp.zeros((QC, N), F4)
         d_c = jnp.zeros((QC, N), F4)
-        for j, at in enumerate(tiles(XW // 128)):
+        grow = grown(lead_last, e)
+        for j, at in enumerate(tiles(XW // WIDE, WIDE)):
             ej = e[:, at]
-            xp = x_r[rows[s], at]
-            dyp = dy_r[rows[s], at]
-            xf = xp.astype(F4)
-            dyf = dyp.astype(F4)
+            xf = x_r[rows[s], at].astype(F4)
+            dyf = dy_r[rows[s], at].astype(F4)
             before = ent[s, :, at]
             now = ds[s, :, at]
             after = now.astype(BF)
-            tailj = spread(tail, ej)
+            tailj = mm(tail, ej)
             u = tailj * mm(b, after)
-            led = dyf * spread(lead, ej)
-            tq = tq + gather_heads(xf * u, ej)
-            lv = lv + gather_heads(led * mm(c, before), ej)
+            led = dyf * mm(lead, ej)
             ledb = led.astype(BF)
+            both = jnp.concatenate([xf * u, led * mm(c, before)], axis=0)
+            got = gather_heads(both, ej[:HP])
+            tq = tq + got[:, :QC]
+            lv = lv + got[:, QC:]
             d_b = d_b + mm_nt((xf * tailj).astype(BF), after)
             d_c = d_c + mm_nt(ledb, before)
             colbuf[s, 0:1, at] = jnp.sum(now * before.astype(F4), axis=0, keepdims=True)
             colbuf[s, 1:2, at] = jnp.sum(dyf * xf, axis=0, keepdims=True)
-            ds[s, :, at] = now * spread_fine(lead_last[:, :8], ej)[0:1, :] + mm_tn(c, ledb)
-            dx = u + skip[:, at] * dyf
-            for half in range(2):
-                h = 2 * j + half
-                gap = jnp.where(inside, cum_cols[:, h : h + 1] - sc[s, h : h + 1, :], NEG)
-                dec = jnp.exp(gap)
-                dtr = sc[s, HP + h : HP + h + 1, :]
-                sl_h = scores * dec
-                d_m = mm_nt(dyp, xp * halves[half])
-                g = d_m * sl_h
-                rowbuf[s, h : h + 1, :] = jnp.sum(g, axis=0, keepdims=True)
-                sums = jnp.where(lane == h, jnp.sum(g * dtr, axis=1, keepdims=True), sums)
-                d_sc = d_sc + d_m * (dec * dtr)
-                dx = dx + mm_tn((sl_h * dtr).astype(BF), dyp * halves[half])
-            conv_back(s, at, xr[rows[s], at].astype(F4), dx.astype(BF).astype(F4), turned)
+            ds[s, :, at] = now * grow[:, at] + mm(c_t, ledb)
+            wide = u + skip[:, at] * dyf
+            for k in range(WIDE // 128):
+                here = slice(j * WIDE + k * 128, j * WIDE + k * 128 + 128)
+                dyp = dy_r[rows[s], here]
+                d_ms = mm_nt(dyp, stacked(x_r[rows[s], here], halves))
+                ws = []
+                for half in range(2):
+                    h = (j * WIDE + k * 128) // PS + half
+                    gap = jnp.where(inside, cum_cols[:, h : h + 1] - sc[s, h : h + 1, :], NEG)
+                    dec = jnp.exp(gap)
+                    dtr = sc[s, HP + h : HP + h + 1, :]
+                    sl_h = scores * dec
+                    d_m = d_ms[:, half * QC : half * QC + QC]
+                    g = d_m * sl_h
+                    rowbuf[s, h : h + 1, :] = jnp.sum(g, axis=0, keepdims=True)
+                    sums = jnp.where(lane == h, jnp.sum(g * dtr, axis=1, keepdims=True), sums)
+                    d_sc = d_sc + d_m * (dec * dtr)
+                    ws.append((sl_h * dtr).astype(BF))
+                dx = wide[:, k * 128 : k * 128 + 128] + mm_tn(
+                    jnp.concatenate(ws, axis=0), stacked(dyp, halves)
+                )
+                conv_back(s, here, xr[rows[s], here].astype(F4), dx.astype(BF).astype(F4), turned)
         d_scb = d_sc.astype(BF)
         d_b = d_b + mm_tn(d_scb, c)
         d_c = d_c + mm(d_scb, b)
         conv_back(s, slice(XW, XW + N), br[rows[s], :N].astype(F4), d_b, turned)
         conv_back(s, slice(XW + N, CW), br[rows[s], N:].astype(F4), d_c, turned)
         ecol = rowbuf[s]
-        both = gather_fine(colbuf[s], e[...])
+        both = gather_fine(colbuf[s], e[:HP, :])
         at_end = jnp.sum(tq, axis=1, keepdims=True) + lead_last * both[:, 0:1]
         d_cum = jnp.transpose(sums)[:HP] - dt * ecol - tq + lv
         d_la = running(d_cum + jnp.where(place == QC - 1, at_end, 0.0), True)
@@ -618,7 +668,7 @@
             fixed(8, CW),
             fixed(2, HP, 128),
             fixed(1, XW),
-            fixed(HP, XW),
+            fixed(128, XW),
         ],
         out_specs=[behind(n, span, AW), fixed(seqs, 8, CW), fixed(8, CW), fixed(3, HP, 128)],
         out_shape=[
@@ -639,6 +689,54 @@
         cost_estimate=work(length, 2),
         name="scan_back",
     )(x, bc, sl, sc, meta, ent, dy, d_end, raw, raw, raw, halo, taps, hp, skip, e)
+
+
+def last_kernel(x_r, xbc_o, dt_o, taps_o, bias_o, gate_o, norm_o, h0_o, h1_o, h2_o):
+    own = xbc_o.shape[0]
+    r = lax.broadcasted_iota(jnp.int32, (128, 128), 0)
+    c = lax.broadcasted_iota(jnp.int32, (128, 128), 1)
+    bc = jnp.zeros((own, 2 * N), F4)
+    dt = jnp.zeros((own, 128), F4)
+    shared = jnp.zeros((8, AW), F4)
+    heads = [jnp.zeros((16, 128), F4) for _ in range(3)]
+    for g in range(GROUP):
+        at = slice(g * XW, g * XW + XW)
+        xbc_o[:, at] = x_r[g, :own, :XW].astype(F4)
+        bc = bc + x_r[g, :own, XW:CW].astype(F4)
+        move = ((c == r + HG * g) & (r < HG)).astype(BF)
+        dt = dt + mm(x_r[g, :own, CW:], move)
+        tail = x_r[g, own:, :].astype(F4)
+        both = tail[:8] + tail[8:]
+        taps_o[:, at] = both[:4, :XW]
+        bias_o[:, at] = both[4:5, :XW]
+        gate_o[:, at] = both[5:6, :XW]
+        shared = shared + both
+        for p in range(3):
+            move = ((c - HG * g == r - HP * p) & (r >= HP * p) & (r < HP * p + HG)).astype(BF)
+            heads[p] = heads[p] + mm(tail[:, XW : XW + 128].astype(BF), move)
+    xbc_o[:, DI:] = bc
+    dt_o[...] = dt[:, :H]
+    taps_o[:, DI:] = shared[:4, XW:CW]
+    bias_o[:, DI:] = shared[4:5, XW:CW]
+    norm_o[:, :AW] = shared[6:7, :]
+    norm_o[:, AW:] = shared[7:8, : norm_o.shape[1] - AW]
+    for p, ref in enumerate((h0_o, h1_o, h2_o)):
+        ref[...] = heads[p][5:6, :H] + heads[p][13:14, :H]
+
+
+def last_outputs(x_all, own, width):
+    sd = jax.ShapeDtypeStruct
+    vm = pl.BlockSpec(memory_space=pltpu.VMEM)
+    shapes = [(own, DI + 2 * N), (own, H), (4, DI + 2 * N), (1, DI + 2 * N), (1, DI), (1, width)]
+    shapes.extend([(1, H)] * 3)
+    return pl.pallas_call(
+        last_kernel,
+        out_shape=[sd(shape, F4) for shape in shapes],
+        in_specs=[vm],
+        out_specs=[vm] * len(shapes),
+        compiler_params=pltpu.CompilerParams(vmem_limit_bytes=LIMIT),
+        name="last_outputs",
+    )(x_all)
 
 
 def pad_lanes(v, width):
@@ -684,8 +782,9 @@
     in_mine, wo_mine, tokens_now = lax.optimization_barrier((in_mine, wo_mine, tokens_in))
     tokens = collected(tokens_now)
     cot = collected(out_cotangent)
-    wx, wz = sums_gather(in_mine, [(0, AW), (AW, AW + XW)])
-    [wo] = sums_gather(wo_mine, [(0, width)])
+    wx, wz = all_rows(near_rows(in_mine), [(0, AW), (AW, AW + XW)])
+    wx, wz, wo_mine = lax.optimization_barrier((wx, wz, wo_mine))
+    wo_near = near_rows(wo_mine)
 
     def mine(v, size):
         return lax.dynamic_slice_in_dim(v, hl * size, size, axis=-1)
@@ -697,7 +796,7 @@
     hp = jnp.broadcast_to(jnp.pad(hp, ((0, 0), (0, HP - HG)))[:, :, None], (2, HP, 128))
     skip = jnp.repeat(mine(d_skip, HG), PS)[None]
     gain = mine(gate_norm, XW)[None]
-    e = (jnp.arange(HP)[:, None] == jnp.arange(XW)[None, :] // PS).astype(BF)
+    e = (jnp.arange(128)[:, None] == jnp.arange(XW)[None, :] // PS).astype(BF)
 
     start = lax.axis_index(CHAIN) * block
     seg_pad = jnp.concatenate([jnp.full((seqs, 8), -1, jnp.int32), seg_ids], axis=1)
@@ -711,18 +810,22 @@
     meta = jnp.stack(lines, axis=2).astype(F4)
     meta = meta.transpose(1, 0, 2, 3).reshape(GROUP * seqs, 8, QC)
 
-    tokens, wx, wz, wo, meta, taps, hp, skip, gain, e = lax.optimization_barrier(
-        (tokens, wx, wz, wo, meta, taps, hp, skip, gain, e)
+    tokens, wx, wz, meta, taps, hp, skip, gain, e = lax.optimization_barrier(
+        (tokens, wx, wz, meta, taps, hp, skip, gain, e)
     )
     normed = norm_rows(tokens.astype(F4), in_norm).astype(BF)
     raw = mm(normed, wx).astype(BF)
+    raw, *wo_near = lax.optimization_barrier((raw, *wo_near))
+    [wo] = all_rows(wo_near, [(0, width)])
     last = raw.reshape(GROUP, seqs, rows, AW)[GROUP - 1, :, rows - 8 :, :CW]
     halo = shift(last, CHAIN, 1)
     x, bc, sl, sc, state, decay = front(seqs, raw, halo, meta, taps, hp, e)
     decay_row = jnp.repeat(decay[:, :HG, 0], PS, axis=-1)[:, None]
+    state, z_normed = lax.optimization_barrier((state, normed))
     s_in = carried(state, decay_row, hops, 1)
-    gates = mm(normed, wz)
-    y, ent, squares = scan(seqs, x, bc, sc, meta, s_in, gates, skip, e)
+    gates = mm(z_normed, wz)
+    s_in, wo = lax.optimization_barrier((s_in, wo))
+    y, sg, ent, squares = scan(seqs, x, bc, sc, meta, s_in, gates, skip, gain, e)
 
     def team_sum(part):
         total = part
@@ -732,106 +835,141 @@
 
     def spread_sum(part):
         total = lax.psum_scatter(part, "hl", scatter_dimension=0, tiled=True)
-        return total.reshape(seqs, rows, width).astype(F4)
-
+        return total.reshape(seqs, rows, width)
+
+    out_rows = mm(sg, wo).astype(BF)
     squares = team_sum(squares)
-    scale = lax.rsqrt(squares.reshape(-1, 1) * (1.0 / DI) + EPS)
-    s_val = y.astype(F4) * jax.nn.silu(gates)
-    gated = (s_val * scale * gain).astype(BF)
-    out_rows = mm(gated, wo).astype(BF)
-    cot, out_rows = lax.optimization_barrier((cot, out_rows))
+    cot, out_rows, squares = lax.optimization_barrier((cot, out_rows, squares))
     d_gated = mm_nt(cot, wo)
-    along = team_sum(jnp.sum(d_gated * gain * s_val, axis=1).reshape(squares.shape))
+    row_scale = lax.rsqrt(squares * (1.0 / DI) + EPS)
+    gated = (sg.astype(F4) * row_scale.reshape(-1, 1)).astype(BF)
+    along = team_sum(jnp.sum(d_gated * sg.astype(F4), axis=1).reshape(squares.shape))
     out_sum = spread_sum(out_rows)
-    o_grad = mm_tn(gated, cot).astype(BF)
+    dp = lax.axis_index("dp")
+    if plain():
+        o_give, o_keep = (mm_tn(half_of(gated, at), cot).astype(BF) for at in (1 - dp, dp))
     dy, dz, gg, d_state = gate(seqs, y, gates, d_gated, squares, along, bc, sc, meta, gain, e)
     d_end = carried(d_state, decay_row, hops, -1)
-    z_grad = mm_tn(normed, dz).astype(BF)
-    from_z = mm_nt(dz, wz)
-    dy, o_grad, z_grad, from_z = lax.optimization_barrier((dy, o_grad, z_grad, from_z))
+    if plain():
+        n_give, n_keep = (half_of(normed, at) for at in (1 - dp, dp))
+        z_give, z_keep = (mm_tn(v, dz).astype(BF) for v in (n_give, n_keep))
+        dy, z_give, z_keep = lax.optimization_barrier((dy, z_give, z_keep))
+        z_got, o_got = swap(z_give, "dp", 1), swap(o_give, "dp", 1)
+        early = []
+        for z_part, o_part in zip(chain_pieces(z_keep, z_got), chain_pieces(o_keep, o_got)):
+            early.append(jnp.concatenate([z_part, o_part[:, : width // 2], o_part[:, width // 2 :]]))
+        dy, *early = lax.optimization_barrier((dy, *early))
+        early = chain_sum(early)
     draw, rim, conv_total, head_total = scan_back(
         seqs, x, bc, sl, sc, meta, ent, dy, d_end, raw, halo, taps, hp, skip, e
     )
     rim = shift(rim, CHAIN, -1)
-    o_half = team_halves(o_grad)
-    z_half = team_halves(z_grad)
-    rim, o_half, z_half, out_sum = lax.optimization_barrier((rim, o_half, z_half, out_sum))
-    for s in range(seqs):
-        at = ((GROUP - 1) * seqs + s) * rows + rows - 8
-        edge = draw[at : at + 8, :CW].astype(F4) + rim[s].astype(F4)
-        draw = lax.dynamic_update_slice(draw, edge.astype(BF), (at, 0))
-    d_low = (from_z + mm_nt(draw, wx)).astype(BF)
-    d_low, o_half, z_half, draw = lax.optimization_barrier((d_low, o_half, z_half, draw))
+    from_z = mm_nt(dz, wz).astype(BF)
+    if plain():
+        rim, from_z, out_sum, early = lax.optimization_barrier((rim, from_z, out_sum, early))
+    draw = draw.reshape(GROUP, seqs, rows, AW)
+    edge = draw[GROUP - 1 :, :, rows - 8 :, :CW].astype(F4) + rim.astype(F4)
+    draw = lax.dynamic_update_slice(draw, edge.astype(BF), (GROUP - 1, 0, rows - 8, 0))
+    draw = draw.reshape(GROUP * seqs * rows, AW)
+
+    def row_dots(grad, w):
+        return jnp.sum(grad.astype(F4) * w.astype(F4), axis=1)
+
+    if plain():
+        z_rows = GROUP * own_rows
+        o_rows = (early.shape[0] - z_rows) // 2
+        z_own = early[:z_rows].reshape(GROUP, own_rows, XW)
+        z_all = lax.all_to_all(z_own, "hl", 0, 0, tiled=True)
+        o_own = jnp.concatenate([early[z_rows : z_rows + o_rows], early[z_rows + o_rows :]], axis=1)
+        d_low = (from_z.astype(F4) + mm_nt(draw, wx)).astype(BF)
+        d_low, draw, z_all = lax.optimization_barrier((d_low, draw, z_all))
+        x_give = mm_tn(n_give, draw).astype(BF)
+        x_give, draw = lax.optimization_barrier((x_give, draw))
+        x_got = swap(x_give, "dp", 1)
+        x_keep = mm_tn(n_keep, draw).astype(BF)
+        x_pieces = chain_pieces(x_keep, x_got)
+        x_give, x_keep, *x_pieces = lax.optimization_barrier((x_give, x_keep, *x_pieces))
+        x_own = chain_sum(x_pieces)
+        norm_parts = []
+        for at, xg, zg in ((1 - dp, x_give, z_give), (dp, x_keep, z_keep)):
+            half = [lax.dynamic_slice_in_dim(w, at * (width // 2), width // 2) for w in (wx, wz)]
+            norm_parts.append(row_dots(xg, half[0]) + row_dots(zg, half[1]))
+        norm_total = joined(norm_parts[1], norm_parts[0], dp)
+    else:
+        grads = [mm_tn(normed, dz), mm_tn(gated, cot), mm_tn(normed, draw)]
+        grads = [g.astype(BF) for g in grads]
+        d_low = (from_z.astype(F4) + mm_nt(draw, wx)).astype(BF)
+        norm_total = row_dots(grads[0], wz) + row_dots(grads[2], wx)
+        z_own, o_own, x_own = (
+            lax.psum_scatter(g, SUMS, scatter_dimension=0, tiled=True) for g in grads
+        )
     d_sum = spread_sum(d_low)
-    x_grad = mm_tn(normed, draw).astype(BF)
-    norm_total = jnp.sum(x_grad.astype(F4) * wx.astype(F4), axis=1)
-    norm_total = norm_total + jnp.sum(z_grad.astype(F4) * wz.astype(F4), axis=1)
-    x_own = chain_sum(team_halves(x_grad)).reshape(GROUP, own_rows, AW)
-    z_own = chain_sum(z_half).reshape(GROUP, own_rows, XW)
-    o_own = chain_sum(o_half)
     out_proj_grad = lax.ppermute(o_own, EVERY, [(b, a) for a, b in pairs]).astype(F4)
-    z_all = lax.all_to_all(z_own, "hl", 0, 0, tiled=True)
-
-    pieces = [
-        conv_total[:5, :XW].reshape(-1),
-        gg[0],
-        jnp.sum(head_total, axis=2).reshape(-1),
-        conv_total[:5, XW:].reshape(-1),
-        norm_total / in_norm,
-    ]
-    sizes = [p.shape[0] for p in pieces]
-    pack = jnp.concatenate(pieces)
-    lines_n = -(-pack.shape[0] // 1024) * 8
-    total = lines_n * 128
-    pack = jnp.pad(pack, (0, total - pack.shape[0])).reshape(lines_n, 128)
+
+    heads = jnp.sum(head_total, axis=2).reshape(1, -1)
+    norm_rows_2 = jnp.pad(norm_total / in_norm, (0, 2 * AW - width)).reshape(2, AW)
+    pack = jnp.concatenate(
+        [
+            pad_lanes(conv_total[:5], AW),
+            pad_lanes(jnp.concatenate([gg[:1], heads], axis=1), AW),
+            norm_rows_2,
+        ],
+        axis=0,
+    )
     for axis in SUMS:
         pack = pack + sum(swap(pack, axis, k) for k in range(1, lax.axis_size(axis)))
     high = pack.astype(BF)
-    rest = (pack - high.astype(F4)).astype(BF)
-    extra = -(-2 * total // (AW * 16)) * 16
-    small = jnp.concatenate([high.reshape(-1), rest.reshape(-1)])
-    small = jnp.pad(small, (0, extra * AW - 2 * total)).reshape(1, extra, AW)
-    x_own = jnp.concatenate([x_own, jnp.broadcast_to(small, (GROUP, extra, AW))], axis=1)
+    small = jnp.concatenate([high, (pack - high.astype(F4)).astype(BF)], axis=0)
+    small = jnp.broadcast_to(small[None], (GROUP, 16, AW))
+    x_own = jnp.concatenate([x_own.reshape(GROUP, own_rows, AW), small], axis=1)
+    if not plain():
+        z_all = lax.all_to_all(z_own.reshape(GROUP, own_rows, XW), "hl", 0, 0, tiled=True)
     x_all = lax.all_to_all(x_own, "hl", 0, 0, tiled=True)
-    x_all, d_sum = lax.optimization_barrier((x_all, d_sum))
 
     u = tokens_in.astype(F4)
     scale = lax.rsqrt(jnp.mean(u * u, axis=-1, keepdims=True) + EPS)
     hat = u * scale
-    dh = d_sum * in_norm
-    d_u = scale * (dh - hat * jnp.mean(dh * hat, axis=-1, keepdims=True))
+    dh = d_sum.astype(F4) * in_norm
+    along = jnp.mean(dh * hat, axis=-1, keepdims=True)
+    x_all, along = lax.optimization_barrier((x_all, along))
+    d_u = scale * (dh - hat * along)
     tokens_grad = d_u + out_cotangent.astype(F4)
-    layer_out = (tokens_in.astype(F4) + out_sum).astype(BF)
+    own_scale = lax.dynamic_index_in_dim(row_scale.reshape(GROUP, seqs, rows, 1), hl, 0, keepdims=False)
+    layer_out = (tokens_in.astype(F4) + own_scale * out_sum.astype(F4)).astype(BF)
     z_proj_grad = z_all.transpose(1, 0, 2).reshape(own_rows, DI).astype(F4)
-    x_parts = x_all[:, :own_rows]
-    xs = x_parts[:, :, :XW].transpose(1, 0, 2).reshape(own_rows, DI).astype(F4)
-    bc_grad = jnp.sum(x_parts[:, :, XW:CW].astype(F4), axis=0)
-    xbc_proj_grad = jnp.concatenate([xs, bc_grad], axis=1)
-    dt_parts = x_parts[:, :, CW : CW + HG].transpose(1, 0, 2)
-    dt_proj_grad = dt_parts.reshape(own_rows, H).astype(F4)
-    got = x_all[:, own_rows:].astype(F4).reshape(GROUP, -1)
-    flat = got[:, :total] + got[:, total : 2 * total]
-    cuts = []
-    low = 0
-    for size in sizes:
-        cuts.append(flat[:, low : low + size])
-        low = low + size
-    conv_x = cuts[0].reshape(GROUP, 5, XW).transpose(1, 0, 2).reshape(5, DI)
-    conv_all = jnp.concatenate([conv_x, jnp.sum(cuts[3], axis=0).reshape(5, 2 * N)], axis=1)
-    per_head = cuts[2].reshape(GROUP, 3, HP)[:, :, :HG].transpose(1, 0, 2).reshape(3, H)
+    if plain():
+        outs = last_outputs(x_all, own_rows, width)
+        xbc_proj_grad, dt_proj_grad, taps_grad = outs[:3]
+        bias_grad, gate_grad, in_norm_grad = (v.reshape(-1) for v in outs[3:6])
+        per_head = [v.reshape(-1) for v in outs[6:]]
+    else:
+        x_parts = x_all[:, :own_rows]
+        xs = x_parts[:, :, :XW].transpose(1, 0, 2).reshape(own_rows, DI).astype(F4)
+        bc_grad = jnp.sum(x_parts[:, :, XW:CW].astype(F4), axis=0)
+        xbc_proj_grad = jnp.concatenate([xs, bc_grad], axis=1)
+        dt_parts = x_parts[:, :, CW : CW + HG].transpose(1, 0, 2)
+        dt_proj_grad = dt_parts.reshape(own_rows, H).astype(F4)
+        got = x_all[:, own_rows:, :AW].astype(F4)
+        got = got[:, :8] + got[:, 8:]
+        conv_x = got[:, :5, :XW].transpose(1, 0, 2).reshape(5, DI)
+        conv_all = jnp.concatenate([conv_x, jnp.sum(got[:, :5, XW:CW], axis=0)], axis=1)
+        per_head = got[:, 5, XW : XW + 3 * HP].reshape(GROUP, 3, HP)[:, :, :HG]
+        per_head = per_head.transpose(1, 0, 2).reshape(3, H)
+        in_norm_grad = jnp.sum(got[:, 6:8], axis=0).reshape(-1)[:width]
+        taps_grad, bias_grad, gate_grad = conv_all[:4], conv_all[4], got[:, 5, :XW].reshape(DI)
     return (
         layer_out,
         tokens_grad,
-        jnp.sum(cuts[4], axis=0),
+        in_norm_grad,
         z_proj_grad,
         xbc_proj_grad,
         dt_proj_grad,
-        conv_all[:4],
-        conv_all[4],
+        taps_grad,
+        bias_grad,
         per_head[0],
         per_head[1],
         per_head[2],
-        cuts[1].reshape(DI),
+        gate_grad,
         out_proj_grad,
     )
 

time: 411 us -> 362 us (0.88)
  the two profiles are of different devices: /device:TPU:6 before, /device:TPU:0 now
where the time goes in v3:
time: 362 us; the launch traced here: 356 us
  waiting for transfers between devices  129 us (36%)
  starting transfers between devices  69.7 us (19%)
  matrix products  48.8 us (13%)
  Pallas kernels  45.7 us (13%)
  other arithmetic  30.4 us (8%)
  local copies, waits for them, and re-layouts  16.6 us (5%)
  between operations  15.2 us (4%)
    ppermute x27, waiting for transfers between devices, swap(): return lax.ppermute(part, axis, [(i, i ^ k) for i in range(count)])  61 us
    ppermute x27, starting transfers between devices, swap(): return lax.ppermute(part, axis, [(i, i ^ k) for i in range(count)])  39.7 us
    reduce_scatter x2, waiting for transfers between devices, spread_sum(): total = lax.psum_scatter(part, 'hl', scatter_dimension=0, tiled=True)  24.3 us
    pallas_call x1, Pallas kernels, scan_back(): pl.pallas_call(back_kernel, grid=(n,), in_specs=[behind(n, span, XW), beh...  20.7 us
    all_to_all x1, waiting for transfers between devices, shards(): lax.all_to_all(jnp.concatenate(parts, axis=-1), 'hl', 0, 0, tiled=True)  19.9 us
    dot_general x3, matrix products, mm_nt(): lax.dot_general(a, b, (((1,), (1,)), ((), ())), preferred_element_type=F4)  19 us
    dot_general x6, matrix products, mm_tn(): lax.dot_general(a, b, (((0,), (0,)), ((), ())), preferred_element_type=F4)  17.2 us
    all_gather x2, waiting for transfers between devices, collected(): lax.all_gather(part, 'hl', axis=0).reshape(GROUP * seqs * rows, width)  14.9 us
  transfers between devices with their start and end apart: 40, of which 17 were waited for; matrix products, arithmetic and copies ran while one was open for 22% of the time, Pallas kernels for 13%

profile of v3, /device:TPU:0, one launch (start us, length us, event | category | flops | bytes accessed | tf_op | source)
XLA Modules:
  0.0 355.5 jit_solution(17183409033108690774)
XLA Ops:
  11.1 6.3 %all-to-all-start = ((bf16[4,48,1920]{2,1,0:T(8,128)(2,1)}), bf16[4,48,1920]{2,1,0:T(8,128)(2,1)S(1)}, u32[]{:S(2)}, u32[]{:S(2)}) async-start(bf16[4,48,1920]{2,1,0:T(8,128)(2,1)} %fusion.22), calls=%async_computation | async-start | bytes 1474560 | tf_op jit(solution)/shard_map/all_to_all | solution.py:778
  18.1 19.9 %all-to-all-done = bf16[4,48,1920]{2,1,0:T(8,128)(2,1)S(1)} async-done(((bf16[4,48,1920]{2,1,0:T(8,128)(2,1)}), bf16[4,48,1920]{2,1,0:T(8,128)(2,1)S(1)}, u32[]{:S(2)}, u32[]{:S(2)}) %all-to-all-start) | async-done | bytes 737312 | tf_op jit(solution)/shard_map/all_to_all | solution.py:778
  38.1 5.7 %collective-permute-start.3 = (bf16[192,1920]{1,0:T(8,128)(2,1)S(1)}, bf16[192,1920]{1,0:T(8,128)(2,1)S(1)}, u32[]{:S(2)}, u32[]{:S(2)}) collective-permute-start(bf16[192,1920]{1,0:T(8,128)(2,1)S(1)} %bitcast.121), channel_id=1, source_target_pairs={{0,12},{4,8},{8,4},{12,0},{1,13},{5,9},{9,5},{13,1},{2,14},{6,10},... | collective-permute-start | bytes 2211848 | tf_op jit(solution)/shard_map/ppermute | solution.py:32
  43.7 2.4 collective-permute-start.2
  47.6 13.5 %collective-permute-done.3.refs_3_ = bf16[192,1920]{1,0:T(8,128)(2,1)S(1)} collective-permute-done((bf16[192,1920]{1,0:T(8,128)(2,1)S(1)}, bf16[192,1920]{1,0:T(8,128)(2,1)S(1)}, u32[]{:S(2)}, u32[]{:S(2)}) %collective-permute-start.3) | collective-permute-done | bytes 737312 | tf_op jit(solution)/shard_map/ppermute | solution.py:32
  62.0 16.8 %collective-permute-done.2.refs_2_ = bf16[192,1920]{1,0:T(8,128)(2,1)S(1)} collective-permute-done((bf16[192,1920]{1,0:T(8,128)(2,1)S(1)}, bf16[192,1920]{1,0:T(8,128)(2,1)S(1)}, u32[]{:S(2)}, u32[]{:S(2)}) %collective-permute-start.2) | collective-permute-done | bytes 737312 | tf_op jit(solution)/shard_map/ppermute | solution.py:32
  88.9 2.9 collective-permute-done.4
  91.8 1.9 broadcast_select_fusion.1
  93.7 2.0 pad_maximum_fusion
  98.8 2.4 collective-permute-start.6
  102.2 5.0 %all-gather.7.cloned.1.call-done = bf16[8,128,1536]{2,1,0:T(8,128)(2,1)} async-done(((bf16[2,128,1536]{2,1,0:T(8,128)(2,1)}), bf16[8,128,1536]{2,1,0:T(8,128)(2,1)}) %all-gather.7.cloned.1.call-update) | async-done | bytes 3145744 | tf_op jit(solution)/shard_map/all_gather | solution.py:771
  107.3 2.7 fusion
  112.1 4.4 %convolution_convert_fusion.2.xr.br.rr = bf16[1024,1152]{1,0:T(8,128)(2,1)S(1)} fusion(bf16[1024,1536]{1,0:T(8,128)(2,1)S(1)} %fusion.2, bf16[1536,1152]{1,0:T(8,128)(2,1)S(1)} %copy-done.15), kind=kOutput, calls=%fused_computation.10 | convolution fusion | flops 3625058304 | bytes 9043968 | tf_op jit(solution)/shard_map/dot_general | solution.py:44
  116.7 3.6 %collective-permute-start.8 = (bf16[2,8,1024]{2,1,0:T(8,128)(2,1)S(1)}, bf16[2,8,1024]{2,1,0:T(8,128)(2,1)S(1)}, u32[]{:S(2)}, u32[]{:S(2)}) collective-permute-start(bf16[2,8,1024]{2,1,0:T(8,128)(2,1)S(1)} %slice_bitcast_fusion), channel_id=1, source_target_pairs={{0,4},{4,8},{8,12},{1,5},{5,9},{9,13},{2,6},{6,10},{10,14},{3,7},{... | collective-permute-start | bytes 98312 | tf_op jit(solution)/shard_map/ppermute | solution.py:40
  121.9 9.1 %conv_state.1 = (bf16[1024,768]{1,0:T(8,128)(2,1)S(1)}, bf16[1024,256]{1,0:T(8,128)(2,1)S(1)}, bf16[1024,1024]{1,0:T(8,128)(2,1)S(1)}, f32[8,32,128]{2,1,0:T(8,1...) custom-call(bf16[1024,1152]{1,0:T(8,128)(2,1)} %copy-done.14, bf16[1024,1152]{1,0:T(8,128)(2,1)} %copy-done.14, ...), custom_call_target="tpu_custom_call" | custom-call | flops 1000000000 | bytes 8388608 | tf_op jit(solution)/shard_map/conv_state/pallas_call | solution.py:298
  131.0 4.4 %collective-permute-start.9 = (bf16[2,128,768]{2,1,0:T(8,128)(2,1)S(1)}, bf16[2,128,768]{2,1,0:T(8,128)(2,1)S(1)}, u32[]{:S(2)}, u32[]{:S(2)}) collective-permute-start(bf16[2,128,768]{2,1,0:T(8,128)(2,1)S(1)} %get-tuple-element.108), channel_id=1, source_target_pairs={{0,4},{4,8},{8,12},{1,5},{5,9},{9,13},{2,6},{6,10},{10,14},{3,7},{... | collective-permute-start | bytes 1179656 | tf_op jit(solution)/shard_map/ppermute | solution.py:40
  135.4 4.2 %fusion.56.z_r = f32[1024,768]{1,0:T(8,128)} fusion(bf16[1024,1536]{1,0:T(8,128)(2,1)S(1)} %fusion.2, bf16[1536,768]{1,0:T(8,128)(2,1)S(1)} %copy-done.19), kind=kOutput, calls=%fused_computation.152 | convolution fusion | flops 2415919104 | bytes 8650752 | tf_op jit(solution)/shard_map/dot_general | solution.py:44
  140.0 3.5 collective-permute-done.9.s_in
  143.5 8.3 %scan_gate.1 = (bf16[1024,768]{1,0:T(8,128)(2,1)S(1)}, bf16[1024,768]{1,0:T(8,128)(2,1)S(1)}, bf16[8,128,768]{2,1,0:T(8,128)(2,1)S(1)}, f32[8,1,128]{2,1,0:T(1,128)S(1)}) custom-call(bf16[1024,768]{1,0:T(8,128)(2,1)} %copy-done, bf16[1024,256]{1,0:T(8,128)(2,1)S(1)} %get-tuple-element.105.bc, f32[8,32,128]{2,1,0:T(8,128)S(1)} %get-tuple-element.106.sc, ...), custom_call_target="tpu_custom_call" | custom-call | flops 1000000000 | bytes 8388608 | tf_op jit(solution)/shard_map/scan_gate/pallas_call | solution.py:405
  154.0 3.3 collective-permute-start.11
  157.3 4.0 %convolution_convert_fusion.1 = bf16[1024,1536]{1,0:T(8,128)(2,1)} fusion(bf16[1024,768]{1,0:T(8,128)(2,1)S(1)} %get-tuple-element.118, bf16[768,1536]{1,0:T(8,128)(2,1)S(1)} %pad_maximum_fusion.2), kind=kOutput, calls=%fused_computation.9 | convolution fusion | flops 2417491968 | bytes 7077888 | tf_op jit(solution)/shard_map/dot_general | solution.py:44
  161.4 9.9 %all-gather.5.cloned.1.call-done = bf16[8,128,1536]{2,1,0:T(8,128)(2,1)} async-done(((bf16[2,128,1536]{2,1,0:T(8,128)(2,1)}), bf16[8,128,1536]{2,1,0:T(8,128)(2,1)}) %all-gather.5.cloned.1.call-update) | async-done | bytes 3145744 | tf_op jit(solution)/shard_map/all_gather | solution.py:771
  171.4 7.7 %fusion.4 = (bf16[1024,768]{1,0:T(8,128)(2,1)S(1)}, f32[1024]{0:T(1024)S(1)}, f32[1024,768]{1,0:T(8,128)}) fusion(bf16[1024,768]{1,0:T(8,128)(2,1)} %copy-done.13, f32[1024]{0:T(1024)S(1)} %bitcast.155, bf16[1024,1536]{1,0:T(8,128)(2,1)} %bitcast.173, bf16[768,1536]{1,0:T(8,128)(2,1)} %copy-done.29), kind=kOutput, calls=%fused_computation.17 | convolution fusion | flops 2419850240 | bytes 11804672 | tf_op jit(solution)/shard_map/dot_general | solution.py:48
  180.0 3.4 collective-permute-start.14
  183.5 2.5 convolution_convert_fusion.5
  187.5 6.4 %gate_back.1 = (bf16[1024,768]{1,0:T(8,128)(2,1)S(1)}, bf16[1024,768]{1,0:T(8,128)(2,1)S(1)}, f32[8,768]{1,0:T(8,128)S(1)}, bf16[2,128,768]{2,1,0:T(8,128)(2,1)S(1)}) custom-call(bf16[1024,768]{1,0:T(8,128)(2,1)S(1)} %copy-done.6, f32[1024,768]{1,0:T(8,128)} %fusion.56.z_r, f32[1024,768]{1,0:T(8,128)} %get-tuple-element.216.dg_r, ...), custom_call_target="tpu_custom_call" | custom-call | flops 1000000000 | bytes 8388608 | tf_op jit(solution)/shard_map/gate_back/pallas_call | solution.py:482
  199.4 1.9 collective-permute-done.17
  201.9 2.6 collective-permute-start.21
  206.8 4.2 %convolution_convert_fusion = bf16[1024,1536]{1,0:T(8,128)(2,1)} fusion(bf16[1024,768]{1,0:T(8,128)(2,1)S(1)} %get-tuple-element.127, bf16[1536,768]{1,0:T(8,128)(2,1)S(1)} %copy-done.20), kind=kOutput, calls=%fused_computation.8 | convolution fusion | flops 2417491968 | bytes 7077888 | tf_op jit(solution)/shard_map/dot_general | solution.py:48
  211.0 20.7 %scan_back.1 = (bf16[1024,1152]{1,0:T(8,128)(2,1)}, bf16[2,8,1024]{2,1,0:T(8,128)(2,1)S(1)}, f32[8,1024]{1,0:T(8,128)S(1)}, f32[3,16,128]{2,1,0:T(8,128)S(1)}) custom-call(bf16[1024,768]{1,0:T(8,128)(2,1)S(1)} %copy-done.1, bf16[1024,256]{1,0:T(8,128)(2,1)S(1)} %get-tuple-element.105.bc, bf16[1024,1024]{1,0:T(8,128)(2,1)} %copy-done.4, ...), custom_call_target="tpu_custom_call" | custom-call | flops 2000000000 | bytes 8388608 | tf_op jit(solution)/shard_map/scan_back/pallas_call | solution.py:652
  233.7 3.9 %collective-permute-done.20 = bf16[2,8,1024]{2,1,0:T(8,128)(2,1)S(1)} collective-permute-done((bf16[2,8,1024]{2,1,0:T(8,128)(2,1)S(1)}, bf16[2,8,1024]{2,1,0:T(8,128)(2,1)S(1)}, u32[]{:S(2)}, u32[]{:S(2)}) %collective-permute-start.20) | collective-permute-done | bytes 32800 | tf_op jit(solution)/shard_map/ppermute | solution.py:40
  238.3 3.5 all-to-all-start.1
  242.1 7.1 %fusion.57 = f32[1024,1536]{1,0:T(8,128)S(1)} fusion(bf16[1024,1152]{1,0:T(8,128)(2,1)S(1)} %bitcast.170, bf16[1536,1152]{1,0:T(8,128)(2,1)} %pad_maximum_fusion), kind=kOutput, calls=%fused_computation.153 | convolution fusion | flops 3623878656 | bytes 12189696 | tf_op jit(solution)/shard_map/dot_general | solution.py:48
  249.3 2.8 add_convert_fusion
  252.1 5.8 %convolution_convert_fusion.4 = bf16[768,1152]{1,0:T(8,128)(2,1)} fusion(bf16[1024,1152]{1,0:T(8,128)(2,1)} %bitcast.171, bf16[1024,1536]{1,0:T(8,128)(2,1)} %copy-done.24, s32[]{:T(128)S(6)} %select_n.139), kind=kOutput, calls=%fused_computation.15 | convolution fusion | flops 1812824064 | bytes 5701636 | tf_op jit(solution)/shard_map/dot_general | solution.py:52
  259.0 4.6 %convolution_convert_fusion.3 = bf16[768,1152]{1,0:T(8,128)(2,1)S(1)} fusion(bf16[1024,1152]{1,0:T(8,128)(2,1)} %bitcast.172, bf16[1024,1536]{1,0:T(8,128)(2,1)} %copy-done.24, s32[]{:T(128)S(6)} %select_n.140), kind=kOutput, calls=%fused_computation.14 | convolution fusion | flops 1812824064 | bytes 5701636 | tf_op jit(solution)/shard_map/dot_general | solution.py:52
  263.6 3.0 fusion.26
  266.7 2.5 multiply_reduce_fusion.1
  270.6 1.7 collective-permute-start.31
  272.3 1.8 collective-permute-start.30
  274.9 4.6 %collective-permute-start.25 = (bf16[192,1152]{1,0:T(8,128)(2,1)}, bf16[192,1152]{1,0:T(8,128)(2,1)S(1)}, u32[]{:S(2)}, u32[]{:S(2)}) collective-permute-start(bf16[192,1152]{1,0:T(8,128)(2,1)} %get-tuple-element.149), channel_id=1, source_target_pairs={{0,4},{4,0},{8,12},{12,8},{1,5},{5,1},{9,13},{13,9},{2,6},{6,2},{1... | collective-permute-start | bytes 1327112 | tf_op jit(solution)/shard_map/ppermute | solution.py:32
  279.5 3.3 collective-permute-start.26
  282.9 12.1 %collective-permute-done.25 = bf16[192,1152]{1,0:T(8,128)(2,1)S(1)} collective-permute-done((bf16[192,1152]{1,0:T(8,128)(2,1)}, bf16[192,1152]{1,0:T(8,128)(2,1)S(1)}, u32[]{:S(2)}, u32[]{:S(2)}) %collective-permute-start.25) | collective-permute-done | bytes 442400 | tf_op jit(solution)/shard_map/ppermute | solution.py:32
  295.0 11.3 %collective-permute-done.26 = bf16[192,1152]{1,0:T(8,128)(2,1)S(1)} collective-permute-done((bf16[192,1152]{1,0:T(8,128)(2,1)}, bf16[192,1152]{1,0:T(8,128)(2,1)S(1)}, u32[]{:S(2)}, u32[]{:S(2)}) %collective-permute-start.26) | collective-permute-done | bytes 442400 | tf_op jit(solution)/shard_map/ppermute | solution.py:32
  307.8 7.6 %all-to-all-start.2 = ((bf16[4,64,1152]{2,1,0:T(8,128)(2,1)}), bf16[4,64,1152]{2,1,0:T(8,128)(2,1)S(1)}, u32[]{:S(2)}, u32[]{:S(2)}) async-start(bf16[4,64,1152]{2,1,0:T(8,128)(2,1)} %pad_maximum_fusion.7), calls=%async_computation.4 | async-start | bytes 1179648 | tf_op jit(solution)/shard_map/all_to_all | solution.py:927
  317.1 24.3 %reduce-scatter.5.cloned.1.call-done = bf16[256,1536]{1,0:T(8,128)(2,1)} async-done(((bf16[1024,1536]{1,0:T(8,128)(2,1)}), bf16[256,1536]{1,0:T(8,128)(2,1)}) %reduce-scatter.5.cloned.1.call-update) | async-done | bytes 786448 | tf_op jit(solution)/shard_map/reduce_scatter | solution.py:837
  341.4 1.6 fusion.7
  345.4 3.2 fusion.10
  (239 shorter events, 50.2 us)
Async XLA Ops:
  11.1 26.9 %all-to-all-start = ((bf16[4,48,1920]{2,1,0:T(8,128)(2,1)}), bf16[4,48,1920]{2,1,0:T(8,128)(2,1)S(1)}, u32[]{:S(2)}, u32[]{:S(2)}) async-start(bf16[4,48,1920]{2,1,0:T(8,128)(2,1)} %fusion.22), calls=%async_computation | async-start | bytes 1474560 | tf_op jit(solution)/shard_map/all_to_all | solution.py:778
  17.4 89.8 %all-gather.7.cloned.1.call-start = ((), (), s32[]{:S(2)}) async-start(), calls=%async_computation.8 | async-start | bytes 3932160 | tf_op jit(solution)/shard_map/all_gather | solution.py:771
  17.4 0.7 collective-permute-start
  38.0 42.6 %copy-start.2 = (bf16[4,48,1920]{2,1,0:T(8,128)(2,1)}, bf16[4,48,1920]{2,1,0:T(8,128)(2,1)S(1)}, u32[]{:S(2)}) copy-start(bf16[4,48,1920]{2,1,0:T(8,128)(2,1)S(1)} %all-to-all-done) | copy-start | bytes 2211844
  38.0 133.3 %all-gather.5.cloned.1.call-start = ((), (), s32[]{:S(2)}) async-start(), calls=%async_computation.7 | async-start | bytes 3932160 | tf_op jit(solution)/shard_map/all_gather | solution.py:771
  38.1 23.0 %collective-permute-start.3 = (bf16[192,1920]{1,0:T(8,128)(2,1)S(1)}, bf16[192,1920]{1,0:T(8,128)(2,1)S(1)}, u32[]{:S(2)}, u32[]{:S(2)}) collective-permute-start(bf16[192,1920]{1,0:T(8,128)(2,1)S(1)} %bitcast.121), channel_id=1, source_target_pairs={{0,12},{4,8},{8,4},{12,0},{1,13},{5,9},{9,5},{13,1},{2,14},{6,10},... | collective-permute-start | bytes 2211848 | tf_op jit(solution)/shard_map/ppermute | solution.py:32
  43.7 35.0 %collective-permute-start.2 = (bf16[192,1920]{1,0:T(8,128)(2,1)S(1)}, bf16[192,1920]{1,0:T(8,128)(2,1)S(1)}, u32[]{:S(2)}, u32[]{:S(2)}) collective-permute-start(bf16[192,1920]{1,0:T(8,128)(2,1)S(1)} %bitcast.122), channel_id=1, source_target_pairs={{0,8},{4,12},{8,0},{12,4},{1,9},{5,13},{9,1},{13,5},{2,10},{6,14},... | collective-permute-start | bytes 2211848 | tf_op jit(solution)/shard_map/ppermute | solution.py:32
  46.2 34.5 %collective-permute-start.1 = (bf16[192,1920]{1,0:T(8,128)(2,1)S(1)}, bf16[192,1920]{1,0:T(8,128)(2,1)S(1)}, u32[]{:S(2)}, u32[]{:S(2)}) collective-permute-start(bf16[192,1920]{1,0:T(8,128)(2,1)S(1)} %bitcast.123), channel_id=1, source_target_pairs={{0,4},{4,0},{8,12},{12,8},{1,5},{5,1},{9,13},{13,9},{2,6},{6,2},{1... | collective-permute-start | bytes 2211848 | tf_op jit(solution)/shard_map/ppermute | solution.py:32
  86.2 5.6 %collective-permute-start.4 = (bf16[768,1920]{1,0:T(8,128)(2,1)S(1)}, bf16[768,1920]{1,0:T(8,128)(2,1)}, u32[]{:S(2)}, u32[]{:S(2)}) collective-permute-start(bf16[768,1920]{1,0:T(8,128)(2,1)S(1)} %place_rows.2), channel_id=1, source_target_pairs={{0,16},{16,0},{1,17},{17,1},{2,18},{18,2},{3,19},{19,3},{4,20},{20... | collective-permute-start | bytes 8847368 | tf_op jit(solution)/shard_map/ppermute | solution.py:32
  86.7 150.9 %reduce-scatter.3.cloned.1.call-start = ((), (), s32[]{:S(2)}) async-start(), calls=%async_computation.5 | async-start | bytes 3932160 | tf_op jit(solution)/shard_map/reduce_scatter | solution.py:837
  98.8 11.3 %copy-start.34 = (f32[1536]{0:T(1024)S(1)}, f32[1536]{0:T(1024)}, u32[]{:S(2)}) copy-start(f32[1536]{0:T(1024)} %param.16) | copy-start | bytes 18436
  98.8 17.7 %collective-permute-start.7 = (bf16[96,1536]{1,0:T(8,128)(2,1)S(1)}, bf16[96,1536]{1,0:T(8,128)(2,1)S(1)}, u32[]{:S(2)}, u32[]{:S(2)}) collective-permute-start(bf16[96,1536]{1,0:T(8,128)(2,1)S(1)} %collective-permute-done.refs_0_), channel_id=1, source_target_pairs={{0,12},{4,8},{8,4},{12,0},{1,13},{5,9},{9,5},{13,1},{2,14},{6,10},... | collective-permute-start | bytes 884744 | tf_op jit(solution)/shard_map/ppermute | solution.py:32
  98.8 17.7 %collective-permute-start.6 = (bf16[96,1536]{1,0:T(8,128)(2,1)S(1)}, bf16[96,1536]{1,0:T(8,128)(2,1)S(1)}, u32[]{:S(2)}, u32[]{:S(2)}) collective-permute-start(bf16[96,1536]{1,0:T(8,128)(2,1)S(1)} %collective-permute-done.refs_0_), channel_id=1, source_target_pairs={{0,8},{4,12},{8,0},{12,4},{1,9},{5,13},{9,1},{13,5},{2,10},{6,14},... | collective-permute-start | bytes 884744 | tf_op jit(solution)/shard_map/ppermute | solution.py:32
  101.2 15.3 %collective-permute-start.5 = (bf16[96,1536]{1,0:T(8,128)(2,1)S(1)}, bf16[96,1536]{1,0:T(8,128)(2,1)S(1)}, u32[]{:S(2)}, u32[]{:S(2)}) collective-permute-start(bf16[96,1536]{1,0:T(8,128)(2,1)S(1)} %collective-permute-done.refs_0_), channel_id=1, source_target_pairs={{0,4},{4,0},{8,12},{12,8},{1,5},{5,1},{9,13},{13,9},{2,6},{6,2},{1... | collective-permute-start | bytes 884744 | tf_op jit(solution)/shard_map/ppermute | solution.py:32
  112.1 23.4 %copy-start.24 = (bf16[1024,1536]{1,0:T(8,128)(2,1)}, bf16[1024,1536]{1,0:T(8,128)(2,1)S(1)}, u32[]{:S(2)}) copy-start(bf16[1024,1536]{1,0:T(8,128)(2,1)S(1)} %fusion.2) | copy-start | bytes 9437188
  116.6 23.1 %collective-permute-start.10 = (bf16[384,1536]{1,0:T(8,128)(2,1)S(1)}, bf16[384,1536]{1,0:T(8,128)(2,1)S(1)}, u32[]{:S(2)}, u32[]{:S(2)}) collective-permute-start(bf16[384,1536]{1,0:T(8,128)(2,1)S(1)} %place_rows.3), channel_id=1, source_target_pairs={{0,16},{16,0},{1,17},{17,1},{2,18},{18,2},{3,19},{19,3},{4,20},{20... | collective-permute-start | bytes 3538952 | tf_op jit(solution)/shard_map/ppermute | solution.py:32
  116.7 18.7 %copy-start.19 = (bf16[1536,768]{1,0:T(8,128)(2,1)S(1)}, bf16[1536,768]{1,0:T(8,128)(2,1)}, u32[]{:S(2)}) copy-start(bf16[1536,768]{1,0:T(8,128)(2,1)} %pad_maximum_fusion.1) | copy-start | bytes 7077892
  116.7 5.2 %collective-permute-start.8 = (bf16[2,8,1024]{2,1,0:T(8,128)(2,1)S(1)}, bf16[2,8,1024]{2,1,0:T(8,128)(2,1)S(1)}, u32[]{:S(2)}, u32[]{:S(2)}) collective-permute-start(bf16[2,8,1024]{2,1,0:T(8,128)(2,1)S(1)} %slice_bitcast_fusion), channel_id=1, source_target_pairs={{0,4},{4,8},{8,12},{1,5},{5,9},{9,13},{2,6},{6,10},{10,14},{3,7},{... | collective-permute-start | bytes 98312 | tf_op jit(solution)/shard_map/ppermute | solution.py:40
  131.0 12.5 %collective-permute-start.9 = (bf16[2,128,768]{2,1,0:T(8,128)(2,1)S(1)}, bf16[2,128,768]{2,1,0:T(8,128)(2,1)S(1)}, u32[]{:S(2)}, u32[]{:S(2)}) collective-permute-start(bf16[2,128,768]{2,1,0:T(8,128)(2,1)S(1)} %get-tuple-element.108), channel_id=1, source_target_pairs={{0,4},{4,8},{8,12},{1,5},{5,9},{9,13},{2,6},{6,10},{10,14},{3,7},{... | collective-permute-start | bytes 1179656 | tf_op jit(solution)/shard_map/ppermute | solution.py:40
  140.0 17.3 %copy-start.29 = (bf16[768,1536]{1,0:T(8,128)(2,1)}, bf16[768,1536]{1,0:T(8,128)(2,1)S(1)}, u32[]{:S(2)}) copy-start(bf16[768,1536]{1,0:T(8,128)(2,1)S(1)} %pad_maximum_fusion.2) | copy-start | bytes 7077892
  152.9 8.4 %collective-permute-start.13 = (f32[8,1,128]{2,1,0:T(1,128)S(1)}, f32[8,1,128]{2,1,0:T(1,128)S(1)}, u32[]{:S(2)}, u32[]{:S(2)}) collective-permute-start(f32[8,1,128]{2,1,0:T(1,128)S(1)} %get-tuple-element.120), channel_id=1, source_target_pairs={{0,3},{1,2},{2,1},{3,0},{4,7},{5,6},{6,5},{7,4},{8,11},{9,10},{10,... | collective-permute-start | bytes 12296 | tf_op jit(solution)/shard_map/ppermute | solution.py:32
  153.9 7.5 %collective-permute-start.12 = (f32[8,1,128]{2,1,0:T(1,128)S(1)}, f32[8,1,128]{2,1,0:T(1,128)S(1)}, u32[]{:S(2)}, u32[]{:S(2)}) collective-permute-start(f32[8,1,128]{2,1,0:T(1,128)S(1)} %get-tuple-element.120), channel_id=1, source_target_pairs={{0,2},{1,3},{2,0},{3,1},{4,6},{5,7},{6,4},{7,5},{8,10},{9,11},{10,... | collective-permute-start | bytes 12296 | tf_op jit(solution)/shard_map/ppermute | solution.py:32
  154.0 7.3 %collective-permute-start.11 = (f32[8,1,128]{2,1,0:T(1,128)S(1)}, f32[8,1,128]{2,1,0:T(1,128)S(1)}, u32[]{:S(2)}, u32[]{:S(2)}) collective-permute-start(f32[8,1,128]{2,1,0:T(1,128)S(1)} %get-tuple-element.120), channel_id=1, source_target_pairs={{0,1},{1,0},{2,3},{3,2},{4,5},{5,4},{6,7},{7,6},{8,9},{9,8},{10,11... | collective-permute-start | bytes 12296 | tf_op jit(solution)/shard_map/ppermute | solution.py:32
  171.4 12.1 %copy-start.41 = (bf16[8,128,1536]{2,1,0:T(8,128)(2,1)S(1)}, bf16[8,128,1536]{2,1,0:T(8,128)(2,1)}, u32[]{:S(2)}) copy-start(bf16[8,128,1536]{2,1,0:T(8,128)(2,1)} %all-gather.5.cloned.1.call-done) | copy-start | bytes 9437188
  179.1 8.3 %collective-permute-start.16 = (f32[8,1,128]{2,1,0:T(1,128)S(1)}, f32[8,1,128]{2,1,0:T(1,128)S(1)}, u32[]{:S(2)}, u32[]{:S(2)}) collective-permute-start(f32[8,1,128]{2,1,0:T(1,128)S(1)} %bitcast.157), channel_id=1, source_target_pairs={{0,3},{1,2},{2,1},{3,0},{4,7},{5,6},{6,5},{7,4},{8,11},{9,10},{10,... | collective-permute-start | bytes 12296 | tf_op jit(solution)/shard_map/ppermute | solution.py:32
  179.8 7.6 %collective-permute-start.15 = (f32[8,1,128]{2,1,0:T(1,128)S(1)}, f32[8,1,128]{2,1,0:T(1,128)S(1)}, u32[]{:S(2)}, u32[]{:S(2)}) collective-permute-start(f32[8,1,128]{2,1,0:T(1,128)S(1)} %bitcast.158), channel_id=1, source_target_pairs={{0,2},{1,3},{2,0},{3,1},{4,6},{5,7},{6,4},{7,5},{8,10},{9,11},{10,... | collective-permute-start | bytes 12296 | tf_op jit(solution)/shard_map/ppermute | solution.py:32
  180.0 7.4 %collective-permute-start.14 = (f32[8,1,128]{2,1,0:T(1,128)S(1)}, f32[8,1,128]{2,1,0:T(1,128)S(1)}, u32[]{:S(2)}, u32[]{:S(2)}) collective-permute-start(f32[8,1,128]{2,1,0:T(1,128)S(1)} %bitcast.159), channel_id=1, source_target_pairs={{0,1},{1,0},{2,3},{3,2},{4,5},{5,4},{6,7},{7,6},{8,9},{9,8},{10,11... | collective-permute-start | bytes 12296 | tf_op jit(solution)/shard_map/ppermute | solution.py:32
  186.0 12.9 %collective-permute-start.18 = (bf16[384,1536]{1,0:T(8,128)(2,1)}, bf16[384,1536]{1,0:T(8,128)(2,1)S(1)}, u32[]{:S(2)}, u32[]{:S(2)}) collective-permute-start(bf16[384,1536]{1,0:T(8,128)(2,1)} %convolution_convert_fusion.5), channel_id=1, source_target_pairs={{0,16},{16,0},{1,17},{17,1},{2,18},{18,2},{3,19},{19,3},{4,20},{20... | collective-permute-start | bytes 3538952 | tf_op jit(solution)/shard_map/ppermute | solution.py:32
  193.8 17.1 %collective-permute-start.19 = (bf16[2,128,768]{2,1,0:T(8,128)(2,1)S(1)}, bf16[2,128,768]{2,1,0:T(8,128)(2,1)S(1)}, u32[]{:S(2)}, u32[]{:S(2)}) collective-permute-start(bf16[2,128,768]{2,1,0:T(8,128)(2,1)S(1)} %get-tuple-element.132), channel_id=1, source_target_pairs={{4,0},{8,4},{12,8},{5,1},{9,5},{13,9},{6,2},{10,6},{14,10},{7,3},{... | collective-permute-start | bytes 1179656 | tf_op jit(solution)/shard_map/ppermute | solution.py:40
  198.3 3.1 collective-permute-start.17
  201.9 31.2 %collective-permute-start.21 = (bf16[384,768]{1,0:T(8,128)(2,1)S(1)}, bf16[384,768]{1,0:T(8,128)(2,1)S(1)}, u32[]{:S(2)}, u32[]{:S(2)}) collective-permute-start(bf16[384,768]{1,0:T(8,128)(2,1)S(1)} %pad_maximum_fusion.4), channel_id=1, source_target_pairs={{0,4},{4,0},{8,12},{12,8},{1,5},{5,1},{9,13},{13,9},{2,6},{6,2},{1... | collective-permute-start | bytes 1769480 | tf_op jit(solution)/shard_map/ppermute | solution.py:32
  204.4 28.6 %collective-permute-start.22 = (bf16[384,768]{1,0:T(8,128)(2,1)S(1)}, bf16[384,768]{1,0:T(8,128)(2,1)S(1)}, u32[]{:S(2)}, u32[]{:S(2)}) collective-permute-start(bf16[384,768]{1,0:T(8,128)(2,1)S(1)} %pad_maximum_fusion.5), channel_id=1, source_target_pairs={{0,8},{4,12},{8,0},{12,4},{1,9},{5,13},{9,1},{13,5},{2,10},{6,14},... | collective-permute-start | bytes 1769480 | tf_op jit(solution)/shard_map/ppermute | solution.py:32
  205.9 27.5 %collective-permute-start.23 = (bf16[384,768]{1,0:T(8,128)(2,1)S(1)}, bf16[384,768]{1,0:T(8,128)(2,1)S(1)}, u32[]{:S(2)}, u32[]{:S(2)}) collective-permute-start(bf16[384,768]{1,0:T(8,128)(2,1)S(1)} %pad_maximum_fusion.6), channel_id=1, source_target_pairs={{0,12},{4,8},{8,4},{12,0},{1,13},{5,9},{9,5},{13,1},{2,14},{6,10},... | collective-permute-start | bytes 1769480 | tf_op jit(solution)/shard_map/ppermute | solution.py:32
  231.6 5.9 %collective-permute-start.20 = (bf16[2,8,1024]{2,1,0:T(8,128)(2,1)S(1)}, bf16[2,8,1024]{2,1,0:T(8,128)(2,1)S(1)}, u32[]{:S(2)}, u32[]{:S(2)}) collective-permute-start(bf16[2,8,1024]{2,1,0:T(8,128)(2,1)S(1)} %get-tuple-element.133), channel_id=1, source_target_pairs={{4,0},{8,4},{12,8},{5,1},{9,5},{13,9},{6,2},{10,6},{14,10},{7,3},{... | collective-permute-start | bytes 98312 | tf_op jit(solution)/shard_map/ppermute | solution.py:40
  238.3 13.7 %all-to-all-start.1 = ((bf16[4,48,768]{2,1,0:T(8,128)(2,1)}), bf16[4,48,768]{2,1,0:T(8,128)(2,1)S(1)}, u32[]{:S(2)}, u32[]{:S(2)}) async-start(bf16[4,48,768]{2,1,0:T(8,128)(2,1)} %bitcast.41), calls=%async_computation.2 | async-start | bytes 589824 | tf_op jit(solution)/shard_map/all_to_all | solution.py:882
  241.7 99.7 %reduce-scatter.5.cloned.1.call-start = ((), (), s32[]{:S(2)}) async-start(), calls=%async_computation.6 | async-start | bytes 3932160 | tf_op jit(solution)/shard_map/reduce_scatter | solution.py:837
  257.9 5.8 %collective-permute-start.24 = (bf16[768,1152]{1,0:T(8,128)(2,1)}, bf16[768,1152]{1,0:T(8,128)(2,1)}, u32[]{:S(2)}, u32[]{:S(2)}) collective-permute-start(bf16[768,1152]{1,0:T(8,128)(2,1)} %convolution_convert_fusion.4), channel_id=1, source_target_pairs={{0,16},{16,0},{1,17},{17,1},{2,18},{18,2},{3,19},{19,3},{4,20},{20... | collective-permute-start | bytes 5308424 | tf_op jit(solution)/shard_map/ppermute | solution.py:32
  269.2 37.5 %copy-start.30 = (bf16[192,1152]{1,0:T(8,128)(2,1)S(1)}, bf16[192,1152]{1,0:T(8,128)(2,1)}, u32[]{:S(2)}) copy-start(bf16[192,1152]{1,0:T(8,128)(2,1)} %get-tuple-element.148) | copy-start | bytes 1327108
  269.3 1.3 collective-permute-start.28
  270.6 8.9 %collective-permute-start.31 = (f32[8,1152]{1,0:T(8,128)S(1)}, f32[8,1152]{1,0:T(8,128)S(1)}, u32[]{:S(2)}, u32[]{:S(2)}) collective-permute-start(f32[8,1152]{1,0:T(8,128)S(1)} %fusion.76), channel_id=1, source_target_pairs={{0,12},{4,8},{8,4},{12,0},{1,13},{5,9},{9,5},{13,1},{2,14},{6,10},... | collective-permute-start | bytes 110600 | tf_op jit(solution)/shard_map/ppermute | solution.py:32
  272.3 10.5 %collective-permute-start.30 = (f32[8,1152]{1,0:T(8,128)S(1)}, f32[8,1152]{1,0:T(8,128)S(1)}, u32[]{:S(2)}, u32[]{:S(2)}) collective-permute-start(f32[8,1152]{1,0:T(8,128)S(1)} %fusion.76), channel_id=1, source_target_pairs={{0,8},{4,12},{8,0},{12,4},{1,9},{5,13},{9,1},{13,5},{2,10},{6,14},... | collective-permute-start | bytes 110600 | tf_op jit(solution)/shard_map/ppermute | solution.py:32
  274.1 8.7 %collective-permute-start.29 = (f32[8,1152]{1,0:T(8,128)S(1)}, f32[8,1152]{1,0:T(8,128)S(1)}, u32[]{:S(2)}, u32[]{:S(2)}) collective-permute-start(f32[8,1152]{1,0:T(8,128)S(1)} %fusion.76), channel_id=1, source_target_pairs={{0,4},{4,0},{8,12},{12,8},{1,5},{5,1},{9,13},{13,9},{2,6},{6,2},{1... | collective-permute-start | bytes 110600 | tf_op jit(solution)/shard_map/ppermute | solution.py:32
  274.2 41.1 %collective-permute-start.32 = (bf16[96,1536]{1,0:T(8,128)(2,1)S(1)}, bf16[96,1536]{1,0:T(8,128)(2,1)S(1)}, u32[]{:S(2)}, u32[]{:S(2)}) collective-permute-start(bf16[96,1536]{1,0:T(8,128)(2,1)S(1)} %pad_maximum_fusion.8), channel_id=1, source_target_pairs={{0,0},{4,1},{8,2},{12,3},{16,4},{20,5},{24,6},{28,7},{1,8},{5,9},{... | collective-permute-start | bytes 884744 | tf_op jit(solution)/shard_map/ppermute | solution.py:907
  274.9 20.1 %collective-permute-start.25 = (bf16[192,1152]{1,0:T(8,128)(2,1)}, bf16[192,1152]{1,0:T(8,128)(2,1)S(1)}, u32[]{:S(2)}, u32[]{:S(2)}) collective-permute-start(bf16[192,1152]{1,0:T(8,128)(2,1)} %get-tuple-element.149), channel_id=1, source_target_pairs={{0,4},{4,0},{8,12},{12,8},{1,5},{5,1},{9,13},{13,9},{2,6},{6,2},{1... | collective-permute-start | bytes 1327112 | tf_op jit(solution)/shard_map/ppermute | solution.py:32
  279.5 26.8 %collective-permute-start.26 = (bf16[192,1152]{1,0:T(8,128)(2,1)}, bf16[192,1152]{1,0:T(8,128)(2,1)S(1)}, u32[]{:S(2)}, u32[]{:S(2)}) collective-permute-start(bf16[192,1152]{1,0:T(8,128)(2,1)} %get-tuple-element.150), channel_id=1, source_target_pairs={{0,8},{4,12},{8,0},{12,4},{1,9},{5,13},{9,1},{13,5},{2,10},{6,14},... | collective-permute-start | bytes 1327112 | tf_op jit(solution)/shard_map/ppermute | solution.py:32
  282.8 23.8 %collective-permute-start.27 = (bf16[192,1152]{1,0:T(8,128)(2,1)}, bf16[192,1152]{1,0:T(8,128)(2,1)S(1)}, u32[]{:S(2)}, u32[]{:S(2)}) collective-permute-start(bf16[192,1152]{1,0:T(8,128)(2,1)} %get-tuple-element.151), channel_id=1, source_target_pairs={{0,12},{4,8},{8,4},{12,0},{1,13},{5,9},{9,5},{13,1},{2,14},{6,10},... | collective-permute-start | bytes 1327112 | tf_op jit(solution)/shard_map/ppermute | solution.py:32
  307.8 35.3 %all-to-all-start.2 = ((bf16[4,64,1152]{2,1,0:T(8,128)(2,1)}), bf16[4,64,1152]{2,1,0:T(8,128)(2,1)S(1)}, u32[]{:S(2)}, u32[]{:S(2)}) async-start(bf16[4,64,1152]{2,1,0:T(8,128)(2,1)} %pad_maximum_fusion.7), calls=%async_computation.4 | async-start | bytes 1179648 | tf_op jit(solution)/shard_map/all_to_all | solution.py:927
  316.2 29.1 %copy-start.27 = (bf16[2,128,1536]{2,1,0:T(8,128)(2,1)S(1)}, bf16[2,128,1536]{2,1,0:T(8,128)(2,1)}, u32[]{:S(2)}) copy-start(bf16[2,128,1536]{2,1,0:T(8,128)(2,1)} %param.27) | copy-start | bytes 2359300
  (37 other events, 148.9 us)
Sparse Core Ops, SparseCore 0:
  38.1 69.0 all-gather.6
  108.8 62.4 all-gather.4
  173.6 59.1 reduce-scatter.2
  252.2 89.1 reduce-scatter.4
